TPU v7x, 32 devices: a whole 2x2x4 slice. The times are simulated.
32 devices in a mesh: dp: 8 (over z, y), tensor: 4 (over x, core).
Axes of the slice: x: 2, y: 2, z: 4, core: 2. Of those that a mesh axis runs over, the one named last changes fastest.
Arguments:
- tokens: bfloat16 [1024, 32, 512], P('dp', 'tensor'), may hold values from -6 to 6
- cotangent: bfloat16 [1024, 32, 512], P('dp', 'tensor'), may hold values from -6 to 6
- lengths: int32 [32], replicated, may hold values from 1 to 1024, 20480 in all
- ln_gain: float32 [512], P('dp'), may hold values from 0.5 to 1.5
- ln_bias: float32 [512], P('dp'), may hold values from -3 to 3
- lam_log: float32 [512, 64], P('tensor', 'dp'), may hold values from -2.3 to 0
- lam_im: float32 [512, 64], P('tensor', 'dp'), may hold values from 0 to 3
- w_re: float32 [512, 64], P('tensor', 'dp'), may hold values from -6 to 6
- w_im: float32 [512, 64], P('tensor', 'dp'), may hold values from -6 to 6
- log_dt: float32 [512], P('dp'), may hold values from -6.9 to -2.3
- skip_gain: float32 [512], P('dp'), may hold values from -4 to 4
- w_out: bfloat16 [512, 1024], P('tensor', 'dp'), may hold values from -0.5 to 0.5
- b_out: float32 [1024], P('dp'), may hold values from -3 to 3
Outputs:
- out: bfloat16 [1024, 32, 512], P('dp', 'tensor')
- grad_tokens: bfloat16 [1024, 32, 512], P('dp', 'tensor')
- grad_ln_gain: float32 [512], P('dp')
- grad_ln_bias: float32 [512], P('dp')
- grad_lam_log: float32 [512, 64], P('tensor', 'dp')
- grad_lam_im: float32 [512, 64], P('tensor', 'dp')
- grad_w_re: float32 [512, 64], P('tensor', 'dp')
- grad_w_im: float32 [512, 64], P('tensor', 'dp')
- grad_log_dt: float32 [512], P('dp')
- grad_skip_gain: float32 [512], P('dp')
- grad_w_out: float32 [512, 1024], P('tensor', 'dp')
- grad_b_out: float32 [1024], P('dp')
Inputs may be any that keep to these rules, and one draw needn't show every extreme that they name: lengths[s] is sequence s's length; its positions at or past it are padding.
All inputs are finite; a program needn't handle non-finite values.
Results may differ from a plain program's by a relative error of at most 0.02.
Values may be sent and summed in bfloat16 or wider, within the bound.
No kernel may reach another device: no remote copies, remote signals or barrier semaphores. Data moves between devices by JAX's collectives and lax.ppermute only.
A program may use at most 256 MiB of HBM per device.

v0:
```python
from functools import partial

import jax
import jax.numpy as jnp
import numpy as np
from jax import lax
from jax.experimental import pallas as pl
from jax.experimental.pallas import tpu as pltpu
from jax.sharding import PartitionSpec as P

epsilon = 1e-05
f32 = jnp.float32
bf16 = jnp.bfloat16


def params(mib):
    return pltpu.CompilerParams(vmem_limit_bytes=mib * 1024 * 1024)


def cost(us):
    return pl.CostEstimate(flops=0, bytes_accessed=int(us * 3.3e6), transcendentals=0)


def keep(shape, dtype):
    return pltpu.VMEM(shape, dtype)


def held_in_vmem(*arrays):
    return [pltpu.with_memory_space_constraint(a, pltpu.VMEM) for a in arrays]


def vspec():
    return pl.BlockSpec(memory_space=pltpu.VMEM)


def sspec():
    return pl.BlockSpec(memory_space=pltpu.SMEM)


def basis(block):
    freq = np.concatenate([np.arange(0, block, 2), np.arange(1, block, 2)])
    angle = np.pi * (2 * freq[:, None] + 1) * np.arange(block)[None, :] / (2 * block)
    forward = np.concatenate([np.cos(angle), -np.sin(angle)], axis=0)
    return forward.astype(np.float32)


def shift_exchange(pieces, axis, size):
    out = [pieces[0]]
    for s in range(1, size):
        out.append(lax.ppermute(pieces[s], axis, [(k, (k + s) % size) for k in range(size)]))
    return out


def flip_bit(value, axis, size, bit):
    return lax.ppermute(value, axis, [(k, k ^ bit) for k in range(size)])


WIDE = 128


def pad_to(value, multiple):
    return -(-value // multiple) * multiple


def split_kernel(n, states, par_ref, vec_ref, w_ref, out):
    rows = 4 * states
    base = 0
    for ref in (par_ref, vec_ref):
        rest = ref[...]
        count = rest.shape[0]
        for _ in range(3):
            plane = rest.astype(bf16)
            out[0, base : base + count, :] = plane
            rest = rest - plane.astype(f32)
            base += count
    top = out.shape[1] - w_ref.shape[0]
    out[0, top:, :] = w_ref[...]
    for d in range(1, n):
        out[d] = out[0]


def pack_weights(n, par, vec, w):
    states = par.shape[0] // 4
    rows = pad_to(3 * (par.shape[0] + vec.shape[0]), 16) + w.shape[0]
    return pl.pallas_call(
        partial(split_kernel, n, states),
        out_shape=jax.ShapeDtypeStruct((n, rows, WIDE), bf16),
        in_specs=[vspec()] * 3,
        out_specs=vspec(),
        compiler_params=params(4),
        name="pack_weights",
    )(par, vec, w)


INNER = 32


def powers(table_r, table_i, zr, zi, count):
    cr, ci = jnp.ones_like(zr), jnp.zeros_like(zi)
    for b in range(count):
        table_r[b] = cr
        table_i[b] = ci
        if b + 1 < count:
            cr, ci = cr * zr - ci * zi, cr * zi + ci * zr


def taps_kernel(n, states, channels, w_cols, sc, blob, out, w_out, par_out, vec_out, b_out, table_r, table_i, part):
    rank_t = sc[2]
    count = 4 * states
    vec_rows = (blob.shape[1] - w_out.shape[1]) // 3 - count
    per = vec_out.shape[1] // n
    plane = [blob[:, k * count : (k + 1) * count, :].astype(f32) for k in range(3)]
    par = plane[0] + plane[1] + plane[2]
    for d in range(n):
        for k in range(4):
            par_out[k, d * states : (d + 1) * states, :] = par[d, k * states : (k + 1) * states, :channels]
    vecs = VEC_ROWS(per)
    for d in range(n):
        vec = sum(
            blob[d, 3 * count + k * vecs : 3 * count + (k + 1) * vecs, :].astype(f32) for k in range(3)
        )
        for k in range(4):
            row, lane = divmod(k * per, WIDE)
            vec_out[k : k + 1, d * per : (d + 1) * per] = vec[row : row + 1, lane : lane + per]
        row, lane = divmod(4 * per, WIDE)
        b_out[:, 2 * d * per : 2 * (d + 1) * per] = vec[row : row + 1, lane : lane + 2 * per]
        w_out[d] = blob[d, blob.shape[1] - w_out.shape[1] :, :w_cols]
    log_step = vec_out[2:3, 0:channels]
    for t in range(1, vec_out.shape[1] // channels):
        log_step = jnp.where(rank_t == t, vec_out[2:3, t * channels : (t + 1) * channels], log_step)
    vec_out[4:5, 0:channels] = log_step
    step = jnp.exp(log_step)
    decay = jnp.exp(par_out[0]) * step
    turn = par_out[1] * step
    size = jnp.exp(-decay)
    powers(table_r, table_i, size * jnp.cos(turn), size * jnp.sin(turn), INNER)
    far = jnp.exp(-INNER * decay)
    far_r, far_i = far * jnp.cos(INNER * turn), far * jnp.sin(INNER * turn)
    total = decay.shape[0]

    def block(a, carry):
        ar, ai = carry
        for b in range(INNER):
            value = ar * table_r[b] - ai * table_i[b]
            part[b * 8 : (b + 1) * 8, :] = jnp.sum(value.reshape(total // 8, 8, channels), axis=0)
        summed = part[pl.ds(0, INNER, stride=8), :]
        for q in range(1, 8):
            summed = summed + part[pl.ds(q, INNER, stride=8), :]
        out[pl.ds(pl.multiple_of(a * INNER, INNER), INNER), :] = summed.astype(bf16)
        return ar * far_r - ai * far_i, ar * far_i + ai * far_r

    lax.fori_loop(0, out.shape[0] // INNER, block, (par_out[2] * step, par_out[3] * step))


def VEC_ROWS(per):
    return -(-6 * per // WIDE)


def make_taps(scalars, blob, states, length, width, channels, w_cols):
    n = blob.shape[0]
    total = n * states
    return pl.pallas_call(
        partial(taps_kernel, n, states, channels, w_cols),
        out_shape=[
            jax.ShapeDtypeStruct((length, channels), bf16),
            jax.ShapeDtypeStruct((n, channels, w_cols), bf16),
            jax.ShapeDtypeStruct((4, total, channels), f32),
            jax.ShapeDtypeStruct((8, width), f32),
            jax.ShapeDtypeStruct((1, 2 * width), f32),
        ],
        in_specs=[sspec(), vspec()],
        out_specs=[vspec()] * 5,
        scratch_shapes=[
            pltpu.VMEM((INNER, total, channels), f32),
            pltpu.VMEM((INNER, total, channels), f32),
            pltpu.VMEM((INNER * 8, channels), f32),
        ],
        compiler_params=params(8),
        cost_estimate=cost(7),
        name="taps",
    )(scalars, blob)


def taps_back_kernel(
    n, states, sc, par, vec, grad_a, grad_b, w_a, w_b, gain8, bias8, out8, msg, table_r, table_i, summed, held
):
    rank_t = sc[2]
    length, channels = summed.shape
    width = vec.shape[1]
    rate = jnp.exp(par[0])
    step = jnp.exp(vec[4:5, 0:channels])
    decay = rate * step
    turn = par[1] * step
    w_re, w_im = par[2], par[3]
    size = jnp.exp(-decay)
    powers(table_r, table_i, size * jnp.cos(turn), size * jnp.sin(turn), INNER)
    far = jnp.exp(-INNER * decay)
    far_r, far_i = far * jnp.cos(INNER * turn), far * jnp.sin(INNER * turn)
    total = decay.shape[0]
    summed[...] = grad_a[...].astype(f32) + grad_b[...].astype(f32)
    zero = jnp.zeros((total, channels), f32)

    def block(k, carry):
        a = length // INNER - 1 - k
        s0r, s0i, s1r, s1i = [held[q] for q in range(4)]
        s1r, s1i = s1r + INNER * s0r, s1i + INNER * s0i
        s0r, s0i = s0r * far_r - s0i * far_i, s0r * far_i + s0i * far_r
        s1r, s1i = s1r * far_r - s1i * far_i, s1r * far_i + s1i * far_r
        for q, value in enumerate((s0r, s0i, s1r, s1i)):
            held[q] = value
        rows = summed[pl.ds(pl.multiple_of(a * INNER, INNER), INNER), :]
        for c in range(total // 8):
            here = slice(c * 8, (c + 1) * 8)
            u0r, u0i, u1r, u1i = [held[q, here, :] for q in range(4)]
            for b in range(INNER):
                g = jnp.broadcast_to(rows[b : b + 1, :], (8, channels))
                tr, ti = g * table_r[b, here, :], g * table_i[b, here, :]
                u0r, u0i = u0r + tr, u0i + ti
                if b:
                    u1r, u1i = u1r + float(b) * tr, u1i + float(b) * ti
            for q, value in enumerate((u0r, u0i, u1r, u1i)):
                held[q, here, :] = value
        return carry

    for q in range(4):
        held[q] = zero
    lax.fori_loop(0, length // INNER, block, 0)
    s0r, s0i, s1r, s1i = [held[q] for q in range(4)]
    wr0 = w_re * s0r - w_im * s0i
    wr1 = w_re * s1r - w_im * s1i
    wi1 = w_re * s1i + w_im * s1r
    dt = jnp.sum(step * (wr0 - decay * wr1 - turn * wi1), axis=0, keepdims=True)
    held[0], held[1] = -step * decay * wr1, -step * step * wi1
    held[2], held[3] = step * s0r, -step * s0i
    rows_w = w_a.shape[1]
    lines = width // WIDE
    top = rows_w + 4 * states
    msg[...] = jnp.zeros_like(msg)
    for d in range(n):
        msg[d, 0:rows_w, : w_a.shape[2]] = (w_a[d].astype(f32) + w_b[d].astype(f32)).astype(bf16)
        for k in range(4):
            msg[d, rows_w + k * states : rows_w + (k + 1) * states, :channels] = held[
                k, d * states : (d + 1) * states, :
            ].astype(bf16)
    gain_sum = jnp.sum(gain8[...], axis=0, keepdims=True)
    bias_sum = jnp.sum(bias8[...], axis=0, keepdims=True)
    out_sum = jnp.sum(out8[...], axis=0, keepdims=True)
    copies = WIDE // channels
    lane = lax.broadcasted_iota(jnp.int32, (1, WIDE), 1) // channels
    skip_row = jnp.concatenate([summed[0:1, :]] * copies, axis=1) if copies > 1 else summed[0:1, :]
    dt_row = jnp.concatenate([dt] * copies, axis=1) if copies > 1 else dt
    for line in range(lines):
        at = slice(line * WIDE, (line + 1) * WIDE)
        mine = lane + line * copies == rank_t
        rows = [
            gain_sum[:, at],
            bias_sum[:, at],
            jnp.where(mine, dt_row, 0.0),
            jnp.where(mine, skip_row, 0.0),
            out_sum[:, at],
            out_sum[:, width + line * WIDE : width + (line + 1) * WIDE],
        ]
        for k, row in enumerate(rows):
            place = top + k * lines + line
            for d in range(n):
                msg[d, place : place + 1, :] = row.astype(bf16)


def taps_back(scalars, par, vec, grads, w_grads, gain8, bias8, out8, n, states):
    length, channels = grads[0].shape
    width = vec.shape[1]
    total = par.shape[1]
    w_grads = [w.reshape(n, channels, -1) for w in w_grads]
    rows = pad_to(channels + 4 * states + 6 * (width // WIDE), 16)
    return pl.pallas_call(
        partial(taps_back_kernel, n, states),
        out_shape=jax.ShapeDtypeStruct((n, rows, WIDE), bf16),
        in_specs=[sspec()] + [vspec()] * 9,
        out_specs=vspec(),
        scratch_shapes=[
            pltpu.VMEM((INNER, total, channels), f32),
            pltpu.VMEM((INNER, total, channels), f32),
            pltpu.VMEM((length, channels), f32),
            pltpu.VMEM((4, total, channels), f32),
        ],
        compiler_params=params(10),
        cost_estimate=cost(10),
        name="taps_back",
    )(scalars, par, vec, *grads, *w_grads, gain8, bias8, out8)


ROWS = 32
TILE = 16
LANES = 128


def normalize(x):
    width = x.shape[-1]
    mean = jnp.sum(x, axis=-1, keepdims=True) * (1.0 / width)
    centred = x - mean
    var = jnp.sum(centred * centred, axis=-1, keepdims=True) * (1.0 / width)
    scale = lax.rsqrt(var + epsilon)
    return centred * scale, scale


def tiles(first, last, width, body):
    def step(r, carry):
        row = pl.multiple_of(r * TILE, TILE)
        for c in range(width // LANES):
            body(row, slice(c * LANES, (c + 1) * LANES))
        return carry

    lax.fori_loop(first // TILE, last // TILE, step, 0)


def enter_kernel(n, blocks, block, sc, vec, basis_ref, *refs):
    pieces = refs[:n]
    tok_all, sig, xs = refs[n:]
    rank = sc[0]
    rows = pieces[0].shape[0]
    length, width = tok_all.shape
    for s in range(n):
        src = lax.rem(rank - s + n, n)
        tok_all[pl.ds(pl.multiple_of(src * rows, rows), rows), :] = pieces[s][...]

    def transform(j, carry):
        def norm(r, carry):
            at = pl.ds(pl.multiple_of(j * block + r * ROWS, ROWS), ROWS)
            xhat, _ = normalize(tok_all[at, :].astype(f32))
            sig[at, :] = (xhat * vec[0:1, :] + vec[1:2, :]).astype(bf16)
            return carry

        lax.fori_loop(0, block // ROWS, norm, 0)
        at = pl.ds(pl.multiple_of(j * block, block), block)
        xs[j] = jnp.dot(basis_ref[...], sig[at, :], preferred_element_type=f32)
        return carry

    lax.fori_loop(0, blocks, transform, 0)


def enter(scalars, vec, pieces, block):
    n = len(pieces)
    rows, width = pieces[0].shape
    length = rows * n
    blocks = length // block
    return pl.pallas_call(
        partial(enter_kernel, n, blocks, block),
        out_shape=[
            keep((length, width), bf16),
            keep((length, width), bf16),
            keep((blocks, 2 * block, width), f32),
        ],
        in_specs=[sspec()] + [vspec()] * (2 + n),
        out_specs=[vspec()] * 3,
        compiler_params=params(6),
        cost_estimate=cost(7),
        name="enter",
    )(scalars, vec, jnp.asarray(basis(block), bf16), *pieces)


def forward_kernel(n, n_t, blocks, block, sc, vec, b_out, basis_ref, basis_t, tok_all, sig, xs, *refs):
    tap_parts, w_parts = refs[:n_t], refs[n_t : 2 * n_t]
    outs = refs[2 * n_t : 2 * n_t + n]
    spec, w, active, slope, val_a, gate = refs[2 * n_t + n : 2 * n_t + n + 6]
    taps, raw, zs, mix, pre, out = refs[2 * n_t + n + 6 :]
    rank, seq_len, rank_t = sc[0], sc[1], sc[2]
    length, width = tok_all.shape
    channels = width // n_t
    half = block // 2
    scale = 1.0 / block
    for e in range(n_t):
        owner = rank_t ^ e
        at = pl.ds(pl.multiple_of(owner * channels, channels), channels)
        if channels % LANES == 0:
            taps[:, at] = tap_parts[e][...]
        else:
            for t in range(n_t):

                @pl.when(owner == t)
                def _(e=e, t=t):
                    taps[:, t * channels : (t + 1) * channels] = tap_parts[e][...]

        count, _, cols = w_parts[e].shape
        for d in range(count):
            w[at, d * cols : (d + 1) * cols] = w_parts[e][d]

    def spectrum(d, carry):
        at = pl.ds(pl.multiple_of(d * block, block), block)
        raw[d] = jnp.dot(basis_ref[...], taps[at, :], preferred_element_type=f32)
        return carry

    lax.fori_loop(0, blocks, spectrum, 0)

    def product(sign, row, lanes):
        re, im = pl.ds(row, TILE), pl.ds(pl.multiple_of(row + block, TILE), TILE)
        xr = [xs[j, re, lanes] for j in range(blocks)]
        xi = [xs[j, im, lanes] for j in range(blocks)]
        kr, ki = [], []
        for d in range(blocks):
            r, i = raw[d, re, lanes], raw[d, im, lanes]
            if d:
                pr, pi = raw[d - 1, re, lanes], raw[d - 1, im, lanes]
                r, i = (r - pi, i + pr) if sign > 0 else (r + pi, i - pr)
            kr.append(r * scale)
            ki.append(i * scale)
            spec[d, re, lanes] = kr[d].astype(bf16)
            spec[d, im, lanes] = ki[d].astype(bf16)
        for m in range(blocks):
            zr = zi = None
            for j in range(m + 1):
                d = m - j
                pr = xr[j] * kr[d] - xi[j] * ki[d]
                pi = xr[j] * ki[d] + xi[j] * kr[d]
                zr = pr if zr is None else zr + pr
                zi = pi if zi is None else zi + pi
            zs[m, re, lanes] = zr.astype(bf16)
            zs[m, im, lanes] = zi.astype(bf16)

    tiles(0, half, width, partial(product, 1))
    tiles(half, block, width, partial(product, -1))

    def tail(j, carry):
        mix[...] = jnp.dot(basis_t[...], zs[j], preferred_element_type=f32)

        def act(r, carry):
            at = pl.ds(pl.multiple_of(r * ROWS, ROWS), ROWS)
            to = pl.ds(pl.multiple_of(j * block + r * ROWS, ROWS), ROWS)
            v = mix[at, :] + vec[3:4, :] * sig[to, :].astype(f32)
            sq = v * v
            t = jnp.tanh(v * (0.7978845608 + (0.7978845608 * 0.044715) * sq))
            half_t = 0.5 + 0.5 * t
            active[to, :] = (v * half_t).astype(bf16)
            inner = 0.7978845608 + (0.7978845608 * 3.0 * 0.044715) * sq
            slope[to, :] = (half_t + 0.5 * v * (1.0 - t * t) * inner).astype(bf16)
            return carry

        lax.fori_loop(0, block // ROWS, act, 0)
        whole = pl.ds(pl.multiple_of(j * block, block), block)
        pre[...] = jnp.dot(active[whole, :], w[...], preferred_element_type=f32)

        def glu(r, carry):
            at = pl.ds(pl.multiple_of(r * ROWS, ROWS), ROWS)
            start = pl.multiple_of(j * block + r * ROWS, ROWS)
            to = pl.ds(start, ROWS)
            a = pre[at, :width] + b_out[:, :width]
            g = jax.nn.sigmoid(pre[at, width:] + b_out[:, width:])
            place = start + lax.broadcasted_iota(jnp.int32, (ROWS, width), 0)
            add = jnp.where(place < seq_len, a * g, 0.0)
            out[to, :] = (tok_all[to, :].astype(f32) + add).astype(bf16)
            val_a[to, :] = a.astype(bf16)
            gate[to, :] = g.astype(bf16)
            return carry

        lax.fori_loop(0, block // ROWS, glu, 0)
        return carry

    lax.fori_loop(0, blocks, tail, 0)
    rows = length // n
    for s in range(n):
        dst = lax.rem(rank + s, n)
        outs[s][...] = out[pl.ds(pl.multiple_of(dst * rows, rows), rows), :]


def forward(scalars, vec, b_out, entered, tap_parts, w_parts, n, block):
    tok_all, sig, xs = entered
    n_t = len(tap_parts)
    length, width = tok_all.shape
    blocks = length // block
    table = basis(block)
    full = keep((length, width), bf16)
    return pl.pallas_call(
        partial(forward_kernel, n, n_t, blocks, block),
        out_shape=[jax.ShapeDtypeStruct((length // n, width), bf16)] * n
        + [
            keep((blocks, 2 * block, width), bf16),
            keep((width, 2 * width), bf16),
            full,
            full,
            full,
            full,
        ],
        in_specs=[sspec()] + [vspec()] * (7 + 2 * n_t),
        out_specs=[vspec()] * (n + 6),
        scratch_shapes=[
            pltpu.VMEM((length, width), bf16),
            pltpu.VMEM((blocks, 2 * block, width), f32),
            pltpu.VMEM((blocks, 2 * block, width), bf16),
            pltpu.VMEM((block, width), f32),
            pltpu.VMEM((block, 2 * width), f32),
            pltpu.VMEM((length, width), bf16),
        ],
        compiler_params=params(15),
        cost_estimate=cost(15),
        name="forward",
    )(
        scalars,
        vec,
        b_out,
        jnp.asarray(table, bf16),
        jnp.asarray(table.T, bf16),
        *held_in_vmem(tok_all, sig, xs),
        *tap_parts,
        *w_parts,
    )


def mix_back_kernel(n, blocks, block, sc, basis_ref, basis_t, w, xs, slope, val_a, gate, *refs):
    pieces = refs[:n]
    taps_keep, taps_send, grad_pre, grad_mix, spec_g, cot, bias_grad, act_f, comb = refs[n:]
    rank, seq_len, core = sc[0], sc[1], sc[2] & 1
    length, width = cot.shape
    rows = length // n
    for s in range(n):
        src = lax.rem(rank - s + n, n)
        cot[pl.ds(pl.multiple_of(src * rows, rows), rows), :] = pieces[s][...]
    half = block // 2
    bias_grad[...] = jnp.zeros_like(bias_grad)

    def front(j, carry):
        def glu(r, carry):
            start = pl.multiple_of(j * block + r * ROWS, ROWS)
            to = pl.ds(start, ROWS)
            place = start + lax.broadcasted_iota(jnp.int32, (ROWS, width), 0)
            q = jnp.where(place < seq_len, cot[to, :].astype(f32), 0.0)
            a, g = val_a[to, :].astype(f32), gate[to, :].astype(f32)
            qg = q * g
            ga = qg.astype(bf16)
            gb = (qg * a * (1.0 - g)).astype(bf16)
            grad_pre[to, :width] = ga
            grad_pre[to, width:] = gb
            ga, gb = ga.astype(f32), gb.astype(f32)
            bias_grad[:, :width] += jnp.sum(ga.reshape(ROWS // 8, 8, width), axis=0)
            bias_grad[:, width:] += jnp.sum(gb.reshape(ROWS // 8, 8, width), axis=0)
            return carry

        lax.fori_loop(0, block // ROWS, glu, 0)
        whole = pl.ds(pl.multiple_of(j * block, block), block)
        act_f[...] = lax.dot_general(
            grad_pre[whole, :], w[...], (((1,), (1,)), ((), ())), preferred_element_type=f32
        )

        def back(r, carry):
            at = pl.ds(pl.multiple_of(r * ROWS, ROWS), ROWS)
            to = pl.ds(pl.multiple_of(j * block + r * ROWS, ROWS), ROWS)
            grad = act_f[at, :].astype(bf16).astype(f32) * slope[to, :].astype(f32)
            grad_mix[to, :] = grad.astype(bf16)
            return carry

        lax.fori_loop(0, block // ROWS, back, 0)
        spec_g[j] = jnp.dot(basis_ref[...], grad_mix[whole, :], preferred_element_type=f32)
        return carry

    lax.fori_loop(0, blocks, front, 0)

    def correlate(sign, row, lanes):
        re, im = pl.ds(row, TILE), pl.ds(pl.multiple_of(row + block, TILE), TILE)
        xr = [xs[j, re, lanes] for j in range(blocks)]
        xi = [xs[j, im, lanes] for j in range(blocks)]
        gr = [spec_g[j, re, lanes] for j in range(blocks)]
        gi = [spec_g[j, im, lanes] for j in range(blocks)]
        next_r = next_i = None
        for d in reversed(range(blocks)):
            dr = di = None
            for m in range(d, blocks):
                j = m - d
                pr = xr[j] * gr[m] + xi[j] * gi[m]
                pi = xr[j] * gi[m] - xi[j] * gr[m]
                dr = pr if dr is None else dr + pr
                di = pi if di is None else di + pi
            cr, ci = dr, di
            if next_r is not None:
                cr = dr + next_i if sign > 0 else dr - next_i
                ci = di - next_r if sign > 0 else di + next_r
            comb[d, re, lanes] = cr.astype(bf16)
            comb[d, im, lanes] = ci.astype(bf16)
            next_r, next_i = dr, di

    tiles(0, half, width, partial(correlate, 1))
    tiles(half, block, width, partial(correlate, -1))
    groups, _, channels = taps_keep.shape

    def finish(d, carry):
        act_f[...] = jnp.dot(basis_t[...], comb[d], preferred_element_type=f32)
        to = pl.ds(pl.multiple_of(d * block, block), block)
        for t in range(2 * groups):
            part = (act_f[:, t * channels : (t + 1) * channels] * (1.0 / block)).astype(bf16)

            @pl.when(core == t & 1)
            def _(t=t, part=part):
                taps_keep[t >> 1, to, :] = part

            @pl.when(core != t & 1)
            def _(t=t, part=part):
                taps_send[t >> 1, to, :] = part

        return carry

    lax.fori_loop(0, blocks, finish, 0)


def mix_back(scalars, pieces, w, xs, slope, val_a, gate, block, n_t):
    n = len(pieces)
    length, width = slope.shape
    blocks = length // block
    table = basis(block)
    halves = jax.ShapeDtypeStruct((n_t // 2, length, width // n_t), bf16)
    return pl.pallas_call(
        partial(mix_back_kernel, n, blocks, block),
        out_shape=[
            halves,
            halves,
            keep((length, 2 * width), bf16),
            keep((length, width), bf16),
            keep((blocks, 2 * block, width), f32),
            keep((length, width), bf16),
            jax.ShapeDtypeStruct((8, 2 * width), f32),
        ],
        in_specs=[sspec()] + [vspec()] * (7 + n),
        out_specs=[vspec()] * 7,
        scratch_shapes=[
            pltpu.VMEM((block, width), f32),
            pltpu.VMEM((blocks, 2 * block, width), bf16),
        ],
        compiler_params=params(8),
        cost_estimate=cost(13),
        name="mix_back",
    )(
        scalars,
        jnp.asarray(table, bf16),
        jnp.asarray(table.T, bf16),
        *held_in_vmem(w, xs, slope, val_a, gate),
        *pieces,
    )


def weight_back_kernel(n, sc, active, grad_pre, w_keep, w_send):
    core = sc[2] & 1
    groups = w_keep.shape[0]
    _, _, channels, cols = w_keep.shape
    for t in range(2 * groups):
        part = lax.dot_general(
            active[:, t * channels : (t + 1) * channels],
            grad_pre[...],
            (((0,), (0,)), ((), ())),
            preferred_element_type=f32,
        ).astype(bf16)

        @pl.when(core == t & 1)
        def _(t=t, part=part):
            for d in range(n):
                w_keep[t >> 1, d] = part[:, d * cols : (d + 1) * cols]

        @pl.when(core != t & 1)
        def _(t=t, part=part):
            for d in range(n):
                w_send[t >> 1, d] = part[:, d * cols : (d + 1) * cols]


def weight_back(scalars, active, grad_pre, n, n_t):
    width = active.shape[1]
    halves = jax.ShapeDtypeStruct((n_t // 2, n, width // n_t, 2 * width // n), bf16)
    return pl.pallas_call(
        partial(weight_back_kernel, n),
        out_shape=[halves, halves],
        in_specs=[sspec()] + [vspec()] * 2,
        out_specs=[vspec()] * 2,
        compiler_params=params(6),
        cost_estimate=cost(4),
        name="weight_back",
    )(scalars, *held_in_vmem(active, grad_pre))


def norm_back_kernel(n, blocks, block, sc, vec, basis_t, spec, spec_g, grad_mix, tok_all, cot_all, *refs):
    outs = refs[:n]
    gain_grad, bias_grad = refs[n : n + 2]
    comb, sig_f, res = refs[n + 2 :]
    rank = sc[0]
    rows = outs[0].shape[0]
    length, width = tok_all.shape
    gain_grad[...] = jnp.zeros_like(gain_grad)
    bias_grad[...] = jnp.zeros_like(bias_grad)

    def correlate(row, lanes):
        re, im = pl.ds(row, TILE), pl.ds(pl.multiple_of(row + block, TILE), TILE)
        kr = [spec[j, re, lanes].astype(f32) for j in range(blocks)]
        ki = [spec[j, im, lanes].astype(f32) for j in range(blocks)]
        gr = [spec_g[j, re, lanes] for j in range(blocks)]
        gi = [spec_g[j, im, lanes] for j in range(blocks)]
        for j in range(blocks):
            dr = di = None
            for m in range(j, blocks):
                d = m - j
                pr = kr[d] * gr[m] + ki[d] * gi[m]
                pi = kr[d] * gi[m] - ki[d] * gr[m]
                dr = pr if dr is None else dr + pr
                di = pi if di is None else di + pi
            comb[j, re, lanes] = dr.astype(bf16)
            comb[j, im, lanes] = di.astype(bf16)

    tiles(0, block, width, correlate)

    def finish(j, carry):
        sig_f[...] = jnp.dot(basis_t[...], comb[j], preferred_element_type=f32)

        def norm(r, carry):
            at = pl.ds(pl.multiple_of(r * ROWS, ROWS), ROWS)
            to = pl.ds(pl.multiple_of(j * block + r * ROWS, ROWS), ROWS)
            grad = sig_f[at, :] + vec[3:4, :] * grad_mix[to, :].astype(f32)
            grad = grad.astype(bf16).astype(f32)
            xhat, scale = normalize(tok_all[to, :].astype(f32))
            gx = grad * xhat
            gain_grad[...] += jnp.sum(gx.reshape(ROWS // 8, 8, width), axis=0)
            bias_grad[...] += jnp.sum(grad.reshape(ROWS // 8, 8, width), axis=0)
            g = grad * vec[0:1, :]
            mean_g = jnp.sum(g, axis=-1, keepdims=True) * (1.0 / width)
            mean_gx = jnp.sum(g * xhat, axis=-1, keepdims=True) * (1.0 / width)
            out = cot_all[to, :].astype(f32) + (g - mean_g - xhat * mean_gx) * scale
            res[to, :] = out.astype(bf16)
            return carry

        lax.fori_loop(0, block // ROWS, norm, 0)
        return carry

    lax.fori_loop(0, blocks, finish, 0)
    for s in range(n):
        dst = lax.rem(rank + s, n)
        outs[s][...] = res[pl.ds(pl.multiple_of(dst * rows, rows), rows), :]


def norm_back(scalars, vec, spec, spec_g, grad_mix, tok_all, cot_all, n, block):
    length, width = tok_all.shape
    blocks = length // block
    rows = length // n
    res = pl.pallas_call(
        partial(norm_back_kernel, n, blocks, block),
        out_shape=[jax.ShapeDtypeStruct((rows, width), bf16)] * n
        + [jax.ShapeDtypeStruct((8, width), f32)] * 2,
        in_specs=[sspec()] + [vspec()] * 7,
        out_specs=[vspec()] * (n + 2),
        scratch_shapes=[
            pltpu.VMEM((blocks, 2 * block, width), bf16),
            pltpu.VMEM((block, width), f32),
            pltpu.VMEM((length, width), bf16),
        ],
        compiler_params=params(8),
        cost_estimate=cost(12),
        name="norm_back",
    )(
        scalars,
        vec,
        jnp.asarray(basis(block).T, bf16),
        *held_in_vmem(spec, spec_g, grad_mix, tok_all, cot_all),
    )
    return res[:n], res[n], res[n + 1]


def halve_kernel(shift, sc, kept, got, keep_out, send_out):
    here = (sc[2] >> shift) & 1
    for i in range(keep_out.shape[0]):
        for k in range(2):
            value = (kept[2 * i + k].astype(f32) + got[2 * i + k].astype(f32)).astype(bf16)

            @pl.when(here == k)
            def _(i=i, value=value):
                keep_out[i] = value

            @pl.when(here != k)
            def _(i=i, value=value):
                send_out[i] = value


def halve(scalars, kept, got, shift):
    shape = jax.ShapeDtypeStruct((kept.shape[0] // 2, *kept.shape[1:]), bf16)
    return pl.pallas_call(
        partial(halve_kernel, shift),
        out_shape=[shape, shape],
        in_specs=[sspec(), vspec(), vspec()],
        out_specs=[vspec()] * 2,
        compiler_params=params(5),
        cost_estimate=cost(1),
        name="halve",
    )(scalars, kept, got)


def weave_kernel(n, sc, *refs):
    pieces, out, held = refs[:n], refs[n], refs[n + 1]
    rank = sc[0]
    rows, width = pieces[0].shape
    step = min(rows, 32)

    def part(r, carry):
        at = pl.ds(pl.multiple_of(r * step, step), step)
        for s in range(n):
            src = lax.rem(rank - s + n, n)
            for c in range(width // LANES):
                lanes = slice(c * LANES, (c + 1) * LANES)
                held[c, pl.ds(src, step, stride=n), :] = pieces[s][at, lanes].astype(f32)
        for c in range(width // LANES):
            lanes = slice(c * LANES, (c + 1) * LANES)
            out[at, :, lanes] = held[c].reshape(step, n, LANES).astype(bf16)
        return carry

    lax.fori_loop(0, rows // step, part, 0)


def weave(scalars, pieces):
    n = len(pieces)
    rows, width = pieces[0].shape
    return pl.pallas_call(
        partial(weave_kernel, n),
        out_shape=jax.ShapeDtypeStruct((rows, n, width), bf16),
        in_specs=[sspec()] + [vspec()] * n,
        out_specs=vspec(),
        scratch_shapes=[pltpu.VMEM((width // LANES, min(rows, 32) * n, LANES), f32)],
        compiler_params=params(8),
        cost_estimate=cost(3),
        name="weave",
    )(scalars, *pieces)


def part_kernel(n, sc, whole, *refs):
    outs, held = refs[:n], refs[n]
    rank = sc[0]
    rows, _, width = whole.shape
    step = min(rows, 32)

    def part(r, carry):
        at = pl.ds(pl.multiple_of(r * step, step), step)
        for c in range(width // LANES):
            lanes = slice(c * LANES, (c + 1) * LANES)
            held[c] = whole[at, :, lanes].astype(f32).reshape(step * n, LANES)
        for s in range(n):
            dst = lax.rem(rank + s, n)
            for c in range(width // LANES):
                lanes = slice(c * LANES, (c + 1) * LANES)
                outs[s][at, lanes] = held[c, pl.ds(dst, step, stride=n), :].astype(bf16)
        return carry

    lax.fori_loop(0, rows // step, part, 0)


def part(scalars, whole):
    rows, n, width = whole.shape
    return pl.pallas_call(
        partial(part_kernel, n),
        out_shape=[jax.ShapeDtypeStruct((rows, width), bf16)] * n,
        in_specs=[sspec(), vspec()],
        out_specs=[vspec()] * n,
        scratch_shapes=[pltpu.VMEM((width // LANES, min(rows, 32) * n, LANES), f32)],
        compiler_params=params(8),
        cost_estimate=cost(3),
        name="part",
    )(scalars, whole)


def total_kernel(states, msg, w_out, g0, g1, g2, g3, vec_out):
    channels, cols = w_out.shape
    total = msg[0].astype(f32)
    for d in range(1, msg.shape[0]):
        total = total + msg[d].astype(f32)
    w_out[...] = total[:channels, :cols]
    for k, ref in enumerate((g0, g1, g2, g3)):
        ref[...] = total[channels + k * states : channels + (k + 1) * states, :channels].T
    top = channels + 4 * states
    vec_out[...] = total[top : top + vec_out.shape[0], :]


def totals(msg, channels, cols, states, lines):
    grad = jax.ShapeDtypeStruct((channels, states), f32)
    return pl.pallas_call(
        partial(total_kernel, states),
        out_shape=[jax.ShapeDtypeStruct((channels, cols), f32)]
        + [grad] * 4
        + [jax.ShapeDtypeStruct((6 * lines, WIDE), f32)],
        in_specs=[vspec()],
        out_specs=[vspec()] * 6,
        compiler_params=params(4),
        cost_estimate=cost(1),
        name="totals",
    )(msg)


def shares_kernel(lines, sc, *refs):
    count = len(refs) - 5
    outs = refs[count:]
    rank = sc[0]
    total = refs[0][...]
    for ref in refs[1:count]:
        total = total + ref[...]
    for k, out in enumerate(outs):
        per = out.shape[1]
        slots = (2 * lines if k == 4 else lines) * WIDE // per
        value = jnp.zeros((1, per), f32)
        for slot in range(slots):
            line, lane = divmod(slot * per, WIDE)
            here = total[k * lines + line : k * lines + line + 1, lane : lane + per]
            value = jnp.where(rank == slot, here, value)
        out[...] = value


def shares(scalars, vectors, per, lines):
    one = jax.ShapeDtypeStruct((1, per), f32)
    return pl.pallas_call(
        partial(shares_kernel, lines),
        out_shape=[one] * 4 + [jax.ShapeDtypeStruct((1, 2 * per), f32)],
        in_specs=[sspec()] + [vspec()] * len(vectors),
        out_specs=[vspec()] * 5,
        compiler_params=params(4),
        cost_estimate=cost(1),
        name="shares",
    )(scalars, *vectors)


def local(n_dp, n_t, tokens, cotangent, lengths, ln_gain, ln_bias, lam_log, lam_im, w_re, w_im, log_dt, skip_gain, w_out, b_out):
    rows, seqs, width = tokens.shape
    assert seqs == n_dp
    length = rows * n_dp
    block = min(256, length)
    rank = lax.axis_index("dp")
    rank_t = lax.axis_index("tensor")
    channels, states = lam_log.shape
    cols = w_out.shape[1]
    per = width // n_dp
    bits = [1 << k for k in range(n_t.bit_length() - 1)]
    seq_len = lax.dynamic_index_in_dim(lengths, rank_t * n_dp + rank, 0, keepdims=False)
    scalars = jnp.stack([rank, seq_len, rank_t]).astype(jnp.int32)

    vec = jnp.concatenate([ln_gain, ln_bias, log_dt, skip_gain, b_out])
    vec_rows = VEC_ROWS(per)
    vec = jnp.pad(vec, (0, vec_rows * WIDE - vec.shape[0])).reshape(vec_rows, WIDE)
    par = jnp.concatenate([lam_log.T, lam_im.T, w_re.T, w_im.T], axis=0)
    par = jnp.pad(par, ((0, 0), (0, WIDE - channels)))
    blob = pack_weights(n_dp, par, vec, jnp.pad(w_out, ((0, 0), (0, WIDE - cols))))
    blob = lax.all_to_all(blob, "dp", 0, 0, tiled=True)

    after = lambda value, *others: lax.optimization_barrier((value, others))[0]
    tok_pieces = shift_exchange(part(scalars, tokens), "dp", n_dp)
    cot_pieces = list(part(scalars, cotangent))
    depth = 5
    for s in range(1, min(depth + 1, n_dp)):
        cot_pieces[s] = after(cot_pieces[s], tok_pieces[min(s + 2, n_dp - 1)])
    blob = after(blob, tok_pieces[1])

    taps, w_own, par_all, vec, b_full = make_taps(
        scalars, blob, states, length, width, channels, cols
    )

    def spread(own):
        parts = {0: own}
        for bit in reversed(bits):
            for e in list(parts):
                parts[e | bit] = flip_bit(parts[e], "tensor", n_t, bit)
        return [parts[e] for e in range(n_t)]

    tap_parts = spread(taps)
    w_parts = spread(w_own)

    entered = enter(scalars, vec, tok_pieces, block)
    tok_all, sig, xs = entered
    for s in range(depth + 1, n_dp):
        cot_pieces[s] = after(cot_pieces[s], sig)
    cot_pieces = shift_exchange(cot_pieces, "dp", n_dp)
    first = cot_pieces[1 : min(3, n_dp)]
    res = forward(scalars, after(vec, first), b_full, entered, tap_parts, w_parts, n_dp, block)
    out_back = shift_exchange(list(res[:n_dp]), "dp", n_dp)
    spec, w_full, active, slope, val_a, gate = res[n_dp:]
    taps_keep, taps_send, grad_pre, grad_mix, spec_g, cot, out8 = mix_back(
        scalars, cot_pieces, w_full, xs, slope, val_a, gate, block, n_t
    )
    active = after(active, out_back[1:4])
    spec_g = after(spec_g, out_back[4 : depth + 1])
    w_keep, w_send = weight_back(scalars, active, grad_pre, n_dp, n_t)

    def reduce_groups(kept, sent):
        got = flip_bit(sent, "tensor", n_t, 1)
        for k, bit in enumerate(bits[1:]):
            kept, sent = halve(scalars, kept, got, k + 1)
            got = flip_bit(sent, "tensor", n_t, bit)
        return kept[0], got[0]

    taps_two = reduce_groups(taps_keep, taps_send)
    grad_pieces, gain8, bias8 = norm_back(
        scalars, vec, spec, spec_g, grad_mix, tok_all, cot, n_dp, block
    )
    grad_back = shift_exchange(grad_pieces, "dp", n_dp)
    out8 = after(out8, out_back[depth + 1 :])
    w_two = reduce_groups(w_keep, w_send)
    msg = taps_back(scalars, par_all, vec, taps_two, w_two, gain8, bias8, out8, n_dp, states)
    msg = after(msg, grad_back[1 : depth + 1])
    msg = lax.all_to_all(msg, "dp", 0, 0, tiled=True)
    lines = width // WIDE
    grad_w_out, g_lam_log, g_lam_im, g_w_re, g_w_im, vec_sum = totals(
        msg, channels, cols, states, lines
    )
    others = [
        lax.ppermute(vec_sum, "tensor", [(k, k ^ e) for k in range(n_t)]) for e in range(1, n_t)
    ]
    g_gain, g_bias, g_dt, g_skip, g_b = (
        v.reshape(-1) for v in shares(scalars, [vec_sum, *others], per, lines)
    )

    out = weave(scalars, out_back)
    grad_tokens = weave(scalars, grad_back)
    return (
        out,
        grad_tokens,
        g_gain,
        g_bias,
        g_lam_log,
        g_lam_im,
        g_w_re,
        g_w_im,
        g_dt,
        g_skip,
        grad_w_out,
        g_b,
    )


def solution(mesh):
    big = P("dp", "tensor", None)
    grid = P("tensor", "dp")
    line = P("dp")
    return jax.shard_map(
        partial(local, mesh.shape["dp"], mesh.shape["tensor"]),
        mesh=mesh,
        in_specs=(big, big, P(), line, line, grid, grid, grid, grid, line, line, grid, line),
        out_specs=(big, big, line, line, grid, grid, grid, grid, line, line, grid, line),
        check_vma=False,
    )
```

profile of v0, /device:TPU:0, one launch (start us, length us, event | category | flops | bytes accessed | tf_op | source)
XLA Modules:
  0.0 186.5 jit_solution(5239682310265066332)
XLA Ops:
  3.9 7.3 %all-to-all-start = ((bf16[8,240,128]{2,1,0:T(8,128)(2,1)}), bf16[8,240,128]{2,1,0:T(8,128)(2,1)S(1)}, u32[]{:S(2)}, u32[]{:S(2)}) async-start(bf16[8,240,128]{2,1,0:T(8,128)(2,1)} %pack_weights.1), calls=%async_computation | async-start | bytes 983040 | tf_op jit(solution)/shard_map/all_to_all | solution.py:934
  15.6 2.1 %collective-permute-start = (bf16[128,512]{1,0:T(8,128)(2,1)S(1)}, bf16[128,512]{1,0:T(8,128)(2,1)S(1)}, u32[]{:S(2)}, u32[]{:S(2)}) collective-permute-start(bf16[128,512]{1,0:T(8,128)(2,1)S(1)} %get-tuple-element.97), channel_id=1, source_target_pairs={{0,4},{4,8},{8,12},{12,16},{16,20},{20,24},{24,28},{28,0},{1,5},{5... | collective-permute-start | bytes 393224 | tf_op jit(solution)/shard_map/ppermute | solution.py:50
  17.6 2.4 %collective-permute-start.1 = (bf16[128,512]{1,0:T(8,128)(2,1)S(1)}, bf16[128,512]{1,0:T(8,128)(2,1)S(1)}, u32[]{:S(2)}, u32[]{:S(2)}) collective-permute-start(bf16[128,512]{1,0:T(8,128)(2,1)S(1)} %get-tuple-element.101), channel_id=1, source_target_pairs={{0,12},{4,16},{8,20},{12,24},{16,28},{20,0},{24,4},{28,8},{1,13},{... | collective-permute-start | bytes 393224 | tf_op jit(solution)/shard_map/ppermute | solution.py:50
  21.0 2.9 %collective-permute-start.6 = (bf16[128,512]{1,0:T(8,128)(2,1)S(1)}, bf16[128,512]{1,0:T(8,128)(2,1)S(1)}, u32[]{:S(2)}, u32[]{:S(2)}) collective-permute-start(bf16[128,512]{1,0:T(8,128)(2,1)S(1)} %get-tuple-element.110), channel_id=1, source_target_pairs={{0,20},{4,24},{8,28},{12,0},{16,4},{20,8},{24,12},{28,16},{1,21},{... | collective-permute-start | bytes 393224 | tf_op jit(solution)/shard_map/ppermute | solution.py:50
  23.8 4.6 %collective-permute-done.refs_1_ = bf16[128,512]{1,0:T(8,128)(2,1)S(1)} collective-permute-done((bf16[128,512]{1,0:T(8,128)(2,1)S(1)}, bf16[128,512]{1,0:T(8,128)(2,1)S(1)}, u32[]{:S(2)}, u32[]{:S(2)}) %collective-permute-start) | collective-permute-done | bytes 131104 | tf_op jit(solution)/shard_map/ppermute | solution.py:50
  28.5 6.4 %all-to-all-done.blob = bf16[8,240,128]{2,1,0:T(8,128)(2,1)S(1)} async-done(((bf16[8,240,128]{2,1,0:T(8,128)(2,1)}), bf16[8,240,128]{2,1,0:T(8,128)(2,1)S(1)}, u32[]{:S(2)}, u32[]{:S(2)}) %all-to-all-start) | async-done | bytes 491552 | tf_op jit(solution)/shard_map/all_to_all | solution.py:934
  34.8 6.1 %taps.1 = (bf16[1024,128]{1,0:T(8,128)(2,1)S(1)}, bf16[8,128,128]{2,1,0:T(8,128)(2,1)S(1)}, f32[4,64,128]{2,1,0:T(8,128)S(1)}, f32[8,512]{1,0:T(8,128)S(1)}, f32[1,1024]{1,0:T(1,128)S(1)}) custom-call(s32[3]{0:T(128)S(1)} %pad_add_fusion.sc, bf16[8,240,128]{2,1,0:T(8,128)(2,1)S(1)} %all-to-all-done.blob), custom_call_target="tpu_custom_call" | custom-call | bytes 23100000 | tf_op jit(solution)/shard_map/taps/pallas_call | solution.py:162
  43.1 3.4 %collective-permute-start.8 = (bf16[128,512]{1,0:T(8,128)(2,1)S(1)}, bf16[128,512]{1,0:T(8,128)(2,1)S(1)}, u32[]{:S(2)}, u32[]{:S(2)}) collective-permute-start(bf16[128,512]{1,0:T(8,128)(2,1)S(1)} %get-tuple-element.112), channel_id=1, source_target_pairs={{0,28},{4,0},{8,4},{12,8},{16,12},{20,16},{24,20},{28,24},{1,29},{... | collective-permute-start | bytes 393224 | tf_op jit(solution)/shard_map/ppermute | solution.py:50
  50.4 6.3 %collective-permute-done.5.refs_2_ = bf16[128,512]{1,0:T(8,128)(2,1)S(1)} collective-permute-done((bf16[128,512]{1,0:T(8,128)(2,1)S(1)}, bf16[128,512]{1,0:T(8,128)(2,1)S(1)}, u32[]{:S(2)}, u32[]{:S(2)}) %collective-permute-start.5) | collective-permute-done | bytes 131104 | tf_op jit(solution)/shard_map/ppermute | solution.py:50
  57.7 7.2 %collective-permute-done.4.refs_2_ = bf16[128,512]{1,0:T(8,128)(2,1)S(1)} collective-permute-done((bf16[128,512]{1,0:T(8,128)(2,1)S(1)}, bf16[128,512]{1,0:T(8,128)(2,1)S(1)}, u32[]{:S(2)}, u32[]{:S(2)}) %collective-permute-start.4) | collective-permute-done | bytes 131104 | tf_op jit(solution)/shard_map/ppermute | solution.py:50
  64.9 3.9 %collective-permute-start.24 = (bf16[128,512]{1,0:T(8,128)(2,1)S(1)}, bf16[128,512]{1,0:T(8,128)(2,1)S(1)}, u32[]{:S(2)}, u32[]{:S(2)}) collective-permute-start(bf16[128,512]{1,0:T(8,128)(2,1)S(1)} %get-tuple-element.137), channel_id=1, source_target_pairs={{0,20},{4,24},{8,28},{12,0},{16,4},{20,8},{24,12},{28,16},{1,21},{... | collective-permute-start | bytes 393224 | tf_op jit(solution)/shard_map/ppermute | solution.py:50
  68.8 7.6 %enter.1 = (bf16[1024,512]{1,0:T(8,128)(2,1)S(1)}, bf16[1024,512]{1,0:T(8,128)(2,1)S(1)}, f32[4,512,512]{2,1,0:T(8,128)S(1)}) custom-call(s32[3]{0:T(128)S(1)} %pad_add_fusion.sc, f32[8,512]{1,0:T(8,128)S(1)} %get-tuple-element.106.vec, bf16[512,256]{1,0:T(8,128)(2,1)S(1)} %copy-done.1, bf16[128,512]{1,0:T(8,128)(2,1)S(1)} %get-tuple-element.108.refs_0_, ...), custom_call_target="tpu_custom_call" | custom-call | bytes 23100000 | tf_op jit(solution)/shard_map/enter/pallas_call | solution.py:346
  78.0 10.0 %forward.1 = (bf16[128,512]{1,0:T(8,128)(2,1)S(1)}, bf16[128,512]{1,0:T(8,128)(2,1)S(1)}, bf16[128,512]{1,0:T(8,128)(2,1)S(1)}, bf16[128,512]{1,0:T(8,128)(2,1)S...) custom-call(s32[3]{0:T(128)S(1)} %pad_add_fusion.sc, ...), custom_call_target="tpu_custom_call" | custom-call | bytes 49500000 | tf_op jit(solution)/shard_map/forward/pallas_call | solution.py:471
  90.6 2.4 %collective-permute-start.17 = (bf16[128,512]{1,0:T(8,128)(2,1)S(1)}, bf16[128,512]{1,0:T(8,128)(2,1)S(1)}, u32[]{:S(2)}, u32[]{:S(2)}) collective-permute-start(bf16[128,512]{1,0:T(8,128)(2,1)S(1)} %get-tuple-element.121), channel_id=1, source_target_pairs={{0,12},{4,16},{8,20},{12,24},{16,28},{20,0},{24,4},{28,8},{1,13},{... | collective-permute-start | bytes 393224 | tf_op jit(solution)/shard_map/ppermute | solution.py:50
  93.0 8.6 %mix_back.1 = (bf16[2,1024,128]{2,1,0:T(8,128)(2,1)S(1)}, bf16[2,1024,128]{2,1,0:T(8,128)(2,1)S(1)}, bf16[1024,1024]{1,0:T(8,128)(2,1)S(1)}, bf16[1024,512]{1,0:...) custom-call(s32[3]{0:T(128)S(1)} %pad_add_fusion.sc, ...), custom_call_target="tpu_custom_call" | custom-call | bytes 42900000 | tf_op jit(solution)/shard_map/mix_back/pallas_call | solution.py:607
  101.7 1.7 collective-permute-done.17.refs_3_
  103.4 2.5 %weight_back.1 = (bf16[2,8,128,128]{3,2,1,0:T(8,128)(2,1)S(1)}, bf16[2,8,128,128]{3,2,1,0:T(8,128)(2,1)S(1)}) custom-call(s32[3]{0:T(128)S(1)} %pad_add_fusion.sc, bf16[1024,512]{1,0:T(8,128)(2,1)S(1)} %get-tuple-element.160.active, bf16[1024,1024]{1,0:T(8,128)(2,1)S(1)} %get-tuple-element.161.grad_pre), custom_call_target="tpu_custom_call" | custom-call | bytes 13200000 | tf_op jit(solution)/shard_map/weight_back/pallas_call | solution.py:662
  110.8 2.0 %collective-permute-start.19 = (bf16[128,512]{1,0:T(8,128)(2,1)S(1)}, bf16[128,512]{1,0:T(8,128)(2,1)S(1)}, u32[]{:S(2)}, u32[]{:S(2)}) collective-permute-start(bf16[128,512]{1,0:T(8,128)(2,1)S(1)} %get-tuple-element.123), channel_id=1, source_target_pairs={{0,20},{4,24},{8,28},{12,0},{16,4},{20,8},{24,12},{28,16},{1,21},{... | collective-permute-start | bytes 393224 | tf_op jit(solution)/shard_map/ppermute | solution.py:50
  113.8 2.3 %collective-permute-done.18.refs_4_ = bf16[128,512]{1,0:T(8,128)(2,1)S(1)} collective-permute-done((bf16[128,512]{1,0:T(8,128)(2,1)S(1)}, bf16[128,512]{1,0:T(8,128)(2,1)S(1)}, u32[]{:S(2)}, u32[]{:S(2)}) %collective-permute-start.18) | collective-permute-done | bytes 131104 | tf_op jit(solution)/shard_map/ppermute | solution.py:50
  116.4 1.7 collective-permute-done.19.refs_5_
  118.1 12.0 %norm_back.1 = (bf16[128,512]{1,0:T(8,128)(2,1)S(1)}, bf16[128,512]{1,0:T(8,128)(2,1)S(1)}, bf16[128,512]{1,0:T(8,128)(2,1)S(1)}, bf16[128,512]{1,0:T(8,128)(2,1...) custom-call(s32[3]{0:T(128)S(1)} %pad_add_fusion.sc, ...), custom_call_target="tpu_custom_call" | custom-call | bytes 39600000 | tf_op jit(solution)/shard_map/norm_back/pallas_call | solution.py:734
  130.1 3.4 %collective-permute-start.27 = (bf16[128,512]{1,0:T(8,128)(2,1)S(1)}, bf16[128,512]{1,0:T(8,128)(2,1)S(1)}, u32[]{:S(2)}, u32[]{:S(2)}) collective-permute-start(bf16[128,512]{1,0:T(8,128)(2,1)S(1)} %get-tuple-element.147), channel_id=1, source_target_pairs={{0,4},{4,8},{8,12},{12,16},{16,20},{20,24},{24,28},{28,0},{1,5},{5... | collective-permute-start | bytes 393224 | tf_op jit(solution)/shard_map/ppermute | solution.py:50
  133.5 3.3 %collective-permute-start.28 = (bf16[128,512]{1,0:T(8,128)(2,1)S(1)}, bf16[128,512]{1,0:T(8,128)(2,1)S(1)}, u32[]{:S(2)}, u32[]{:S(2)}) collective-permute-start(bf16[128,512]{1,0:T(8,128)(2,1)S(1)} %get-tuple-element.148), channel_id=1, source_target_pairs={{0,8},{4,12},{8,16},{12,20},{16,24},{20,28},{24,0},{28,4},{1,9},{5... | collective-permute-start | bytes 393224 | tf_op jit(solution)/shard_map/ppermute | solution.py:50
  136.9 2.8 %collective-permute-start.29 = (bf16[128,512]{1,0:T(8,128)(2,1)S(1)}, bf16[128,512]{1,0:T(8,128)(2,1)S(1)}, u32[]{:S(2)}, u32[]{:S(2)}) collective-permute-start(bf16[128,512]{1,0:T(8,128)(2,1)S(1)} %get-tuple-element.149), channel_id=1, source_target_pairs={{0,12},{4,16},{8,20},{12,24},{16,28},{20,0},{24,4},{28,8},{1,13},{... | collective-permute-start | bytes 393224 | tf_op jit(solution)/shard_map/ppermute | solution.py:50
  139.7 2.4 %collective-permute-start.30 = (bf16[128,512]{1,0:T(8,128)(2,1)S(1)}, bf16[128,512]{1,0:T(8,128)(2,1)S(1)}, u32[]{:S(2)}, u32[]{:S(2)}) collective-permute-start(bf16[128,512]{1,0:T(8,128)(2,1)S(1)} %get-tuple-element.150), channel_id=1, source_target_pairs={{0,16},{4,20},{8,24},{12,28},{16,0},{20,4},{24,8},{28,12},{1,17},{... | collective-permute-start | bytes 393224 | tf_op jit(solution)/shard_map/ppermute | solution.py:50
  142.1 3.4 %collective-permute-start.31 = (bf16[128,512]{1,0:T(8,128)(2,1)S(1)}, bf16[128,512]{1,0:T(8,128)(2,1)S(1)}, u32[]{:S(2)}, u32[]{:S(2)}) collective-permute-start(bf16[128,512]{1,0:T(8,128)(2,1)S(1)} %get-tuple-element.151), channel_id=1, source_target_pairs={{0,20},{4,24},{8,28},{12,0},{16,4},{20,8},{24,12},{28,16},{1,21},{... | collective-permute-start | bytes 393224 | tf_op jit(solution)/shard_map/ppermute | solution.py:50
  145.5 11.5 %taps_back.1 = bf16[8,192,128]{2,1,0:T(8,128)(2,1)} custom-call(s32[3]{0:T(128)S(1)} %pad_add_fusion.sc, f32[4,64,128]{2,1,0:T(8,128)S(1)} %get-tuple-element.154.par, f32[8,512]{1,0:T(8,128)S(1)} %get-tuple-element.106.vec, bf16[1024,128]{1,0:T(8,128)(2,1)S(1)} %bitcast.16, bf16[1024,128]{1,0:T(8,128)(2,1)S(1)} %bitcast.17, ...), custom_call_target="tpu_custom_call" | custom-call | bytes 33000000 | tf_op jit(solution)/shard_map/taps_back/pallas_call | solution.py:275
  157.0 5.1 %all-to-all-start.1 = ((bf16[8,192,128]{2,1,0:T(8,128)(2,1)}), bf16[8,192,128]{2,1,0:T(8,128)(2,1)S(1)}, u32[]{:S(2)}, u32[]{:S(2)}) async-start(bf16[8,192,128]{2,1,0:T(8,128)(2,1)} %taps_back.1), calls=%async_computation.1 | async-start | bytes 786432 | tf_op jit(solution)/shard_map/all_to_all | solution.py:990
  162.1 3.8 %collective-permute-start.32 = (bf16[128,512]{1,0:T(8,128)(2,1)S(1)}, bf16[128,512]{1,0:T(8,128)(2,1)S(1)}, u32[]{:S(2)}, u32[]{:S(2)}) collective-permute-start(bf16[128,512]{1,0:T(8,128)(2,1)S(1)} %get-tuple-element.152), channel_id=1, source_target_pairs={{0,24},{4,28},{8,0},{12,4},{16,8},{20,12},{24,16},{28,20},{1,25},{... | collective-permute-start | bytes 393224 | tf_op jit(solution)/shard_map/ppermute | solution.py:50
  167.4 7.8 %all-to-all-done.1.msg = bf16[8,192,128]{2,1,0:T(8,128)(2,1)S(1)} async-done(((bf16[8,192,128]{2,1,0:T(8,128)(2,1)}), bf16[8,192,128]{2,1,0:T(8,128)(2,1)S(1)}, u32[]{:S(2)}, u32[]{:S(2)}) %all-to-all-start.1) | async-done | bytes 393248 | tf_op jit(solution)/shard_map/all_to_all | solution.py:990
  177.8 2.2 %weave.2 = bf16[128,8,512]{2,1,0:T(8,128)(2,1)} custom-call(s32[3]{0:T(128)S(1)} %pad_add_fusion.sc, bf16[128,512]{1,0:T(8,128)(2,1)S(1)} %get-tuple-element.118.refs_0_, bf16[128,512]{1,0:T(8,128)(2,1)S(1)} %collective-permute-done.15.refs_1_, bf16[128,512]{1,0:T(8,128)(2,1)S(1)} %collective-permute-done.16.refs_2_, ...), custom_call_target="tpu_custom_call" | custom-call | bytes 9900000 | tf_op jit(solution)/shard_map/weave/pallas_call | solution.py:809
  180.0 2.2 %weave.3 = bf16[128,8,512]{2,1,0:T(8,128)(2,1)} custom-call(s32[3]{0:T(128)S(1)} %pad_add_fusion.sc, bf16[128,512]{1,0:T(8,128)(2,1)S(1)} %get-tuple-element.146.refs_0_, bf16[128,512]{1,0:T(8,128)(2,1)S(1)} %collective-permute-done.27.refs_1_, bf16[128,512]{1,0:T(8,128)(2,1)S(1)} %collective-permute-done.28.refs_2_, ...), custom_call_target="tpu_custom_call" | custom-call | bytes 9900000 | tf_op jit(solution)/shard_map/weave/pallas_call | solution.py:809
  (88 shorter events, 34.4 us)
Async XLA Ops:
  3.9 31.0 %all-to-all-start = ((bf16[8,240,128]{2,1,0:T(8,128)(2,1)}), bf16[8,240,128]{2,1,0:T(8,128)(2,1)S(1)}, u32[]{:S(2)}, u32[]{:S(2)}) async-start(bf16[8,240,128]{2,1,0:T(8,128)(2,1)} %pack_weights.1), calls=%async_computation | async-start | bytes 983040 | tf_op jit(solution)/shard_map/all_to_all | solution.py:934
  15.6 12.9 %collective-permute-start = (bf16[128,512]{1,0:T(8,128)(2,1)S(1)}, bf16[128,512]{1,0:T(8,128)(2,1)S(1)}, u32[]{:S(2)}, u32[]{:S(2)}) collective-permute-start(bf16[128,512]{1,0:T(8,128)(2,1)S(1)} %get-tuple-element.97), channel_id=1, source_target_pairs={{0,4},{4,8},{8,12},{12,16},{16,20},{20,24},{24,28},{28,0},{1,5},{5... | collective-permute-start | bytes 393224 | tf_op jit(solution)/shard_map/ppermute | solution.py:50
  17.6 25.4 %collective-permute-start.1 = (bf16[128,512]{1,0:T(8,128)(2,1)S(1)}, bf16[128,512]{1,0:T(8,128)(2,1)S(1)}, u32[]{:S(2)}, u32[]{:S(2)}) collective-permute-start(bf16[128,512]{1,0:T(8,128)(2,1)S(1)} %get-tuple-element.101), channel_id=1, source_target_pairs={{0,12},{4,16},{8,20},{12,24},{16,28},{20,0},{24,4},{28,8},{1,13},{... | collective-permute-start | bytes 393224 | tf_op jit(solution)/shard_map/ppermute | solution.py:50
  20.0 23.1 %collective-permute-start.3 = (bf16[128,512]{1,0:T(8,128)(2,1)S(1)}, bf16[128,512]{1,0:T(8,128)(2,1)S(1)}, u32[]{:S(2)}, u32[]{:S(2)}) collective-permute-start(bf16[128,512]{1,0:T(8,128)(2,1)S(1)} %get-tuple-element.104), channel_id=1, source_target_pairs={{0,16},{4,20},{8,24},{12,28},{16,0},{20,4},{24,8},{28,12},{1,17},{... | collective-permute-start | bytes 393224 | tf_op jit(solution)/shard_map/ppermute | solution.py:50
  21.0 25.5 %collective-permute-start.6 = (bf16[128,512]{1,0:T(8,128)(2,1)S(1)}, bf16[128,512]{1,0:T(8,128)(2,1)S(1)}, u32[]{:S(2)}, u32[]{:S(2)}) collective-permute-start(bf16[128,512]{1,0:T(8,128)(2,1)S(1)} %get-tuple-element.110), channel_id=1, source_target_pairs={{0,20},{4,24},{8,28},{12,0},{16,4},{20,8},{24,12},{28,16},{1,21},{... | collective-permute-start | bytes 393224 | tf_op jit(solution)/shard_map/ppermute | solution.py:50
  41.0 15.7 %collective-permute-start.10 = (bf16[1024,128]{1,0:T(8,128)(2,1)S(1)}, bf16[1024,128]{1,0:T(8,128)(2,1)S(1)}, u32[]{:S(2)}, u32[]{:S(2)}) collective-permute-start(bf16[1024,128]{1,0:T(8,128)(2,1)S(1)} %get-tuple-element.116.refs_0_), channel_id=1, source_target_pairs={{0,2},{1,3},{2,0},{3,1},{4,6},{5,7},{6,4},{7,5},{8,10},{9,11},{10,... | collective-permute-start | bytes 786440 | tf_op jit(solution)/shard_map/ppermute | solution.py:55
  42.5 14.7 %collective-permute-start.13 = (bf16[8,128,128]{2,1,0:T(8,128)(2,1)S(1)}, bf16[8,128,128]{2,1,0:T(8,128)(2,1)S(1)}, u32[]{:S(2)}, u32[]{:S(2)}) collective-permute-start(bf16[8,128,128]{2,1,0:T(8,128)(2,1)S(1)} %get-tuple-element.117.refs_4_), channel_id=1, source_target_pairs={{0,2},{1,3},{2,0},{3,1},{4,6},{5,7},{6,4},{7,5},{8,10},{9,11},{10,... | collective-permute-start | bytes 786440 | tf_op jit(solution)/shard_map/ppermute | solution.py:55
  46.4 10.2 %collective-permute-start.5 = (bf16[128,512]{1,0:T(8,128)(2,1)S(1)}, bf16[128,512]{1,0:T(8,128)(2,1)S(1)}, u32[]{:S(2)}, u32[]{:S(2)}) collective-permute-start(bf16[128,512]{1,0:T(8,128)(2,1)S(1)} %get-tuple-element.109), channel_id=1, source_target_pairs={{0,8},{4,12},{8,16},{12,20},{16,24},{20,28},{24,0},{28,4},{1,9},{5... | collective-permute-start | bytes 393224 | tf_op jit(solution)/shard_map/ppermute | solution.py:50
  50.4 14.5 %collective-permute-start.12 = (bf16[8,128,128]{2,1,0:T(8,128)(2,1)S(1)}, bf16[8,128,128]{2,1,0:T(8,128)(2,1)S(1)}, u32[]{:S(2)}, u32[]{:S(2)}) collective-permute-start(bf16[8,128,128]{2,1,0:T(8,128)(2,1)S(1)} %get-tuple-element.117.refs_4_), channel_id=1, source_target_pairs={{0,1},{1,0},{2,3},{3,2},{4,5},{5,4},{6,7},{7,6},{8,9},{9,8},{10,11... | collective-permute-start | bytes 786440 | tf_op jit(solution)/shard_map/ppermute | solution.py:55
  56.7 19.7 %collective-permute-start.11 = (bf16[1024,128]{1,0:T(8,128)(2,1)S(1)}, bf16[1024,128]{1,0:T(8,128)(2,1)S(1)}, u32[]{:S(2)}, u32[]{:S(2)}) collective-permute-start(bf16[1024,128]{1,0:T(8,128)(2,1)S(1)} %collective-permute-done.10.refs_2_), channel_id=1, source_target_pairs={{0,1},{1,0},{2,3},{3,2},{4,5},{5,4},{6,7},{7,6},{8,9},{9,8},{10,11... | collective-permute-start | bytes 786440 | tf_op jit(solution)/shard_map/ppermute | solution.py:55
  57.2 20.0 %collective-permute-start.14 = (bf16[8,128,128]{2,1,0:T(8,128)(2,1)S(1)}, bf16[8,128,128]{2,1,0:T(8,128)(2,1)S(1)}, u32[]{:S(2)}, u32[]{:S(2)}) collective-permute-start(bf16[8,128,128]{2,1,0:T(8,128)(2,1)S(1)} %collective-permute-done.13.refs_6_), channel_id=1, source_target_pairs={{0,1},{1,0},{2,3},{3,2},{4,5},{5,4},{6,7},{7,6},{8,9},{9,8},{10,11... | collective-permute-start | bytes 786440 | tf_op jit(solution)/shard_map/ppermute | solution.py:55
  64.9 23.1 %collective-permute-start.22 = (bf16[128,512]{1,0:T(8,128)(2,1)S(1)}, bf16[128,512]{1,0:T(8,128)(2,1)S(1)}, u32[]{:S(2)}, u32[]{:S(2)}) collective-permute-start(bf16[128,512]{1,0:T(8,128)(2,1)S(1)} %get-tuple-element.133), channel_id=1, source_target_pairs={{0,12},{4,16},{8,20},{12,24},{16,28},{20,0},{24,4},{28,8},{1,13},{... | collective-permute-start | bytes 393224 | tf_op jit(solution)/shard_map/ppermute | solution.py:50
  64.9 24.4 %collective-permute-start.23 = (bf16[128,512]{1,0:T(8,128)(2,1)S(1)}, bf16[128,512]{1,0:T(8,128)(2,1)S(1)}, u32[]{:S(2)}, u32[]{:S(2)}) collective-permute-start(bf16[128,512]{1,0:T(8,128)(2,1)S(1)} %get-tuple-element.135), channel_id=1, source_target_pairs={{0,16},{4,20},{8,24},{12,28},{16,0},{20,4},{24,8},{28,12},{1,17},{... | collective-permute-start | bytes 393224 | tf_op jit(solution)/shard_map/ppermute | solution.py:50
  64.9 25.6 %collective-permute-start.24 = (bf16[128,512]{1,0:T(8,128)(2,1)S(1)}, bf16[128,512]{1,0:T(8,128)(2,1)S(1)}, u32[]{:S(2)}, u32[]{:S(2)}) collective-permute-start(bf16[128,512]{1,0:T(8,128)(2,1)S(1)} %get-tuple-element.137), channel_id=1, source_target_pairs={{0,20},{4,24},{8,28},{12,0},{16,4},{20,8},{24,12},{28,16},{1,21},{... | collective-permute-start | bytes 393224 | tf_op jit(solution)/shard_map/ppermute | solution.py:50
  76.4 16.6 %collective-permute-start.25 = (bf16[128,512]{1,0:T(8,128)(2,1)S(1)}, bf16[128,512]{1,0:T(8,128)(2,1)S(1)}, u32[]{:S(2)}, u32[]{:S(2)}) collective-permute-start(bf16[128,512]{1,0:T(8,128)(2,1)S(1)} %get-tuple-element.139), channel_id=1, source_target_pairs={{0,24},{4,28},{8,0},{12,4},{16,8},{20,12},{24,16},{28,20},{1,25},{... | collective-permute-start | bytes 393224 | tf_op jit(solution)/shard_map/ppermute | solution.py:50
  77.2 15.7 %collective-permute-start.26 = (bf16[128,512]{1,0:T(8,128)(2,1)S(1)}, bf16[128,512]{1,0:T(8,128)(2,1)S(1)}, u32[]{:S(2)}, u32[]{:S(2)}) collective-permute-start(bf16[128,512]{1,0:T(8,128)(2,1)S(1)} %get-tuple-element.141), channel_id=1, source_target_pairs={{0,28},{4,0},{8,4},{12,8},{16,12},{20,16},{24,20},{28,24},{1,29},{... | collective-permute-start | bytes 393224 | tf_op jit(solution)/shard_map/ppermute | solution.py:50
  88.0 13.7 %collective-permute-start.15 = (bf16[128,512]{1,0:T(8,128)(2,1)S(1)}, bf16[128,512]{1,0:T(8,128)(2,1)S(1)}, u32[]{:S(2)}, u32[]{:S(2)}) collective-permute-start(bf16[128,512]{1,0:T(8,128)(2,1)S(1)} %get-tuple-element.119), channel_id=1, source_target_pairs={{0,4},{4,8},{8,12},{12,16},{16,20},{20,24},{24,28},{28,0},{1,5},{5... | collective-permute-start | bytes 393224 | tf_op jit(solution)/shard_map/ppermute | solution.py:50
  89.3 12.4 %collective-permute-start.16 = (bf16[128,512]{1,0:T(8,128)(2,1)S(1)}, bf16[128,512]{1,0:T(8,128)(2,1)S(1)}, u32[]{:S(2)}, u32[]{:S(2)}) collective-permute-start(bf16[128,512]{1,0:T(8,128)(2,1)S(1)} %get-tuple-element.120), channel_id=1, source_target_pairs={{0,8},{4,12},{8,16},{12,20},{16,24},{20,28},{24,0},{28,4},{1,9},{5... | collective-permute-start | bytes 393224 | tf_op jit(solution)/shard_map/ppermute | solution.py:50
  90.6 12.8 %collective-permute-start.17 = (bf16[128,512]{1,0:T(8,128)(2,1)S(1)}, bf16[128,512]{1,0:T(8,128)(2,1)S(1)}, u32[]{:S(2)}, u32[]{:S(2)}) collective-permute-start(bf16[128,512]{1,0:T(8,128)(2,1)S(1)} %get-tuple-element.121), channel_id=1, source_target_pairs={{0,12},{4,16},{8,20},{12,24},{16,28},{20,0},{24,4},{28,8},{1,13},{... | collective-permute-start | bytes 393224 | tf_op jit(solution)/shard_map/ppermute | solution.py:50
  106.0 10.2 %collective-permute-start.18 = (bf16[128,512]{1,0:T(8,128)(2,1)S(1)}, bf16[128,512]{1,0:T(8,128)(2,1)S(1)}, u32[]{:S(2)}, u32[]{:S(2)}) collective-permute-start(bf16[128,512]{1,0:T(8,128)(2,1)S(1)} %get-tuple-element.122), channel_id=1, source_target_pairs={{0,16},{4,20},{8,24},{12,28},{16,0},{20,4},{24,8},{28,12},{1,17},{... | collective-permute-start | bytes 393224 | tf_op jit(solution)/shard_map/ppermute | solution.py:50
  107.9 31.8 %collective-permute-start.35 = (bf16[1,1024,128]{2,1,0:T(8,128)(2,1)S(1)}, bf16[1,1024,128]{2,1,0:T(8,128)(2,1)S(1)}, u32[]{:S(2)}, u32[]{:S(2)}) collective-permute-start(bf16[1,1024,128]{2,1,0:T(8,128)(2,1)S(1)} %get-tuple-element.158), channel_id=1, source_target_pairs={{0,2},{1,3},{2,0},{3,1},{4,6},{5,7},{6,4},{7,5},{8,10},{9,11},{10,... | collective-permute-start | bytes 786440 | tf_op jit(solution)/shard_map/ppermute | solution.py:55
  110.2 31.8 %collective-permute-start.37 = (bf16[1,8,128,128]{3,2,1,0:T(8,128)(2,1)S(1)}, bf16[1,8,128,128]{3,2,1,0:T(8,128)(2,1)S(1)}, u32[]{:S(2)}, u32[]{:S(2)}) collective-permute-start(bf16[1,8,128,128]{3,2,1,0:T(8,128)(2,1)S(1)} %get-tuple-element.165), channel_id=1, source_target_pairs={{0,2},{1,3},{2,0},{3,1},{4,6},{5,7},{6,4},{7,5},{8,10},{9,11},{10,... | collective-permute-start | bytes 786440 | tf_op jit(solution)/shard_map/ppermute | solution.py:55
  112.9 20.7 %collective-permute-start.20 = (bf16[128,512]{1,0:T(8,128)(2,1)S(1)}, bf16[128,512]{1,0:T(8,128)(2,1)S(1)}, u32[]{:S(2)}, u32[]{:S(2)}) collective-permute-start(bf16[128,512]{1,0:T(8,128)(2,1)S(1)} %get-tuple-element.124), channel_id=1, source_target_pairs={{0,24},{4,28},{8,0},{12,4},{16,8},{20,12},{24,16},{28,20},{1,25},{... | collective-permute-start | bytes 393224 | tf_op jit(solution)/shard_map/ppermute | solution.py:50
  116.1 20.7 %collective-permute-start.21 = (bf16[128,512]{1,0:T(8,128)(2,1)S(1)}, bf16[128,512]{1,0:T(8,128)(2,1)S(1)}, u32[]{:S(2)}, u32[]{:S(2)}) collective-permute-start(bf16[128,512]{1,0:T(8,128)(2,1)S(1)} %get-tuple-element.125), channel_id=1, source_target_pairs={{0,28},{4,0},{8,4},{12,8},{16,12},{20,16},{24,20},{28,24},{1,29},{... | collective-permute-start | bytes 393224 | tf_op jit(solution)/shard_map/ppermute | solution.py:50
  130.1 26.9 %collective-permute-start.27 = (bf16[128,512]{1,0:T(8,128)(2,1)S(1)}, bf16[128,512]{1,0:T(8,128)(2,1)S(1)}, u32[]{:S(2)}, u32[]{:S(2)}) collective-permute-start(bf16[128,512]{1,0:T(8,128)(2,1)S(1)} %get-tuple-element.147), channel_id=1, source_target_pairs={{0,4},{4,8},{8,12},{12,16},{16,20},{20,24},{24,28},{28,0},{1,5},{5... | collective-permute-start | bytes 393224 | tf_op jit(solution)/shard_map/ppermute | solution.py:50
  133.5 23.5 %collective-permute-start.28 = (bf16[128,512]{1,0:T(8,128)(2,1)S(1)}, bf16[128,512]{1,0:T(8,128)(2,1)S(1)}, u32[]{:S(2)}, u32[]{:S(2)}) collective-permute-start(bf16[128,512]{1,0:T(8,128)(2,1)S(1)} %get-tuple-element.148), channel_id=1, source_target_pairs={{0,8},{4,12},{8,16},{12,20},{16,24},{20,28},{24,0},{28,4},{1,9},{5... | collective-permute-start | bytes 393224 | tf_op jit(solution)/shard_map/ppermute | solution.py:50
  136.9 20.1 %collective-permute-start.29 = (bf16[128,512]{1,0:T(8,128)(2,1)S(1)}, bf16[128,512]{1,0:T(8,128)(2,1)S(1)}, u32[]{:S(2)}, u32[]{:S(2)}) collective-permute-start(bf16[128,512]{1,0:T(8,128)(2,1)S(1)} %get-tuple-element.149), channel_id=1, source_target_pairs={{0,12},{4,16},{8,20},{12,24},{16,28},{20,0},{24,4},{28,8},{1,13},{... | collective-permute-start | bytes 393224 | tf_op jit(solution)/shard_map/ppermute | solution.py:50
  139.7 17.3 %collective-permute-start.30 = (bf16[128,512]{1,0:T(8,128)(2,1)S(1)}, bf16[128,512]{1,0:T(8,128)(2,1)S(1)}, u32[]{:S(2)}, u32[]{:S(2)}) collective-permute-start(bf16[128,512]{1,0:T(8,128)(2,1)S(1)} %get-tuple-element.150), channel_id=1, source_target_pairs={{0,16},{4,20},{8,24},{12,28},{16,0},{20,4},{24,8},{28,12},{1,17},{... | collective-permute-start | bytes 393224 | tf_op jit(solution)/shard_map/ppermute | solution.py:50
  142.1 14.9 %collective-permute-start.31 = (bf16[128,512]{1,0:T(8,128)(2,1)S(1)}, bf16[128,512]{1,0:T(8,128)(2,1)S(1)}, u32[]{:S(2)}, u32[]{:S(2)}) collective-permute-start(bf16[128,512]{1,0:T(8,128)(2,1)S(1)} %get-tuple-element.151), channel_id=1, source_target_pairs={{0,20},{4,24},{8,28},{12,0},{16,4},{20,8},{24,12},{28,16},{1,21},{... | collective-permute-start | bytes 393224 | tf_op jit(solution)/shard_map/ppermute | solution.py:50
  157.0 18.2 %all-to-all-start.1 = ((bf16[8,192,128]{2,1,0:T(8,128)(2,1)}), bf16[8,192,128]{2,1,0:T(8,128)(2,1)S(1)}, u32[]{:S(2)}, u32[]{:S(2)}) async-start(bf16[8,192,128]{2,1,0:T(8,128)(2,1)} %taps_back.1), calls=%async_computation.1 | async-start | bytes 786432 | tf_op jit(solution)/shard_map/all_to_all | solution.py:990
  162.1 17.9 %collective-permute-start.32 = (bf16[128,512]{1,0:T(8,128)(2,1)S(1)}, bf16[128,512]{1,0:T(8,128)(2,1)S(1)}, u32[]{:S(2)}, u32[]{:S(2)}) collective-permute-start(bf16[128,512]{1,0:T(8,128)(2,1)S(1)} %get-tuple-element.152), channel_id=1, source_target_pairs={{0,24},{4,28},{8,0},{12,4},{16,8},{20,12},{24,16},{28,20},{1,25},{... | collective-permute-start | bytes 393224 | tf_op jit(solution)/shard_map/ppermute | solution.py:50
  165.9 14.1 %collective-permute-start.33 = (bf16[128,512]{1,0:T(8,128)(2,1)S(1)}, bf16[128,512]{1,0:T(8,128)(2,1)S(1)}, u32[]{:S(2)}, u32[]{:S(2)}) collective-permute-start(bf16[128,512]{1,0:T(8,128)(2,1)S(1)} %get-tuple-element.153), channel_id=1, source_target_pairs={{0,28},{4,0},{8,4},{12,8},{16,12},{20,16},{24,20},{28,24},{1,29},{... | collective-permute-start | bytes 393224 | tf_op jit(solution)/shard_map/ppermute | solution.py:50
  (16 other events, 227.6 us)
where the time goes:
time: 188 us; the launch traced here: 186 us
  Pallas kernels  70 us (37%)
  starting transfers between devices  67.4 us (36%)
  waiting for transfers between devices  38.8 us (21%)
  local copies, waits for them, and re-layouts  7.89 us (4%)
    ppermute x28, starting transfers between devices, shift_exchange(): lax.ppermute(pieces[s], axis, [(k, (k + s) % size) for k in range(size)])  48.2 us
    ppermute x28, waiting for transfers between devices, shift_exchange(): lax.ppermute(pieces[s], axis, [(k, (k + s) % size) for k in range(size)])  24.6 us
    pallas_call x1, Pallas kernels, norm_back(): pl.pallas_call(partial(norm_back_kernel, n, blocks, block), out_shape=[ja...  12 us
    pallas_call x1, Pallas kernels, taps_back(): pl.pallas_call(partial(taps_back_kernel, n, states), out_shape=jax.ShapeD...  11.5 us
    pallas_call x1, Pallas kernels, forward(): pl.pallas_call(partial(forward_kernel, n, n_t, blocks, block), out_shape=...  9.99 us
    pallas_call x1, Pallas kernels, mix_back(): pl.pallas_call(partial(mix_back_kernel, n, blocks, block), out_shape=[hal...  8.64 us
    all_to_all x1, waiting for transfers between devices, local(): msg = lax.all_to_all(msg, 'dp', 0, 0, tiled=True)  7.84 us
    pallas_call x1, Pallas kernels, enter(): pl.pallas_call(partial(enter_kernel, n, blocks, block), out_shape=[keep((...  7.58 us
  transfers between devices with their start and end apart: 43, of which 9 were waited for; matrix products, arithmetic and copies ran while one was open for 2% of the time, Pallas kernels for 36%

commit v1 on v0

v1 whole, which is shorter than its diff:
```python
from functools import partial

import jax
import jax.numpy as jnp
import ml_dtypes
import numpy as np
from jax import lax
from jax.experimental import pallas as pl
from jax.experimental.pallas import tpu as pltpu
from jax.sharding import PartitionSpec as P

epsilon = 1e-05
f32 = jnp.float32
bf16 = jnp.bfloat16


def params(mib):
    return pltpu.CompilerParams(vmem_limit_bytes=mib * 1024 * 1024)


def cost(us):
    return pl.CostEstimate(flops=0, bytes_accessed=int(us * 1e4), transcendentals=0)


def keep(shape, dtype):
    return pltpu.VMEM(shape, dtype)


def held_in_vmem(*arrays):
    return [pltpu.with_memory_space_constraint(a, pltpu.VMEM) for a in arrays]


def hbm(shape, dtype):
    return pltpu.HBM(shape, dtype)


def hspec():
    return pl.BlockSpec(memory_space=pltpu.HBM)


def copies(sems, index, block, j, pairs):
    at = pl.ds(pl.multiple_of(j * block, block), block)
    return [
        pltpu.make_async_copy(src.at[at], dst.at[at], sems.at[index + k, j])
        for k, (src, dst) in enumerate(pairs)
    ]


def gather_rows(rank, pieces, whole, sems):
    n = len(pieces)
    if n == 1:
        return [pltpu.make_async_copy(pieces[0], whole, sems.at[0])]
    rows = whole.shape[0] // n
    moves = []
    for s, piece in enumerate(pieces):
        to = pl.ds(pl.multiple_of(lax.rem(rank - s + n, n) * rows, rows), rows)
        moves.append(pltpu.make_async_copy(piece.at[pl.ds(0, rows)], whole.at[to], sems.at[s]))
    return moves


def held_in_hbm(*arrays):
    return [pltpu.with_memory_space_constraint(a, pltpu.HBM) for a in arrays]


def vspec():
    return pl.BlockSpec(memory_space=pltpu.VMEM)


def sspec():
    return pl.BlockSpec(memory_space=pltpu.SMEM)


def basis(block):
    freq = np.concatenate([np.arange(0, block, 2), np.arange(1, block, 2)])
    angle = np.pi * (2 * freq[:, None] + 1) * np.arange(block)[None, :] / (2 * block)
    forward = np.concatenate([np.cos(angle), -np.sin(angle)], axis=0)
    return forward.astype(np.float32)


def two_parts(value):
    high = value.astype(ml_dtypes.bfloat16)
    low = (value - high.astype(np.float32)).astype(ml_dtypes.bfloat16)
    return jnp.asarray(high), jnp.asarray(low)


def shift_exchange(pieces, axis, size):
    out = [pieces[0]]
    for s in range(1, size):
        out.append(lax.ppermute(pieces[s], axis, [(k, (k + s) % size) for k in range(size)]))
    return out


def flip_bit(value, axis, size, bit):
    return lax.ppermute(value, axis, [(k, k ^ bit) for k in range(size)])


WIDE = 128


def pad_to(value, multiple):
    return -(-value // multiple) * multiple


def planes(value):
    parts = []
    for _ in range(3):
        part = value.astype(bf16)
        parts.append(part)
        value = value - part.astype(f32)
    return parts


def split_kernel(rows_f, *refs):
    parts, vecs, w_ref, out, held = refs[:4], refs[4:9], refs[9], refs[10], refs[11]
    states, channels = parts[0].shape
    held[...] = jnp.zeros_like(held)
    for k, ref in enumerate(parts):
        held[k * states : (k + 1) * states, :channels] = ref[...]
    flat = 0
    for ref in vecs:
        row, lane = divmod(flat, WIDE)
        size = ref.shape[1]
        held[4 * states + row : 4 * states + row + 1, lane : lane + size] = ref[...]
        flat += size
    for p, plane in enumerate(planes(held[...])):
        out[0, p * rows_f : (p + 1) * rows_f, :] = plane
    if w_ref.shape[1] < WIDE:
        out[0, 3 * rows_f :, :] = jnp.zeros((w_ref.shape[0], WIDE), bf16)
    out[0, 3 * rows_f :, : w_ref.shape[1]] = w_ref[...]


def float_rows(states, vec_rows):
    return pad_to(4 * states + vec_rows, 8)


def pack(parts, vecs, w):
    vecs = [v.reshape(1, -1) for v in vecs]
    rows_f = float_rows(parts[0].shape[0], -(-sum(v.shape[1] for v in vecs) // WIDE))
    return pl.pallas_call(
        partial(split_kernel, rows_f),
        out_shape=jax.ShapeDtypeStruct((1, 3 * rows_f + w.shape[0], WIDE), bf16),
        in_specs=[vspec()] * 10,
        out_specs=vspec(),
        scratch_shapes=[pltpu.VMEM((rows_f, WIDE), f32)],
        compiler_params=params(4),
        name="pack",
    )(*held_in_hbm(*parts, *vecs, w))


def merge_kernel(which, shift, sc, own, got, out):
    here = (sc[which] >> shift) & 1
    for i in range(own.shape[0]):
        out[2 * i + here] = own[i]
        out[2 * i + 1 - here] = got[i]


def merge(scalars, own, got, which, shift):
    return pl.pallas_call(
        partial(merge_kernel, which, shift),
        out_shape=jax.ShapeDtypeStruct((2 * own.shape[0], *own.shape[1:]), own.dtype),
        in_specs=[sspec(), vspec(), vspec()],
        out_specs=vspec(),
        compiler_params=params(4),
        cost_estimate=cost(1),
        name="merge",
    )(scalars, own, got)


def collect_kernel(blob, out):
    for d in range(out.shape[0]):
        out[d] = blob[d, :, : out.shape[2]]


def collect(blob, channels, cols):
    n, rows, _ = blob.shape
    if (rows - channels) % channels:
        return blob[:, rows - channels :, :cols]
    return pl.pallas_call(
        collect_kernel,
        out_shape=jax.ShapeDtypeStruct((n, channels, cols), bf16),
        grid=(1,),
        in_specs=[pl.BlockSpec((n, channels, WIDE), lambda i: (0, rows // channels - 1, 0))],
        out_specs=pl.BlockSpec((n, channels, cols), lambda i: (0, 0, 0)),
        compiler_params=params(4),
        cost_estimate=cost(1),
        name="collect",
    )(blob)


INNER = 32


def powers(table_r, table_i, zr, zi, count):
    cr, ci = jnp.ones_like(zr), jnp.zeros_like(zi)
    for b in range(count):
        table_r[b] = cr
        table_i[b] = ci
        if b + 1 < count:
            cr, ci = cr * zr - ci * zi, cr * zi + ci * zr


def taps_kernel(n, states, channels, sc, blob, out, par_out, vec_out, b_out, table_r, table_i, part, held):
    rank_t = sc[1]
    per = vec_out.shape[1] // n
    rows_f = float_rows(states, VEC_ROWS(per))
    plane = [blob[:, k * rows_f : (k + 1) * rows_f, :].astype(f32) for k in range(3)]
    held[...] = plane[0] + plane[1] + plane[2]
    for d in range(n):
        for k in range(4):
            par_out[k, d * states : (d + 1) * states, :] = held[d, k * states : (k + 1) * states, :channels]
        top = 4 * states
        for k in range(4):
            row, lane = divmod(k * per, WIDE)
            vec_out[k : k + 1, d * per : (d + 1) * per] = held[d, top + row : top + row + 1, lane : lane + per]
        row, lane = divmod(4 * per, WIDE)
        b_out[:, 2 * d * per : 2 * (d + 1) * per] = held[d, top + row : top + row + 1, lane : lane + 2 * per]
    log_step = vec_out[2:3, 0:channels]
    for t in range(1, vec_out.shape[1] // channels):
        log_step = jnp.where(rank_t == t, vec_out[2:3, t * channels : (t + 1) * channels], log_step)
    vec_out[4:5, 0:channels] = log_step
    step = jnp.exp(log_step)
    decay = jnp.exp(par_out[0]) * step
    turn = par_out[1] * step
    size = jnp.exp(-decay)
    powers(table_r, table_i, size * jnp.cos(turn), size * jnp.sin(turn), INNER)
    far = jnp.exp(-INNER * decay)
    far_r, far_i = far * jnp.cos(INNER * turn), far * jnp.sin(INNER * turn)
    total = decay.shape[0]

    def block(a, carry):
        ar, ai = carry
        for b in range(INNER):
            value = ar * table_r[b] - ai * table_i[b]
            part[b * 8 : (b + 1) * 8, :] = jnp.sum(value.reshape(total // 8, 8, channels), axis=0)
        summed = part[pl.ds(0, INNER, stride=8), :]
        for q in range(1, 8):
            summed = summed + part[pl.ds(q, INNER, stride=8), :]
        out[pl.ds(pl.multiple_of(a * INNER, INNER), INNER), :] = summed.astype(bf16)
        return ar * far_r - ai * far_i, ar * far_i + ai * far_r

    lax.fori_loop(0, out.shape[0] // INNER, block, (par_out[2] * step, par_out[3] * step))


def VEC_ROWS(per):
    return -(-6 * per // WIDE)


def make_taps(scalars, blob, states, length, width, channels):
    n = blob.shape[0]
    total = n * states
    return pl.pallas_call(
        partial(taps_kernel, n, states, channels),
        out_shape=[
            jax.ShapeDtypeStruct((length, channels), bf16),
            jax.ShapeDtypeStruct((4, total, channels), f32),
            jax.ShapeDtypeStruct((8, width), f32),
            jax.ShapeDtypeStruct((1, 2 * width), f32),
        ],
        in_specs=[sspec(), vspec()],
        out_specs=[vspec()] * 4,
        scratch_shapes=[
            pltpu.VMEM((INNER, total, channels), f32),
            pltpu.VMEM((INNER, total, channels), f32),
            pltpu.VMEM((INNER * 8, channels), f32),
            pltpu.VMEM((n, float_rows(states, VEC_ROWS(width // n)), WIDE), f32),
        ],
        compiler_params=params(8),
        cost_estimate=cost(7),
        name="taps",
    )(scalars, blob)


def taps_back_kernel(
    n, states, sc, par, vec, grad_a, grad_b, gain8, bias8, out8, keep_out, send_out, vec_sum, table_r, table_i, summed, held, msg
):
    rank_t = sc[1]
    length, channels = summed.shape
    width = vec.shape[1]
    rate = jnp.exp(par[0])
    step = jnp.exp(vec[4:5, 0:channels])
    decay = rate * step
    turn = par[1] * step
    w_re, w_im = par[2], par[3]
    size = jnp.exp(-decay)
    powers(table_r, table_i, size * jnp.cos(turn), size * jnp.sin(turn), INNER)
    far = jnp.exp(-INNER * decay)
    far_r, far_i = far * jnp.cos(INNER * turn), far * jnp.sin(INNER * turn)
    total = decay.shape[0]
    summed[...] = grad_a[:length, :].astype(f32) + grad_b[:length, :].astype(f32)
    zero = jnp.zeros((total, channels), f32)

    def block(k, carry):
        a = length // INNER - 1 - k
        s0r, s0i, s1r, s1i = [held[q] for q in range(4)]
        s1r, s1i = s1r + INNER * s0r, s1i + INNER * s0i
        s0r, s0i = s0r * far_r - s0i * far_i, s0r * far_i + s0i * far_r
        s1r, s1i = s1r * far_r - s1i * far_i, s1r * far_i + s1i * far_r
        for q, value in enumerate((s0r, s0i, s1r, s1i)):
            held[q] = value
        rows = summed[pl.ds(pl.multiple_of(a * INNER, INNER), INNER), :]
        group = min(32, total)
        for c in range(total // group):
            here = slice(c * group, (c + 1) * group)
            u0r, u0i, u1r, u1i = [held[q, here, :] for q in range(4)]
            tail_r = tail_i = jnp.zeros((group, channels), f32)
            for b in reversed(range(INNER)):
                g = jnp.broadcast_to(rows[b : b + 1, :], (group, channels))
                if b:
                    tail_r, tail_i = tail_r + g * table_r[b, here, :], tail_i + g * table_i[b, here, :]
                    u1r, u1i = u1r + tail_r, u1i + tail_i
                else:
                    tail_r = tail_r + g
            u0r, u0i = u0r + tail_r, u0i + tail_i
            for q, value in enumerate((u0r, u0i, u1r, u1i)):
                held[q, here, :] = value
        return carry

    for q in range(4):
        held[q] = zero
    lax.fori_loop(0, length // INNER, block, 0)
    s0r, s0i, s1r, s1i = [held[q] for q in range(4)]
    wr0 = w_re * s0r - w_im * s0i
    wr1 = w_re * s1r - w_im * s1i
    wi1 = w_re * s1i + w_im * s1r
    dt = jnp.sum(step * (wr0 - decay * wr1 - turn * wi1), axis=0, keepdims=True)
    held[0], held[1] = -step * decay * wr1, -step * step * wi1
    held[2], held[3] = step * s0r, -step * s0i
    rows_w = channels
    lines = width // WIDE
    msg[...] = jnp.zeros_like(msg)
    for d in range(n):
        for k in range(4):
            msg[d, rows_w + k * states : rows_w + (k + 1) * states, :channels] = held[
                k, d * states : (d + 1) * states, :
            ].astype(bf16)
    gain_sum, bias_sum, out_sum = gain8[0:1, :], bias8[0:1, :], out8[0:1, :]
    copies = WIDE // channels
    lane = lax.broadcasted_iota(jnp.int32, (1, WIDE), 1) // channels
    skip_row = jnp.concatenate([summed[0:1, :]] * copies, axis=1) if copies > 1 else summed[0:1, :]
    dt_row = jnp.concatenate([dt] * copies, axis=1) if copies > 1 else dt
    for line in range(lines):
        at = slice(line * WIDE, (line + 1) * WIDE)
        mine = lane + line * copies == rank_t
        rows = [
            gain_sum[:, at],
            bias_sum[:, at],
            jnp.where(mine, dt_row, 0.0),
            jnp.where(mine, skip_row, 0.0),
            out_sum[:, at],
            out_sum[:, width + line * WIDE : width + (line + 1) * WIDE],
        ]
        for k, row in enumerate(rows):
            vec_sum[k * lines + line : k * lines + line + 1, :] = row
    here = sc[0] & 1
    for i in range(n // 2):
        keep_out[i] = msg[2 * i + here]
        send_out[i] = msg[2 * i + 1 - here]


def taps_back(scalars, par, vec, grads, gain8, bias8, out8, length, n, states):
    channels = grads[0].shape[1]
    width = vec.shape[1]
    total = par.shape[1]
    rows = pad_to(channels + 4 * states, 16)
    return pl.pallas_call(
        partial(taps_back_kernel, n, states),
        out_shape=[jax.ShapeDtypeStruct((n // 2, rows, WIDE), bf16)] * 2
        + [jax.ShapeDtypeStruct((6 * (width // WIDE), WIDE), f32)],
        in_specs=[sspec()] + [vspec()] * 7,
        out_specs=[vspec()] * 3,
        scratch_shapes=[
            pltpu.VMEM((INNER, total, channels), f32),
            pltpu.VMEM((INNER, total, channels), f32),
            pltpu.VMEM((length, channels), f32),
            pltpu.VMEM((4, total, channels), f32),
            pltpu.VMEM((n, rows, WIDE), bf16),
        ],
        compiler_params=params(10),
        cost_estimate=cost(10),
        name="taps_back",
    )(scalars, par, vec, *grads, gain8, bias8, out8)


ROWS = 32
TILE = 16
LANES = 128


def chunks(block, width):
    step = min(64, block)
    for r in range(block // step):
        for c in range(width // LANES):
            yield slice(r * step, (r + 1) * step), slice(c * LANES, (c + 1) * LANES)


def row_sums(x):
    ones = jnp.ones((x.shape[1], LANES), bf16)
    return jnp.dot(x, ones, preferred_element_type=f32)


def column_sums(x):
    ones = jnp.ones((8, x.shape[0]), bf16)
    return jnp.dot(ones, x, preferred_element_type=f32)


def shifted(rows, base):
    size = rows.stop - rows.start
    return pl.ds(pl.multiple_of(base + rows.start, size), size)


def tiles(first, last, width, body):
    def step(r, carry):
        row = pl.multiple_of(r * TILE, TILE)
        for c in range(width // LANES):
            body(row, slice(c * LANES, (c + 1) * LANES))
        return carry

    lax.fori_loop(first // TILE, last // TILE, step, 0)


def enter_kernel(n, blocks, block, sc, vec, basis_ref, basis_low, *refs):
    pieces = refs[:n]
    tok_all, sig, xs, sig_out, xhat_out, scale_out = refs[n : n + 6]
    xhat, scale, mean, square, sems, sem_in = refs[n + 6 :]
    length, width = tok_all.shape
    moves = gather_rows(sc[0], pieces, tok_all, sem_in)
    for move in moves:
        move.start()
    for move in moves:
        move.wait()
    saves = [(sig, sig_out), (xhat, xhat_out), (scale, scale_out)]

    def transform(j, carry):
        base = j * block
        at = pl.ds(pl.multiple_of(base, block), block)
        mean[...] = row_sums(tok_all[at, :]) * (1.0 / width)
        for r, c in chunks(block, width):
            centred = tok_all[shifted(r, base), c].astype(f32) - mean[r, :]
            square[r, c] = (centred * centred).astype(bf16)
        scale[at, :] = lax.rsqrt(row_sums(square[...]) * (1.0 / width) + epsilon)
        for r, c in chunks(block, width):
            to = shifted(r, base)
            value = (tok_all[to, c].astype(f32) - mean[r, :]) * scale[to, :]
            xhat[to, c] = value.astype(bf16)
            sig[to, c] = (value * vec[0:1, c] + vec[1:2, c]).astype(bf16)
        for copy in copies(sems, 0, block, j, saves):
            copy.start()
        value = sig[at, :]
        xs[j] = jnp.dot(basis_ref[...], value, preferred_element_type=f32)
        xs[j] += jnp.dot(basis_low[...], value, preferred_element_type=f32)
        return carry

    lax.fori_loop(0, blocks, transform, 0)
    for j in range(blocks):
        for copy in copies(sems, 0, block, j, saves):
            copy.wait()


def enter(scalars, vec, pieces, length, block):
    n = len(pieces)
    width = pieces[0].shape[1]
    blocks = length // block
    return pl.pallas_call(
        partial(enter_kernel, n, blocks, block),
        out_shape=[
            keep((length, width), bf16),
            keep((length, width), bf16),
            keep((blocks, 2 * block, width), f32),
            hbm((length, width), bf16),
            hbm((length, width), bf16),
            hbm((length, LANES), f32),
        ],
        in_specs=[sspec()] + [vspec()] * 3 + [hspec()] * n,
        out_specs=[vspec()] * 3 + [hspec()] * 3,
        scratch_shapes=[
            pltpu.VMEM((length, width), bf16),
            pltpu.VMEM((length, LANES), f32),
            pltpu.VMEM((block, LANES), f32),
            pltpu.VMEM((block, width), bf16),
            pltpu.SemaphoreType.DMA((3, blocks)),
            pltpu.SemaphoreType.DMA((n,)),
        ],
        compiler_params=params(8),
        cost_estimate=cost(7),
        name="enter",
    )(scalars, vec, *two_parts(basis(block)), *pieces)


def forward_kernel(n, n_t, blocks, block, sc, lengths, vec, b_out, basis_ref, basis_low, basis_t, basis_t_low, tok_all, sig, xs, *refs):
    tap_parts, w_parts = refs[:n_t], refs[n_t : 2 * n_t]
    out_h, spec_h, w_h, active_h, slope_h, val_h, gate_h = refs[2 * n_t : 2 * n_t + 7]
    taps, raw, zs, zs_low, mix, pre, spec, w, out, active, slope, val_a, gate, sems, sem_w = refs[2 * n_t + 7 :]
    rank_t = sc[1]
    seq_len = lengths[rank_t * n + sc[0]]
    results = [(out, out_h), (active, active_h), (slope, slope_h), (val_a, val_h), (gate, gate_h)]
    length, width = tok_all.shape
    channels = width // n_t
    half = block // 2
    scale = 1.0 / block
    for e in range(n_t):
        owner = rank_t ^ e
        at = pl.ds(pl.multiple_of(owner * channels, channels), channels)
        if channels % LANES == 0:
            taps[:, at] = tap_parts[e][...]
        else:
            for t in range(n_t):

                @pl.when(owner == t)
                def _(e=e, t=t):
                    taps[:, t * channels : (t + 1) * channels] = tap_parts[e][...]

        count, _, cols = w_parts[e].shape
        for d in range(count):
            w[at, d * cols : (d + 1) * cols] = w_parts[e][d]
    copy_w = pltpu.make_async_copy(w, w_h, sem_w.at[0])
    copy_w.start()

    def spectrum(d, carry):
        at = pl.ds(pl.multiple_of(d * block, block), block)
        value = taps[at, :]
        raw[d] = jnp.dot(basis_ref[...], value, preferred_element_type=f32)
        raw[d] += jnp.dot(basis_low[...], value, preferred_element_type=f32)
        return carry

    lax.fori_loop(0, blocks, spectrum, 0)

    def product(sign, row, lanes):
        re, im = pl.ds(row, TILE), pl.ds(pl.multiple_of(row + block, TILE), TILE)
        xr = [xs[j, re, lanes] for j in range(blocks)]
        xi = [xs[j, im, lanes] for j in range(blocks)]
        kr, ki = [], []
        for d in range(blocks):
            r, i = raw[d, re, lanes], raw[d, im, lanes]
            if d:
                pr, pi = raw[d - 1, re, lanes], raw[d - 1, im, lanes]
                r, i = (r - pi, i + pr) if sign > 0 else (r + pi, i - pr)
            kr.append(r * scale)
            ki.append(i * scale)
            spec[d, re, lanes] = kr[d].astype(bf16)
            spec[d, im, lanes] = ki[d].astype(bf16)
        for m in range(blocks):
            zr = zi = None
            for j in range(m + 1):
                d = m - j
                pr = xr[j] * kr[d] - xi[j] * ki[d]
                pi = xr[j] * ki[d] + xi[j] * kr[d]
                zr = pr if zr is None else zr + pr
                zi = pi if zi is None else zi + pi
            for at, value in ((re, zr), (im, zi)):
                high = value.astype(bf16)
                zs[m, at, lanes] = high
                zs_low[m, at, lanes] = (value - high.astype(f32)).astype(bf16)

    tiles(0, half, width, partial(product, 1))
    tiles(half, block, width, partial(product, -1))
    copy_spec = pltpu.make_async_copy(spec, spec_h, sem_w.at[1])
    copy_spec.start()

    def tail(j, carry):
        mix[...] = jnp.dot(basis_t[...], zs[j], preferred_element_type=f32)
        mix[...] += jnp.dot(basis_t_low[...], zs[j], preferred_element_type=f32)
        mix[...] += jnp.dot(basis_t[...], zs_low[j], preferred_element_type=f32)

        base = j * block
        for r, c in chunks(block, width):
            to = shifted(r, base)
            v = mix[r, c] + vec[3:4, c] * sig[to, c].astype(f32)
            sq = v * v
            t = jnp.tanh(v * (0.7978845608 + (0.7978845608 * 0.044715) * sq))
            half_t = 0.5 + 0.5 * t
            active[to, c] = (v * half_t).astype(bf16)
            inner = 0.7978845608 * 0.5 + (0.7978845608 * 1.5 * 0.044715) * sq
            slope[to, c] = (half_t + v * (1.0 - t * t) * inner).astype(bf16)
        whole = pl.ds(pl.multiple_of(base, block), block)
        pre[...] = jnp.dot(active[whole, :], w[...], preferred_element_type=f32)
        for r, c in chunks(block, width):
            to = shifted(r, base)
            far = slice(width + c.start, width + c.stop)
            a = pre[r, c] + b_out[:, c]
            t = 0.5 * jnp.tanh(0.5 * (pre[r, far] + b_out[:, far]))
            g = 0.5 + t
            place = base + r.start + lax.broadcasted_iota(jnp.int32, a.shape, 0)
            add = jnp.where(place < seq_len, a * g, 0.0)
            out[to, c] = (tok_all[to, c].astype(f32) + add).astype(bf16)
            val_a[to, c] = (a * (0.5 - t)).astype(bf16)
            gate[to, c] = g.astype(bf16)
        for c in copies(sems, 0, block, j, results):
            c.start()
        return carry

    lax.fori_loop(0, blocks, tail, 0)
    copy_w.wait()
    copy_spec.wait()
    for j in range(blocks):
        for c in copies(sems, 0, block, j, results):
            c.wait()


def forward(scalars, lengths, vec, b_out, entered, tap_parts, w_parts, n, block):
    tok_all, sig, xs = entered
    n_t = len(tap_parts)
    length, width = tok_all.shape
    blocks = length // block
    table = basis(block)
    full = hbm((length, width), bf16)
    buffer = pltpu.VMEM((length, width), bf16)
    return pl.pallas_call(
        partial(forward_kernel, n, n_t, blocks, block),
        out_shape=[
            full,
            hbm((blocks, 2 * block, width), bf16),
            hbm((width, 2 * width), bf16),
            full,
            full,
            full,
            full,
        ],
        in_specs=[sspec()] * 2 + [vspec()] * (9 + 2 * n_t),
        out_specs=[hspec()] * 7,
        scratch_shapes=[
            buffer,
            pltpu.VMEM((blocks, 2 * block, width), f32),
            pltpu.VMEM((blocks, 2 * block, width), bf16),
            pltpu.VMEM((blocks, 2 * block, width), bf16),
            pltpu.VMEM((block, width), f32),
            pltpu.VMEM((block, 2 * width), f32),
            pltpu.VMEM((blocks, 2 * block, width), bf16),
            pltpu.VMEM((width, 2 * width), bf16),
            buffer,
            buffer,
            buffer,
            buffer,
            buffer,
            pltpu.SemaphoreType.DMA((5, blocks)),
            pltpu.SemaphoreType.DMA((2,)),
        ],
        compiler_params=params(24),
        cost_estimate=cost(15),
        name="forward",
    )(
        scalars,
        lengths,
        vec,
        b_out,
        *two_parts(table),
        *two_parts(table.T),
        *held_in_vmem(tok_all, sig, xs),
        *tap_parts,
        *w_parts,
    )


def mix_back_kernel(n, n_t, blocks, block, sc, lengths, basis_ref, basis_t, w_h, *refs):
    inputs, pieces = refs[:4], refs[4:5]
    kept, sent, grad_pre, grad_mix, spec_g, bias_grad = refs[5:11]
    val_a, gate, slope, sig, w, cot, xs, act_f, comb, sems, sem_w, sem_in = refs[11:]
    loads = list(zip(inputs, (val_a, gate, slope, sig)))
    seq_len, core = lengths[sc[1] * n + sc[0]], sc[1] & 1
    moves = gather_rows(sc[0], pieces, cot, sem_in)
    for move in moves:
        move.start()
    for c in copies(sems, 0, block, 0, loads):
        c.start()
    copy_w = pltpu.make_async_copy(w_h, w, sem_w.at[0])
    copy_w.start()
    for j in range(1, blocks):
        for c in copies(sems, 0, block, j, loads):
            c.start()
    for move in moves:
        move.wait()
    length, width = cot.shape
    half = block // 2
    bias_grad[...] = jnp.zeros_like(bias_grad)

    def front(j, carry):
        for c in copies(sems, 0, block, j, loads):
            c.wait()

        base = j * block
        for r, c in chunks(block, width):
            to = shifted(r, base)
            far = slice(width + c.start, width + c.stop)
            q = cot[to, c].astype(f32)
            place = base + r.start + lax.broadcasted_iota(jnp.int32, q.shape, 0)
            g = gate[to, c].astype(f32)
            qg = jnp.where(place < seq_len, q * g, 0.0)
            grad_pre[to, c] = qg.astype(bf16)
            grad_pre[to, far] = (qg * val_a[to, c].astype(f32)).astype(bf16)

        @pl.when(j == 0)
        def _():
            copy_w.wait()

        whole = pl.ds(pl.multiple_of(base, block), block)
        bias_grad[...] += column_sums(grad_pre[whole, :])
        xs[j] = jnp.dot(basis_ref[...], sig[whole, :], preferred_element_type=f32)
        act_f[...] = lax.dot_general(
            grad_pre[whole, :], w[...], (((1,), (1,)), ((), ())), preferred_element_type=f32
        )

        for r, c in chunks(block, width):
            to = shifted(r, base)
            grad = act_f[r, c].astype(bf16).astype(f32) * slope[to, c].astype(f32)
            grad_mix[to, c] = grad.astype(bf16)
        spec_g[j] = jnp.dot(basis_ref[...], grad_mix[whole, :], preferred_element_type=f32)
        return carry

    lax.fori_loop(0, blocks, front, 0)

    def correlate(sign, row, lanes):
        re, im = pl.ds(row, TILE), pl.ds(pl.multiple_of(row + block, TILE), TILE)
        xr = [xs[j, re, lanes] for j in range(blocks)]
        xi = [xs[j, im, lanes] for j in range(blocks)]
        gr = [spec_g[j, re, lanes] for j in range(blocks)]
        gi = [spec_g[j, im, lanes] for j in range(blocks)]
        next_r = next_i = None
        for d in reversed(range(blocks)):
            dr = di = None
            for m in range(d, blocks):
                j = m - d
                pr = xr[j] * gr[m] + xi[j] * gi[m]
                pi = xr[j] * gi[m] - xi[j] * gr[m]
                dr = pr if dr is None else dr + pr
                di = pi if di is None else di + pi
            cr, ci = dr, di
            if next_r is not None:
                cr = dr + next_i if sign > 0 else dr - next_i
                ci = di - next_r if sign > 0 else di + next_r
            comb[d, re, lanes] = cr.astype(bf16)
            comb[d, im, lanes] = ci.astype(bf16)
            next_r, next_i = dr, di

    tiles(0, half, width, partial(correlate, 1))
    tiles(half, block, width, partial(correlate, -1))
    channels = width // n_t

    def store(t, to, value):
        @pl.when(core == t & 1)
        def _():
            kept[t >> 1, to, : value.shape[1]] = value

        @pl.when(core != t & 1)
        def _():
            sent[t >> 1, to, : value.shape[1]] = value

    def finish(d, carry):
        act_f[...] = jnp.dot(basis_t[...], comb[d], preferred_element_type=f32)
        to = pl.ds(pl.multiple_of(d * block, block), block)
        for t in range(n_t):
            part = act_f[:, t * channels : (t + 1) * channels] * (1.0 / block)
            store(t, to, part.astype(bf16))
        return carry

    lax.fori_loop(0, blocks, finish, 0)

def mix_back(scalars, lengths, w, saved, cot, block, n, n_t):
    length, width = saved[0].shape
    blocks = length // block
    channels = width // n_t
    table = basis(block)
    halves = jax.ShapeDtypeStruct((n_t // 2, length, channels), bf16)
    buffer = pltpu.VMEM((length, width), bf16)
    return pl.pallas_call(
        partial(mix_back_kernel, n, n_t, blocks, block),
        out_shape=[
            halves,
            halves,
            keep((length, 2 * width), bf16),
            keep((length, width), bf16),
            keep((blocks, 2 * block, width), f32),
            jax.ShapeDtypeStruct((8, 2 * width), f32),
        ],
        in_specs=[sspec()] * 2 + [vspec()] * 2 + [hspec()] * 6,
        out_specs=[vspec()] * 6,
        scratch_shapes=[
            buffer,
            buffer,
            buffer,
            buffer,
            pltpu.VMEM((width, 2 * width), bf16),
            buffer,
            pltpu.VMEM((blocks, 2 * block, width), f32),
            pltpu.VMEM((block, width), f32),
            pltpu.VMEM((blocks, 2 * block, width), bf16),
            pltpu.SemaphoreType.DMA((4, blocks)),
            pltpu.SemaphoreType.DMA((1,)),
            pltpu.SemaphoreType.DMA((1,)),
        ],
        compiler_params=params(20),
        cost_estimate=cost(12),
        name="mix_back",
    )(
        scalars,
        lengths,
        jnp.asarray(table, bf16),
        jnp.asarray(table.T, bf16),
        *held_in_hbm(w, *saved, cot),
    )


def weight_back_kernel(n, sc, active, grad_pre, w_keep, w_send):
    core = sc[1] & 1
    groups, _, channels, cols = w_keep.shape
    for t in range(2 * groups):
        value = lax.dot_general(
            active[:, t * channels : (t + 1) * channels],
            grad_pre[...],
            (((0,), (0,)), ((), ())),
            preferred_element_type=f32,
        ).astype(bf16)

        @pl.when(core == t & 1)
        def _(t=t, value=value):
            for d in range(n):
                w_keep[t >> 1, d] = value[:, d * cols : (d + 1) * cols]

        @pl.when(core != t & 1)
        def _(t=t, value=value):
            for d in range(n):
                w_send[t >> 1, d] = value[:, d * cols : (d + 1) * cols]


def weight_back(scalars, active, grad_pre, n, n_t):
    width = active.shape[1]
    halves = jax.ShapeDtypeStruct((n_t // 2, n, width // n_t, 2 * width // n), bf16)
    return pl.pallas_call(
        partial(weight_back_kernel, n),
        out_shape=[halves, halves],
        in_specs=[sspec()] + [vspec()] * 2,
        out_specs=[vspec()] * 2,
        compiler_params=params(8),
        cost_estimate=cost(3),
        name="weight_back",
    )(scalars, active, *held_in_vmem(grad_pre))


def join_kernel(sc, part_keep, part_send, w_a, w_b, keep_out, send_out):
    here = sc[0] & 1
    _, channels, cols = w_a.shape
    for i in range(keep_out.shape[0]):
        for ref, part, k in ((keep_out, part_keep, here), (send_out, part_send, 1 - here)):
            ref[i] = part[i]
            value = w_a[2 * i + k].astype(f32) + w_b[2 * i + k].astype(f32)
            ref[i, 0:channels, :cols] = value.astype(bf16)


def join(scalars, kept, sent, w_a, w_b):
    shape = jax.ShapeDtypeStruct(kept.shape, bf16)
    return pl.pallas_call(
        join_kernel,
        out_shape=[shape, shape],
        in_specs=[sspec()] + [vspec()] * 4,
        out_specs=[vspec()] * 2,
        compiler_params=params(6),
        cost_estimate=cost(1),
        name="join",
    )(scalars, kept, sent, w_a, w_b)


def norm_back_kernel(blocks, block, sc, vec, basis_t, spec_g, grad_mix, spec_h, xhat_h, scale_h, *refs):
    pieces, (res_h, gain_grad, bias_grad) = refs[:1], refs[1:4]
    comb, sig_f, res, spec, xhat, scale, cot_all, grad, cross, mean_g, mean_c, gain_all, sems, sem_w, sem_in = refs[4:]
    loads = [(xhat_h, xhat), (scale_h, scale)]
    copy_spec = pltpu.make_async_copy(spec_h, spec, sem_w.at[0])
    copy_spec.start()
    for j in range(blocks):
        for c in copies(sems, 0, block, j, loads):
            c.start()
    moves = gather_rows(sc[0], pieces, cot_all, sem_in)
    for move in moves:
        move.start()
    copy_spec.wait()
    for move in moves:
        move.wait()
    length, width = xhat.shape
    for k in range(width // LANES):
        gain_all[k * LANES : (k + 1) * LANES, :] = jnp.broadcast_to(
            vec[0:1, k * LANES : (k + 1) * LANES], (LANES, LANES)
        ).T.astype(bf16)
    gain_grad[...] = jnp.zeros_like(gain_grad)
    bias_grad[...] = jnp.zeros_like(bias_grad)

    def correlate(row, lanes):
        re, im = pl.ds(row, TILE), pl.ds(pl.multiple_of(row + block, TILE), TILE)
        kr = [spec[j, re, lanes].astype(f32) for j in range(blocks)]
        ki = [spec[j, im, lanes].astype(f32) for j in range(blocks)]
        gr = [spec_g[j, re, lanes] for j in range(blocks)]
        gi = [spec_g[j, im, lanes] for j in range(blocks)]
        for j in range(blocks):
            dr = di = None
            for m in range(j, blocks):
                d = m - j
                pr = kr[d] * gr[m] + ki[d] * gi[m]
                pi = kr[d] * gi[m] - ki[d] * gr[m]
                dr = pr if dr is None else dr + pr
                di = pi if di is None else di + pi
            comb[j, re, lanes] = dr.astype(bf16)
            comb[j, im, lanes] = di.astype(bf16)

    tiles(0, block, width, correlate)

    def finish(j, carry):
        for c in copies(sems, 0, block, j, loads):
            c.wait()
        sig_f[...] = jnp.dot(basis_t[...], comb[j], preferred_element_type=f32)

        base = j * block
        for r, c in chunks(block, width):
            to = shifted(r, base)
            value = sig_f[r, c] + vec[3:4, c] * grad_mix[to, c].astype(f32)
            value = value.astype(bf16)
            grad[r, c] = value
            cross[r, c] = (value.astype(f32) * xhat[to, c].astype(f32)).astype(bf16)
        gain_grad[...] += column_sums(cross[...])
        bias_grad[...] += column_sums(grad[...])
        weights = gain_all[...]
        mean_g[...] = jnp.dot(grad[...], weights, preferred_element_type=f32) * (1.0 / width)
        mean_c[...] = jnp.dot(cross[...], weights, preferred_element_type=f32) * (1.0 / width)
        for r, c in chunks(block, width):
            to = shifted(r, base)
            g = grad[r, c].astype(f32) * vec[0:1, c]
            g = g - mean_g[r, :] - xhat[to, c].astype(f32) * mean_c[r, :]
            res[to, c] = (cot_all[to, c].astype(f32) + g * scale[to, :]).astype(bf16)
        for copy in copies(sems, 2, block, j, [(res, res_h)]):
            copy.start()
        return carry

    lax.fori_loop(0, blocks, finish, 0)
    for j in range(blocks):
        for copy in copies(sems, 2, block, j, [(res, res_h)]):
            copy.wait()


def norm_back(scalars, vec, spec, spec_g, grad_mix, xhat, scale, cot, block):
    length, width = xhat.shape
    blocks = length // block
    buffer = pltpu.VMEM((length, width), bf16)
    return pl.pallas_call(
        partial(norm_back_kernel, blocks, block),
        out_shape=[hbm((length, width), bf16)] + [jax.ShapeDtypeStruct((8, width), f32)] * 2,
        in_specs=[sspec()] + [vspec()] * 4 + [hspec()] * 4,
        out_specs=[hspec()] + [vspec()] * 2,
        scratch_shapes=[
            pltpu.VMEM((blocks, 2 * block, width), bf16),
            pltpu.VMEM((block, width), f32),
            buffer,
            pltpu.VMEM((blocks, 2 * block, width), bf16),
            buffer,
            pltpu.VMEM((length, LANES), f32),
            buffer,
            pltpu.VMEM((block, width), bf16),
            pltpu.VMEM((block, width), bf16),
            pltpu.VMEM((block, LANES), f32),
            pltpu.VMEM((block, LANES), f32),
            pltpu.VMEM((width, LANES), bf16),
            pltpu.SemaphoreType.DMA((3, blocks)),
            pltpu.SemaphoreType.DMA((1,)),
            pltpu.SemaphoreType.DMA((1,)),
        ],
        compiler_params=params(14),
        cost_estimate=cost(10),
        name="norm_back",
    )(
        scalars,
        vec,
        jnp.asarray(basis(block).T, bf16),
        *held_in_vmem(spec_g, grad_mix),
        *held_in_hbm(spec, xhat, scale, cot),
    )


def halve_kernel(which, shift, sc, kept, got, keep_out, send_out):
    here = (sc[which] >> shift) & 1
    for i in range(keep_out.shape[0]):
        for k in range(2):
            value = (kept[2 * i + k].astype(f32) + got[2 * i + k].astype(f32)).astype(bf16)

            @pl.when(here == k)
            def _(i=i, value=value):
                keep_out[i] = value

            @pl.when(here != k)
            def _(i=i, value=value):
                send_out[i] = value


def deal_kernel(shift, place, vectors, sc, kept, got, *refs):
    vecs, outs = refs[:vectors], refs[vectors:]
    here = sc[0] >> shift
    vec = vecs[0][...]
    for ref in vecs[1:]:
        vec = vec + ref[...]
    for e, out in enumerate(outs):
        out[: kept.shape[1], :] = (kept[here ^ e].astype(f32) + got[here ^ e].astype(f32)).astype(bf16)
        out[place : place + vec.shape[0], :] = vec.astype(bf16)


def deal(scalars, kept, got, vecs, shift, place):
    rows = pad_to(place + vecs[0].shape[0], 16)
    shape = jax.ShapeDtypeStruct((rows, kept.shape[2]), bf16)
    return pl.pallas_call(
        partial(deal_kernel, shift, place, len(vecs)),
        out_shape=[shape] * kept.shape[0],
        in_specs=[sspec()] + [vspec()] * (2 + len(vecs)),
        out_specs=[vspec()] * kept.shape[0],
        compiler_params=params(5),
        cost_estimate=cost(1),
        name="deal",
    )(scalars, kept, got, *vecs)


def halve(scalars, kept, got, which, shift):
    shape = jax.ShapeDtypeStruct((kept.shape[0] // 2, *kept.shape[1:]), bf16)
    return pl.pallas_call(
        partial(halve_kernel, which, shift),
        out_shape=[shape, shape],
        in_specs=[sspec(), vspec(), vspec()],
        out_specs=[vspec()] * 2,
        compiler_params=params(5),
        cost_estimate=cost(1),
        name="halve",
    )(scalars, kept, got)


def weave_kernel(n, whole, sc, *refs):
    if whole:
        pieces, out, held = [refs[0].at[s] for s in range(n)], refs[1], refs[2]
    else:
        pieces, out, held = refs[:n], refs[n], refs[n + 1]
    rank = sc[0]
    rows, width = pieces[0].shape
    step = min(rows, 32)

    def part(r, carry):
        at = pl.ds(pl.multiple_of(r * step, step), step)
        for s in range(n):
            src = s if whole else lax.rem(rank - s + n, n)
            for c in range(width // LANES):
                lanes = slice(c * LANES, (c + 1) * LANES)
                held[c, pl.ds(src, step, stride=n), :] = pieces[s][at, lanes].astype(f32)
        for c in range(width // LANES):
            lanes = slice(c * LANES, (c + 1) * LANES)
            out[at, :, lanes] = held[c].reshape(step, n, LANES).astype(bf16)
        return carry

    lax.fori_loop(0, rows // step, part, 0)


def weave(scalars, pieces):
    whole = not isinstance(pieces, list)
    n = pieces.shape[0] if whole else len(pieces)
    rows, width = pieces[0].shape
    args = [pieces] if whole else pieces
    return pl.pallas_call(
        partial(weave_kernel, n, whole),
        out_shape=jax.ShapeDtypeStruct((rows, n, width), bf16),
        in_specs=[sspec()] + [vspec()] * len(args),
        out_specs=vspec(),
        scratch_shapes=[pltpu.VMEM((width // LANES, min(rows, 32) * n, LANES), f32)],
        compiler_params=params(8),
        cost_estimate=cost(3),
        name="weave",
    )(scalars, *args)


def part_kernel(n, ordered, sc, whole, *refs):
    if ordered:
        outs, held = [refs[0].at[s] for s in range(n)], refs[1]
    else:
        outs, held = refs[-n - 1 : -1], refs[-1]
    rank = sc[0]
    rows, _, width = whole.shape
    step = min(rows, 32)

    def part(r, carry):
        at = pl.ds(pl.multiple_of(r * step, step), step)
        for c in range(width // LANES):
            lanes = slice(c * LANES, (c + 1) * LANES)
            held[c] = whole[at, :, lanes].astype(f32).reshape(step * n, LANES)
        for s in range(n):
            dst = s if ordered else lax.rem(rank + s, n)
            for c in range(width // LANES):
                lanes = slice(c * LANES, (c + 1) * LANES)
                outs[s][at, lanes] = held[c, pl.ds(dst, step, stride=n), :].astype(bf16)
        return carry

    lax.fori_loop(0, rows // step, part, 0)
    if not ordered and len(refs) > n + 1:
        for s in range(n):
            outs[s][rows:, :] = refs[0][...]


def part(scalars, whole, *extra, ordered=False):
    rows, n, width = whole.shape
    more = extra[0].shape[0] if extra else 0
    if ordered:
        shapes = [jax.ShapeDtypeStruct((n, rows, width), bf16)]
    else:
        shapes = [jax.ShapeDtypeStruct((rows + more, width), bf16)] * n
    return pl.pallas_call(
        partial(part_kernel, n, ordered),
        out_shape=shapes,
        in_specs=[sspec(), vspec()] + [vspec()] * len(extra),
        out_specs=[vspec()] * len(shapes),
        scratch_shapes=[pltpu.VMEM((width // LANES, min(rows, 32) * n, LANES), f32)],
        compiler_params=params(8),
        cost_estimate=cost(3),
        name="part",
    )(scalars, *held_in_hbm(whole, *extra))


def total_kernel(states, lines, count, sc, *refs):
    w_out, *grads = refs[count : count + 5]
    outs = refs[count + 5 :]
    channels, cols = w_out.shape
    rank = sc[0]
    total = refs[0][...].astype(f32)
    for ref in refs[1:count]:
        total = total + ref[...].astype(f32)
    w_out[...] = total[:channels, :cols]
    for k, ref in enumerate(grads):
        ref[...] = total[channels + k * states : channels + (k + 1) * states, :channels]
    top = channels + 4 * states
    for k, out in enumerate(outs):
        per = out.shape[1]
        slots = (2 * lines if k == 4 else lines) * WIDE // per
        value = jnp.zeros((1, per), f32)
        for slot in range(slots):
            line, lane = divmod(slot * per, WIDE)
            row = top + k * lines + line
            value = jnp.where(rank == slot, total[row : row + 1, lane : lane + per], value)
        out[...] = value


def totals(scalars, terms, channels, cols, states, per, lines):
    grad = jax.ShapeDtypeStruct((states, channels), f32)
    one = jax.ShapeDtypeStruct((1, per), f32)
    return pl.pallas_call(
        partial(total_kernel, states, lines, len(terms)),
        out_shape=[jax.ShapeDtypeStruct((channels, cols), f32)]
        + [grad] * 4
        + [one] * 4
        + [jax.ShapeDtypeStruct((1, 2 * per), f32)],
        in_specs=[sspec()] + [vspec()] * len(terms),
        out_specs=[vspec()] * 10,
        compiler_params=params(4),
        cost_estimate=cost(1),
        name="totals",
    )(scalars, *terms)


def local(n_dp, n_t, tokens, cotangent, lengths, ln_gain, ln_bias, lam_log, lam_im, w_re, w_im, log_dt, skip_gain, w_out, b_out):
    rows, seqs, width = tokens.shape
    assert seqs == n_dp
    length = rows * n_dp
    block = min(256, length)
    rank = lax.axis_index("dp")
    rank_t = lax.axis_index("tensor")
    channels, states = lam_log.shape
    cols = w_out.shape[1]
    per = width // n_dp
    bits = [1 << k for k in range(n_t.bit_length() - 1)]
    scalars = jnp.stack([rank, rank_t]).astype(jnp.int32)

    after = lambda value, *others: lax.optimization_barrier((value, others))[0]
    pieces = list(part(scalars, tokens))
    vecs = [after(ln_gain, pieces), ln_bias, log_dt, skip_gain, b_out]
    blob = pack([lam_log.T, lam_im.T, w_re.T, w_im.T], vecs, w_out)
    tok_pieces = dict(enumerate(pieces[:1]))
    waits, needs = {0: [], 1: [1], 2: [2, 3, 4, 5, 6]}, {5: 0, 6: 1, 7: 1}
    merges = {-1: ()}
    steps = n_dp.bit_length() - 1

    def send(s):
        if s not in tok_pieces and s < n_dp:
            piece = after(pieces[s], merges[min(needs.get(s, -1), steps - 1)])
            pairs = [(k, (k + s) % n_dp) for k in range(n_dp)]
            tok_pieces[s] = lax.ppermute(piece, "dp", pairs)
        return tok_pieces.get(s, ())

    for k in range(steps):
        got = flip_bit(blob, "dp", n_dp, n_dp >> (k + 1))
        before = [send(s) for s in waits.get(k, [])]
        blob = merge(scalars, after(blob, before), got, 0, steps - 1 - k)
        merges[k] = blob
    tok_pieces = [send(s) for s in range(n_dp)]
    w_own = collect(blob, channels, cols)
    taps, par_all, vec, b_full = make_taps(
        scalars, after(blob, w_own), states, length, width, channels
    )
    cot = after(part(scalars, cotangent, ordered=True)[0], blob, tok_pieces)
    cot = lax.all_to_all(cot, "dp", 0, 0, tiled=True).reshape(length, width)
    tok_all, sig, xs, sig_keep, xhat, scale = enter(scalars, vec, tok_pieces, length, block)

    def spread(own):
        parts = {0: own}
        for bit in reversed(bits):
            for e in list(parts):
                value = after(parts[e], sig) if bit == 1 else parts[e]
                parts[e | bit] = flip_bit(value, "tensor", n_t, bit)
        return [parts[e] for e in range(n_t)]

    tap_parts = spread(taps)
    w_parts = spread(w_own)

    out_t, spec, w_full, *saved = forward(
        scalars, lengths, vec, b_full, (tok_all, sig, xs), tap_parts, w_parts, n_dp, block
    )
    active, slope, val_a, gate = saved
    out_back = lax.all_to_all(out_t.reshape(n_dp, rows, width), "dp", 0, 0, tiled=True)
    saved = [val_a, gate, slope, sig_keep]
    kept, sent, grad_pre, grad_mix, spec_g, out8 = mix_back(
        scalars, lengths, w_full, saved, cot, block, n_dp, n_t
    )

    def reduce_groups(kept, sent, axis, size, which, hook=lambda value: value):
        got = hook(flip_bit(sent, axis, size, 1))
        for shift in range(1, size.bit_length() - 1):
            kept, sent = halve(scalars, kept, got, which, shift)
            got = flip_bit(sent, axis, size, 1 << shift)
        return kept[0], got[0], sent

    w_keep, w_send = weight_back(scalars, active, grad_pre, n_dp, n_t)
    *grads, sent = reduce_groups(
        kept, sent, "tensor", n_t, 1, lambda got: after(got, w_keep)
    )
    spec_g = after(spec_g, sent)
    grad_rows, gain8, bias8 = norm_back(
        scalars, vec, spec, spec_g, grad_mix, xhat, scale, cot, block
    )
    *w_two, w_sent = reduce_groups(w_keep, w_send, "tensor", n_t, 1)
    grad_rows = after(grad_rows, out_back, grads, w_sent)
    grad_back = lax.all_to_all(grad_rows.reshape(n_dp, rows, width), "dp", 0, 0, tiled=True)
    kept, sent, vec_sum = taps_back(
        scalars, par_all, vec, grads, gain8, bias8, out8, length, n_dp, states
    )
    out = weave(scalars, after(out_back, kept))
    kept, sent = join(scalars, kept, sent, *w_two)
    others = [
        lax.ppermute(vec_sum, "tensor", [(k, k ^ e) for k in range(n_t)]) for e in range(1, n_t)
    ]
    vec_sum = sum(others, vec_sum)
    got = flip_bit(sent, "dp", n_dp, 1)
    got_vec = flip_bit(vec_sum, "dp", n_dp, 1)
    shift = 1
    while kept.shape[0] > 4:
        kept, sent = halve(scalars, after(kept, out), got, 0, shift)
        got = flip_bit(sent, "dp", n_dp, 1 << shift)
        vec_sum = vec_sum + got_vec
        got_vec = flip_bit(vec_sum, "dp", n_dp, 1 << shift)
        shift += 1
    vecs = [vec_sum, got_vec]
    terms = deal(scalars, after(kept, out), got, vecs, shift, channels + 4 * states)
    terms = list(terms[:1]) + [
        flip_bit(terms[e], "dp", n_dp, e << shift) for e in range(1, len(terms))
    ]
    grad_tokens = weave(scalars, after(grad_back, terms[0]))
    terms[0] = after(terms[0], grad_tokens)
    grad_w_out, *grads = totals(scalars, terms, channels, cols, states, per, width // WIDE)
    g_lam_log, g_lam_im, g_w_re, g_w_im = (g.T for g in grads[:4])
    g_gain, g_bias, g_dt, g_skip, g_b = (v.reshape(-1) for v in grads[4:])

    return (
        out,
        grad_tokens,
        g_gain,
        g_bias,
        g_lam_log,
        g_lam_im,
        g_w_re,
        g_w_im,
        g_dt,
        g_skip,
        grad_w_out,
        g_b,
    )


def solution(mesh):
    big = P("dp", "tensor", None)
    grid = P("tensor", "dp")
    line = P("dp")
    return jax.shard_map(
        partial(local, mesh.shape["dp"], mesh.shape["tensor"]),
        mesh=mesh,
        in_specs=(big, big, P(), line, line, grid, grid, grid, grid, line, line, grid, line),
        out_specs=(big, big, line, line, grid, grid, grid, grid, line, line, grid, line),
        check_vma=False,
    )
```

time: 188 us -> 145 us (0.77)
  waiting for transfers between devices: 38.8 us -> 18.7 us
  starting transfers between devices: 67.4 us -> 53.3 us
  local copies, waits for them, and re-layouts: 7.89 us -> 0.6 us
    ppermute x28 -> x7, starting transfers between devices: 48.2 us -> 12.6 us  [send(): tok_pieces[s] = lax.ppermute(piece, 'dp', pairs)]
    ppermute x28 -> x7, waiting for transfers between devices: 24.6 us -> 6.64 us  [send(): tok_pieces[s] = lax.ppermute(piece, 'dp', pairs)]
    ppermute x10 -> x18, starting transfers between devices: 4.99 us -> 20 us  [flip_bit(): return lax.ppermute(value, axis, [(k, k ^ bit) for k in range(size)])]
    all_to_all x2 -> x3, waiting for transfers between devices: 14.2 us -> 0.16 us  [the longest x1 0.15 us: local(): lax.all_to_all(out_t.reshape(n_dp, rows, width), 'dp', 0, 0, tiled=True)]
    ppermute x10 -> x18, waiting for transfers between devices: 0.03 us -> 11.9 us  [flip_bit(): return lax.ppermute(value, axis, [(k, k ^ bit) for k in range(size)])]
    all_to_all x2 -> x3, starting transfers between devices: 12.4 us -> 18.7 us  [the longest x1 6.57 us: local(): cot = lax.all_to_all(cot, 'dp', 0, 0, tiled=True).reshape(length, width)]
    unnamed x14, local copies, waits for them, and re-layouts: 5.86 us -> 0.58 us
    pallas_call x1, Pallas kernels: 9.99 us -> 12.4 us  [forward(): pl.pallas_call(partial(forward_kernel, n, n_t, blocks, block), out_shape=...]
  transfers between devices with their start and end apart: 43 -> 31, of which waited for: 9 -> 13; matrix products, arithmetic and copies ran while one was open for 2% -> 0% of each run, Pallas kernels for 36% -> 46%
where the time goes in v1:
time: 145 us
  Pallas kernels  71.3 us (49%)
  starting transfers between devices  53.3 us (37%)
  waiting for transfers between devices  18.7 us (13%)
    ppermute x18, starting transfers between devices, flip_bit(): return lax.ppermute(value, axis, [(k, k ^ bit) for k in range(size)])  20 us
    ppermute x7, starting transfers between devices, send(): tok_pieces[s] = lax.ppermute(piece, 'dp', pairs)  12.6 us
    pallas_call x1, Pallas kernels, forward(): pl.pallas_call(partial(forward_kernel, n, n_t, blocks, block), out_shape=...  12.4 us
    ppermute x18, waiting for transfers between devices, flip_bit(): return lax.ppermute(value, axis, [(k, k ^ bit) for k in range(size)])  11.9 us
    pallas_call x1, Pallas kernels, mix_back(): pl.pallas_call(partial(mix_back_kernel, n, n_t, blocks, block), out_shape...  11 us
    pallas_call x1, Pallas kernels, norm_back(): pl.pallas_call(partial(norm_back_kernel, blocks, block), out_shape=[hbm((...  8.57 us
    pallas_call x1, Pallas kernels, taps_back(): pl.pallas_call(partial(taps_back_kernel, n, states), out_shape=[jax.Shape...  8.34 us
    ppermute x7, waiting for transfers between devices, send(): tok_pieces[s] = lax.ppermute(piece, 'dp', pairs)  6.64 us
  transfers between devices with their start and end apart: 31, of which 13 were waited for; matrix products, arithmetic and copies ran while one was open for 0% of the time, Pallas kernels for 46%

profile of v1, /device:TPU:0, one launch (start us, length us, event | category | flops | bytes accessed | tf_op | source)
XLA Modules:
  0.0 144.8 jit_solution(12190656648158628503)
XLA Ops:
  0.7 2.0 %part.2 = (bf16[128,512]{1,0:T(8,128)(2,1)S(1)}, bf16[128,512]{1,0:T(8,128)(2,1)S(1)}, bf16[128,512]{1,0:T(8,128)(2,1)S(1)}, bf16[128,512]{1,0:T(8,128)(2,1)S(1)...) custom-call(s32[2]{0:T(128)S(1)} %pad_add_fusion.sc, ...), custom_call_target="tpu_custom_call" | custom-call | bytes 30000 | tf_op jit(solution)/shard_map/part/pallas_call | solution.py:1100
  3.7 4.1 %collective-permute-start = (bf16[1,248,128]{2,1,0:T(8,128)(2,1)S(1)}, bf16[1,248,128]{2,1,0:T(8,128)(2,1)S(1)}, u32[]{:S(2)}, u32[]{:S(2)}) collective-permute-start(bf16[1,248,128]{2,1,0:T(8,128)(2,1)S(1)} %pack.1.own), channel_id=1, source_target_pairs={{0,16},{4,20},{8,24},{12,28},{16,0},{20,4},{24,8},{28,12},{1,17},{... | collective-permute-start | bytes 190472 | tf_op jit(solution)/shard_map/ppermute | solution.py:94
  7.8 1.5 %collective-permute-start.1 = (bf16[128,512]{1,0:T(8,128)(2,1)S(1)}, bf16[128,512]{1,0:T(8,128)(2,1)S(1)}, u32[]{:S(2)}, u32[]{:S(2)}) collective-permute-start(bf16[128,512]{1,0:T(8,128)(2,1)S(1)} %get-tuple-element.91), channel_id=1, source_target_pairs={{0,4},{4,8},{8,12},{12,16},{16,20},{20,24},{24,28},{28,0},{1,5},{5... | collective-permute-start | bytes 393224 | tf_op jit(solution)/shard_map/ppermute | solution.py:1178
  9.3 2.1 %collective-permute-done.got = bf16[1,248,128]{2,1,0:T(8,128)(2,1)S(1)} collective-permute-done((bf16[1,248,128]{2,1,0:T(8,128)(2,1)S(1)}, bf16[1,248,128]{2,1,0:T(8,128)(2,1)S(1)}, u32[]{:S(2)}, u32[]{:S(2)}) %collective-permute-start) | collective-permute-done | bytes 63520 | tf_op jit(solution)/shard_map/ppermute | solution.py:94
  12.6 3.4 %collective-permute-start.5 = (bf16[128,512]{1,0:T(8,128)(2,1)S(1)}, bf16[128,512]{1,0:T(8,128)(2,1)S(1)}, u32[]{:S(2)}, u32[]{:S(2)}) collective-permute-start(bf16[128,512]{1,0:T(8,128)(2,1)S(1)} %get-tuple-element.94), channel_id=1, source_target_pairs={{0,16},{4,20},{8,24},{12,28},{16,0},{20,4},{24,8},{28,12},{1,17},{... | collective-permute-start | bytes 393224 | tf_op jit(solution)/shard_map/ppermute | solution.py:1178
  16.0 1.5 %collective-permute-start.4 = (bf16[128,512]{1,0:T(8,128)(2,1)S(1)}, bf16[128,512]{1,0:T(8,128)(2,1)S(1)}, u32[]{:S(2)}, u32[]{:S(2)}) collective-permute-start(bf16[128,512]{1,0:T(8,128)(2,1)S(1)} %get-tuple-element.93), channel_id=1, source_target_pairs={{0,12},{4,16},{8,20},{12,24},{16,28},{20,0},{24,4},{28,8},{1,13},{... | collective-permute-start | bytes 393224 | tf_op jit(solution)/shard_map/ppermute | solution.py:1178
  17.5 1.6 %collective-permute-done.2.got = bf16[2,248,128]{2,1,0:T(8,128)(2,1)S(1)} collective-permute-done((bf16[2,248,128]{2,1,0:T(8,128)(2,1)S(1)}, bf16[2,248,128]{2,1,0:T(8,128)(2,1)S(1)}, u32[]{:S(2)}, u32[]{:S(2)}) %collective-permute-start.2) | collective-permute-done | bytes 127008 | tf_op jit(solution)/shard_map/ppermute | solution.py:94
  19.6 1.5 %collective-permute-start.8 = (bf16[4,248,128]{2,1,0:T(8,128)(2,1)S(1)}, bf16[4,248,128]{2,1,0:T(8,128)(2,1)S(1)}, u32[]{:S(2)}, u32[]{:S(2)}) collective-permute-start(bf16[4,248,128]{2,1,0:T(8,128)(2,1)S(1)} %merge.4.own), channel_id=1, source_target_pairs={{0,4},{4,0},{8,12},{12,8},{16,20},{20,16},{24,28},{28,24},{1,5},{5... | collective-permute-start | bytes 761864 | tf_op jit(solution)/shard_map/ppermute | solution.py:94
  21.2 5.0 %collective-permute-start.6 = (bf16[128,512]{1,0:T(8,128)(2,1)S(1)}, bf16[128,512]{1,0:T(8,128)(2,1)S(1)}, u32[]{:S(2)}, u32[]{:S(2)}) collective-permute-start(bf16[128,512]{1,0:T(8,128)(2,1)S(1)} %get-tuple-element.100), channel_id=1, source_target_pairs={{0,20},{4,24},{8,28},{12,0},{16,4},{20,8},{24,12},{28,16},{1,21},{... | collective-permute-start | bytes 393224 | tf_op jit(solution)/shard_map/ppermute | solution.py:1178
  26.2 2.8 %collective-permute-done.5.refs_4_ = bf16[128,512]{1,0:T(8,128)(2,1)S(1)} collective-permute-done((bf16[128,512]{1,0:T(8,128)(2,1)S(1)}, bf16[128,512]{1,0:T(8,128)(2,1)S(1)}, u32[]{:S(2)}, u32[]{:S(2)}) %collective-permute-start.5) | collective-permute-done | bytes 131104 | tf_op jit(solution)/shard_map/ppermute | solution.py:1178
  29.0 3.4 %collective-permute-done.4.refs_3_ = bf16[128,512]{1,0:T(8,128)(2,1)S(1)} collective-permute-done((bf16[128,512]{1,0:T(8,128)(2,1)S(1)}, bf16[128,512]{1,0:T(8,128)(2,1)S(1)}, u32[]{:S(2)}, u32[]{:S(2)}) %collective-permute-start.4) | collective-permute-done | bytes 131104 | tf_op jit(solution)/shard_map/ppermute | solution.py:1178
  33.7 2.8 %part.3 = bf16[8,128,512]{2,1,0:T(8,128)(2,1)} custom-call(s32[2]{0:T(128)S(1)} %pad_add_fusion.sc, bf16[128,8,512]{2,1,0:T(8,128)(2,1)} %whole.3), custom_call_target="tpu_custom_call" | custom-call | bytes 30000 | tf_op jit(solution)/shard_map/part/pallas_call | solution.py:1100
  37.4 6.6 %all-to-all-start.1 = ((bf16[8,128,512]{2,1,0:T(8,128)(2,1)}), bf16[8,128,512]{2,1,0:T(8,128)(2,1)}, u32[]{:S(2)}, u32[]{:S(2)}) async-start(bf16[8,128,512]{2,1,0:T(8,128)(2,1)} %part.3), calls=%async_computation.1 | async-start | bytes 2097152 | tf_op jit(solution)/shard_map/all_to_all | solution.py:1192
  44.0 1.6 %collective-permute-start.14 = (bf16[8,128,128]{2,1,0:T(8,128)(2,1)S(1)}, bf16[8,128,128]{2,1,0:T(8,128)(2,1)S(1)}, u32[]{:S(2)}, u32[]{:S(2)}) collective-permute-start(bf16[8,128,128]{2,1,0:T(8,128)(2,1)S(1)} %slice.4.refs_4_), channel_id=1, source_target_pairs={{0,2},{1,3},{2,0},{3,1},{4,6},{5,7},{6,4},{7,5},{8,10},{9,11},{10,... | collective-permute-start | bytes 786440 | tf_op jit(solution)/shard_map/ppermute | solution.py:94
  45.5 6.1 %taps.1 = (bf16[1024,128]{1,0:T(8,128)(2,1)S(1)}, f32[4,64,128]{2,1,0:T(8,128)S(1)}, f32[8,512]{1,0:T(8,128)S(1)}, f32[1,1024]{1,0:T(1,128)S(1)}) custom-call(s32[2]{0:T(128)S(1)} %pad_add_fusion.sc, bf16[8,248,128]{2,1,0:T(8,128)(2,1)S(1)} %merge.5.blob), custom_call_target="tpu_custom_call" | custom-call | bytes 70000 | tf_op jit(solution)/shard_map/taps/pallas_call | solution.py:251
  52.3 6.1 %enter.1 = (bf16[1024,512]{1,0:T(8,128)(2,1)S(1)}, bf16[1024,512]{1,0:T(8,128)(2,1)S(1)}, f32[4,512,512]{2,1,0:T(8,128)S(1)}, bf16[1024,512]{1,0:T(8,128)(2,1)},...) custom-call(s32[2]{0:T(128)S(1)} %pad_add_fusion.sc, f32[8,512]{1,0:T(8,128)S(1)} %get-tuple-element.104.vec, ...), custom_call_target="tpu_custom_call" | custom-call | bytes 70000 | tf_op jit(solution)/shard_map/enter/pallas_call | solution.py:463
  61.2 12.4 %forward.1 = (bf16[1024,512]{1,0:T(8,128)(2,1)}, bf16[4,512,512]{2,1,0:T(8,128)(2,1)}, bf16[512,1024]{1,0:T(8,128)(2,1)}, bf16[1024,512]{1,0:T(8,128)(2,1)}, bf1...) custom-call(s32[2]{0:T(128)S(1)} %pad_add_fusion.sc, s32[32]{0:T(128)S(1)} %copy-done.5, ...), custom_call_target="tpu_custom_call" | custom-call | bytes 150000 | tf_op jit(solution)/shard_map/forward/pallas_call | solution.py:607
  73.6 6.1 %all-to-all-start = ((bf16[8,128,512]{2,1,0:T(8,128)(2,1)}), bf16[8,128,512]{2,1,0:T(8,128)(2,1)S(1)}, u32[]{:S(2)}, u32[]{:S(2)}) async-start(bf16[8,128,512]{2,1,0:T(8,128)(2,1)} %bitcast.32), calls=%async_computation | async-start | bytes 2097152 | tf_op jit(solution)/shard_map/all_to_all | solution.py:1210
  79.7 11.0 %mix_back.1 = (bf16[2,1024,128]{2,1,0:T(8,128)(2,1)S(1)}, bf16[2,1024,128]{2,1,0:T(8,128)(2,1)S(1)}, bf16[1024,1024]{1,0:T(8,128)(2,1)S(1)}, bf16[1024,512]{1,0:...) custom-call(s32[2]{0:T(128)S(1)} %pad_add_fusion.sc, s32[32]{0:T(128)S(1)} %copy-done.5, ...), custom_call_target="tpu_custom_call" | custom-call | bytes 120000 | tf_op jit(solution)/shard_map/mix_back/pallas_call | solution.py:763
  90.8 2.5 %weight_back.1 = (bf16[2,8,128,128]{3,2,1,0:T(8,128)(2,1)S(1)}, bf16[2,8,128,128]{3,2,1,0:T(8,128)(2,1)S(1)}) custom-call(s32[2]{0:T(128)S(1)} %pad_add_fusion.sc, bf16[1024,512]{1,0:T(8,128)(2,1)S(1)} %copy-done.2, bf16[1024,1024]{1,0:T(8,128)(2,1)S(1)} %get-tuple-element.126.grad_pre), custom_call_target="tpu_custom_call" | custom-call | bytes 30000 | tf_op jit(solution)/shard_map/weight_back/pallas_call | solution.py:826
  94.7 1.6 %collective-permute-start.17 = (bf16[1,1024,128]{2,1,0:T(8,128)(2,1)S(1)}, bf16[1,1024,128]{2,1,0:T(8,128)(2,1)S(1)}, u32[]{:S(2)}, u32[]{:S(2)}) collective-permute-start(bf16[1,1024,128]{2,1,0:T(8,128)(2,1)S(1)} %get-tuple-element.130), channel_id=1, source_target_pairs={{0,2},{1,3},{2,0},{3,1},{4,6},{5,7},{6,4},{7,5},{8,10},{9,11},{10,... | collective-permute-start | bytes 786440 | tf_op jit(solution)/shard_map/ppermute | solution.py:94
  96.3 8.6 %norm_back.1 = (bf16[1024,512]{1,0:T(8,128)(2,1)}, f32[8,512]{1,0:T(8,128)S(1)}, f32[8,512]{1,0:T(8,128)S(1)}) custom-call(s32[2]{0:T(128)S(1)} %pad_add_fusion.sc, f32[8,512]{1,0:T(8,128)S(1)} %get-tuple-element.104.vec, bf16[256,512]{1,0:T(8,128)(2,1)S(1)} %copy-done, f32[4,512,512]{2,1,0:T(8,128)S(1)} %get-tuple-element.132.spec_g, ...), custom_call_target="tpu_custom_call" | custom-call | bytes 100000 | tf_op jit(solution)/shard_map/norm_back/pallas_call | solution.py:938
  106.4 6.0 %all-to-all-start.2 = ((bf16[8,128,512]{2,1,0:T(8,128)(2,1)}), bf16[8,128,512]{2,1,0:T(8,128)(2,1)S(1)}, u32[]{:S(2)}, u32[]{:S(2)}) async-start(bf16[8,128,512]{2,1,0:T(8,128)(2,1)} %bitcast.31), calls=%async_computation.2 | async-start | bytes 2097152 | tf_op jit(solution)/shard_map/all_to_all | solution.py:1233
  112.9 8.3 %taps_back.1 = (bf16[4,160,128]{2,1,0:T(8,128)(2,1)S(1)}, bf16[4,160,128]{2,1,0:T(8,128)(2,1)S(1)}, f32[24,128]{1,0:T(8,128)S(1)}) custom-call(s32[2]{0:T(128)S(1)} %pad_add_fusion.sc, f32[4,64,128]{2,1,0:T(8,128)S(1)} %get-tuple-element.116.par, f32[8,512]{1,0:T(8,128)S(1)} %get-tuple-element.104.vec, bf16[1024,128]{1,0:T(8,128)(2,1)S(1)} %bitcast.29, ...), custom_call_target="tpu_custom_call" | custom-call | bytes 100000 | tf_op jit(solution)/shard_map/taps_back/pallas_call | solution.py:365
  123.8 2.1 %collective-permute-start.20 = (bf16[4,160,128]{2,1,0:T(8,128)(2,1)S(1)}, bf16[4,160,128]{2,1,0:T(8,128)(2,1)S(1)}, u32[]{:S(2)}, u32[]{:S(2)}) collective-permute-start(bf16[4,160,128]{2,1,0:T(8,128)(2,1)S(1)} %get-tuple-element.150), channel_id=1, source_target_pairs={{0,4},{4,0},{8,12},{12,8},{16,20},{20,16},{24,28},{28,24},{1,5},{5... | collective-permute-start | bytes 491528 | tf_op jit(solution)/shard_map/ppermute | solution.py:94
  127.1 2.2 %weave.2 = bf16[128,8,512]{2,1,0:T(8,128)(2,1)} custom-call(s32[2]{0:T(128)S(1)} %pad_add_fusion.sc, bf16[8,128,512]{2,1,0:T(8,128)(2,1)S(1)} %all-to-all-done.refs_0_), custom_call_target="tpu_custom_call" | custom-call | bytes 30000 | tf_op jit(solution)/shard_map/weave/pallas_call | solution.py:1054
  129.3 4.2 %collective-permute-done.24.refs_1_ = f32[24,128]{1,0:T(8,128)S(1)} collective-permute-done((f32[24,128]{1,0:T(8,128)S(1)}, f32[24,128]{1,0:T(8,128)S(1)}, u32[]{:S(2)}, u32[]{:S(2)}) %collective-permute-start.24) | collective-permute-done | bytes 12320 | tf_op jit(solution)/shard_map/ppermute | solution.py:94
  135.0 2.2 %collective-permute-start.26 = (bf16[192,128]{1,0:T(8,128)(2,1)S(1)}, bf16[192,128]{1,0:T(8,128)(2,1)S(1)}, u32[]{:S(2)}, u32[]{:S(2)}) collective-permute-start(bf16[192,128]{1,0:T(8,128)(2,1)S(1)} %get-tuple-element.156), channel_id=1, source_target_pairs={{0,16},{4,20},{8,24},{12,28},{16,0},{20,4},{24,8},{28,12},{1,17},{... | collective-permute-start | bytes 147464 | tf_op jit(solution)/shard_map/ppermute | solution.py:94
  137.2 1.3 collective-permute-start.27
  138.6 2.2 %weave.3 = bf16[128,8,512]{2,1,0:T(8,128)(2,1)} custom-call(s32[2]{0:T(128)S(1)} %pad_add_fusion.sc, bf16[8,128,512]{2,1,0:T(8,128)(2,1)S(1)} %all-to-all-done.2.refs_0_), custom_call_target="tpu_custom_call" | custom-call | bytes 30000 | tf_op jit(solution)/shard_map/weave/pallas_call | solution.py:1054
  140.8 2.3 %collective-permute-done.27.refs_3_ = bf16[192,128]{1,0:T(8,128)(2,1)S(1)} collective-permute-done((bf16[192,128]{1,0:T(8,128)(2,1)S(1)}, bf16[192,128]{1,0:T(8,128)(2,1)S(1)}, u32[]{:S(2)}, u32[]{:S(2)}) %collective-permute-start.27) | collective-permute-done | bytes 49184 | tf_op jit(solution)/shard_map/ppermute | solution.py:94
  143.1 1.7 %totals.1 = (f32[128,128]{1,0:T(8,128)}, f32[8,128]{1,0:T(8,128)}, f32[8,128]{1,0:T(8,128)}, f32[8,128]{1,0:T(8,128)}, f32[8,128]{1,0:T(8,128)}, /*index=5*/f32[...) custom-call(s32[2]{0:T(128)S(1)} %pad_add_fusion.sc, ...), custom_call_target="tpu_custom_call" | custom-call | bytes 10000 | tf_op jit(solution)/shard_map/totals/pallas_call | solution.py:1138
  (67 shorter events, 17.2 us)
Async XLA Ops:
  0.6 51.6 %copy-start.1 = (bf16[512,256]{1,0:T(8,128)(2,1)S(1)}, bf16[512,256]{1,0:T(8,128)(2,1)}, u32[]{:S(2)}) copy-start(bf16[512,256]{1,0:T(8,128)(2,1)} %constant.17.clone.basis_ref) | copy-start | bytes 786436
  3.7 7.7 %collective-permute-start = (bf16[1,248,128]{2,1,0:T(8,128)(2,1)S(1)}, bf16[1,248,128]{2,1,0:T(8,128)(2,1)S(1)}, u32[]{:S(2)}, u32[]{:S(2)}) collective-permute-start(bf16[1,248,128]{2,1,0:T(8,128)(2,1)S(1)} %pack.1.own), channel_id=1, source_target_pairs={{0,16},{4,20},{8,24},{12,28},{16,0},{20,4},{24,8},{28,12},{1,17},{... | collective-permute-start | bytes 190472 | tf_op jit(solution)/shard_map/ppermute | solution.py:94
  7.8 9.7 %collective-permute-start.1 = (bf16[128,512]{1,0:T(8,128)(2,1)S(1)}, bf16[128,512]{1,0:T(8,128)(2,1)S(1)}, u32[]{:S(2)}, u32[]{:S(2)}) collective-permute-start(bf16[128,512]{1,0:T(8,128)(2,1)S(1)} %get-tuple-element.91), channel_id=1, source_target_pairs={{0,4},{4,8},{8,12},{12,16},{16,20},{20,24},{24,28},{28,0},{1,5},{5... | collective-permute-start | bytes 393224 | tf_op jit(solution)/shard_map/ppermute | solution.py:1178
  12.0 7.1 %collective-permute-start.2 = (bf16[2,248,128]{2,1,0:T(8,128)(2,1)S(1)}, bf16[2,248,128]{2,1,0:T(8,128)(2,1)S(1)}, u32[]{:S(2)}, u32[]{:S(2)}) collective-permute-start(bf16[2,248,128]{2,1,0:T(8,128)(2,1)S(1)} %merge.3.own), channel_id=1, source_target_pairs={{0,8},{4,12},{8,0},{12,4},{16,24},{20,28},{24,16},{28,20},{1,9},{5... | collective-permute-start | bytes 380936 | tf_op jit(solution)/shard_map/ppermute | solution.py:94
  12.6 16.4 %collective-permute-start.5 = (bf16[128,512]{1,0:T(8,128)(2,1)S(1)}, bf16[128,512]{1,0:T(8,128)(2,1)S(1)}, u32[]{:S(2)}, u32[]{:S(2)}) collective-permute-start(bf16[128,512]{1,0:T(8,128)(2,1)S(1)} %get-tuple-element.94), channel_id=1, source_target_pairs={{0,16},{4,20},{8,24},{12,28},{16,0},{20,4},{24,8},{28,12},{1,17},{... | collective-permute-start | bytes 393224 | tf_op jit(solution)/shard_map/ppermute | solution.py:1178
  16.0 16.4 %collective-permute-start.4 = (bf16[128,512]{1,0:T(8,128)(2,1)S(1)}, bf16[128,512]{1,0:T(8,128)(2,1)S(1)}, u32[]{:S(2)}, u32[]{:S(2)}) collective-permute-start(bf16[128,512]{1,0:T(8,128)(2,1)S(1)} %get-tuple-element.93), channel_id=1, source_target_pairs={{0,12},{4,16},{8,20},{12,24},{16,28},{20,0},{24,4},{28,8},{1,13},{... | collective-permute-start | bytes 393224 | tf_op jit(solution)/shard_map/ppermute | solution.py:1178
  19.6 16.8 %collective-permute-start.8 = (bf16[4,248,128]{2,1,0:T(8,128)(2,1)S(1)}, bf16[4,248,128]{2,1,0:T(8,128)(2,1)S(1)}, u32[]{:S(2)}, u32[]{:S(2)}) collective-permute-start(bf16[4,248,128]{2,1,0:T(8,128)(2,1)S(1)} %merge.4.own), channel_id=1, source_target_pairs={{0,4},{4,0},{8,12},{12,8},{16,20},{20,16},{24,28},{28,24},{1,5},{5... | collective-permute-start | bytes 761864 | tf_op jit(solution)/shard_map/ppermute | solution.py:94
  21.2 15.2 %collective-permute-start.3 = (bf16[128,512]{1,0:T(8,128)(2,1)S(1)}, bf16[128,512]{1,0:T(8,128)(2,1)S(1)}, u32[]{:S(2)}, u32[]{:S(2)}) collective-permute-start(bf16[128,512]{1,0:T(8,128)(2,1)S(1)} %get-tuple-element.92), channel_id=1, source_target_pairs={{0,8},{4,12},{8,16},{12,20},{16,24},{20,28},{24,0},{28,4},{1,9},{5... | collective-permute-start | bytes 393224 | tf_op jit(solution)/shard_map/ppermute | solution.py:1178
  21.2 15.2 %collective-permute-start.6 = (bf16[128,512]{1,0:T(8,128)(2,1)S(1)}, bf16[128,512]{1,0:T(8,128)(2,1)S(1)}, u32[]{:S(2)}, u32[]{:S(2)}) collective-permute-start(bf16[128,512]{1,0:T(8,128)(2,1)S(1)} %get-tuple-element.100), channel_id=1, source_target_pairs={{0,20},{4,24},{8,28},{12,0},{16,4},{20,8},{24,12},{28,16},{1,21},{... | collective-permute-start | bytes 393224 | tf_op jit(solution)/shard_map/ppermute | solution.py:1178
  29.0 7.4 %collective-permute-start.7 = (bf16[128,512]{1,0:T(8,128)(2,1)S(1)}, bf16[128,512]{1,0:T(8,128)(2,1)S(1)}, u32[]{:S(2)}, u32[]{:S(2)}) collective-permute-start(bf16[128,512]{1,0:T(8,128)(2,1)S(1)} %get-tuple-element.101), channel_id=1, source_target_pairs={{0,24},{4,28},{8,0},{12,4},{16,8},{20,12},{24,16},{28,20},{1,25},{... | collective-permute-start | bytes 393224 | tf_op jit(solution)/shard_map/ppermute | solution.py:1178
  32.4 5.0 %collective-permute-start.9 = (bf16[128,512]{1,0:T(8,128)(2,1)S(1)}, bf16[128,512]{1,0:T(8,128)(2,1)S(1)}, u32[]{:S(2)}, u32[]{:S(2)}) collective-permute-start(bf16[128,512]{1,0:T(8,128)(2,1)S(1)} %get-tuple-element.106), channel_id=1, source_target_pairs={{0,28},{4,0},{8,4},{12,8},{16,12},{20,16},{24,20},{28,24},{1,29},{... | collective-permute-start | bytes 393224 | tf_op jit(solution)/shard_map/ppermute | solution.py:1178
  37.4 36.2 %all-to-all-start.1 = ((bf16[8,128,512]{2,1,0:T(8,128)(2,1)}), bf16[8,128,512]{2,1,0:T(8,128)(2,1)}, u32[]{:S(2)}, u32[]{:S(2)}) async-start(bf16[8,128,512]{2,1,0:T(8,128)(2,1)} %part.3), calls=%async_computation.1 | async-start | bytes 2097152 | tf_op jit(solution)/shard_map/all_to_all | solution.py:1192
  44.0 15.0 %collective-permute-start.14 = (bf16[8,128,128]{2,1,0:T(8,128)(2,1)S(1)}, bf16[8,128,128]{2,1,0:T(8,128)(2,1)S(1)}, u32[]{:S(2)}, u32[]{:S(2)}) collective-permute-start(bf16[8,128,128]{2,1,0:T(8,128)(2,1)S(1)} %slice.4.refs_4_), channel_id=1, source_target_pairs={{0,2},{1,3},{2,0},{3,1},{4,6},{5,7},{6,4},{7,5},{8,10},{9,11},{10,... | collective-permute-start | bytes 786440 | tf_op jit(solution)/shard_map/ppermute | solution.py:94
  51.7 7.3 %collective-permute-start.11 = (bf16[1024,128]{1,0:T(8,128)(2,1)S(1)}, bf16[1024,128]{1,0:T(8,128)(2,1)S(1)}, u32[]{:S(2)}, u32[]{:S(2)}) collective-permute-start(bf16[1024,128]{1,0:T(8,128)(2,1)S(1)} %get-tuple-element.111.refs_0_), channel_id=1, source_target_pairs={{0,2},{1,3},{2,0},{3,1},{4,6},{5,7},{6,4},{7,5},{8,10},{9,11},{10,... | collective-permute-start | bytes 786440 | tf_op jit(solution)/shard_map/ppermute | solution.py:94
  58.4 1.6 %collective-permute-start.10 = (bf16[1024,128]{1,0:T(8,128)(2,1)S(1)}, bf16[1024,128]{1,0:T(8,128)(2,1)S(1)}, u32[]{:S(2)}, u32[]{:S(2)}) collective-permute-start(bf16[1024,128]{1,0:T(8,128)(2,1)S(1)} %get-tuple-element.111.refs_0_), channel_id=1, source_target_pairs={{0,1},{1,0},{2,3},{3,2},{4,5},{5,4},{6,7},{7,6},{8,9},{9,8},{10,11... | collective-permute-start | bytes 786440 | tf_op jit(solution)/shard_map/ppermute | solution.py:94
  58.5 1.9 %collective-permute-start.13 = (bf16[8,128,128]{2,1,0:T(8,128)(2,1)S(1)}, bf16[8,128,128]{2,1,0:T(8,128)(2,1)S(1)}, u32[]{:S(2)}, u32[]{:S(2)}) collective-permute-start(bf16[8,128,128]{2,1,0:T(8,128)(2,1)S(1)} %slice.4.refs_4_), channel_id=1, source_target_pairs={{0,1},{1,0},{2,3},{3,2},{4,5},{5,4},{6,7},{7,6},{8,9},{9,8},{10,11... | collective-permute-start | bytes 786440 | tf_op jit(solution)/shard_map/ppermute | solution.py:94
  59.0 1.8 %collective-permute-start.12 = (bf16[1024,128]{1,0:T(8,128)(2,1)S(1)}, bf16[1024,128]{1,0:T(8,128)(2,1)S(1)}, u32[]{:S(2)}, u32[]{:S(2)}) collective-permute-start(bf16[1024,128]{1,0:T(8,128)(2,1)S(1)} %collective-permute-done.11.refs_2_), channel_id=1, source_target_pairs={{0,1},{1,0},{2,3},{3,2},{4,5},{5,4},{6,7},{7,6},{8,9},{9,8},{10,11... | collective-permute-start | bytes 786440 | tf_op jit(solution)/shard_map/ppermute | solution.py:94
  59.1 2.1 %collective-permute-start.15 = (bf16[8,128,128]{2,1,0:T(8,128)(2,1)S(1)}, bf16[8,128,128]{2,1,0:T(8,128)(2,1)S(1)}, u32[]{:S(2)}, u32[]{:S(2)}) collective-permute-start(bf16[8,128,128]{2,1,0:T(8,128)(2,1)S(1)} %collective-permute-done.14.refs_6_), channel_id=1, source_target_pairs={{0,1},{1,0},{2,3},{3,2},{4,5},{5,4},{6,7},{7,6},{8,9},{9,8},{10,11... | collective-permute-start | bytes 786440 | tf_op jit(solution)/shard_map/ppermute | solution.py:94
  73.6 32.2 %all-to-all-start = ((bf16[8,128,512]{2,1,0:T(8,128)(2,1)}), bf16[8,128,512]{2,1,0:T(8,128)(2,1)S(1)}, u32[]{:S(2)}, u32[]{:S(2)}) async-start(bf16[8,128,512]{2,1,0:T(8,128)(2,1)} %bitcast.32), calls=%async_computation | async-start | bytes 2097152 | tf_op jit(solution)/shard_map/all_to_all | solution.py:1210
  90.7 3.2 %collective-permute-start.16 = (bf16[2,1024,128]{2,1,0:T(8,128)(2,1)S(1)}, bf16[2,1024,128]{2,1,0:T(8,128)(2,1)S(1)}, u32[]{:S(2)}, u32[]{:S(2)}) collective-permute-start(bf16[2,1024,128]{2,1,0:T(8,128)(2,1)S(1)} %get-tuple-element.124), channel_id=1, source_target_pairs={{0,1},{1,0},{2,3},{3,2},{4,5},{5,4},{6,7},{7,6},{8,9},{9,8},{10,11... | collective-permute-start | bytes 1572872 | tf_op jit(solution)/shard_map/ppermute | solution.py:94
  93.3 11.5 %collective-permute-start.18 = (bf16[2,8,128,128]{3,2,1,0:T(8,128)(2,1)S(1)}, bf16[2,8,128,128]{3,2,1,0:T(8,128)(2,1)S(1)}, u32[]{:S(2)}, u32[]{:S(2)}) collective-permute-start(bf16[2,8,128,128]{3,2,1,0:T(8,128)(2,1)S(1)} %get-tuple-element.143), channel_id=1, source_target_pairs={{0,1},{1,0},{2,3},{3,2},{4,5},{5,4},{6,7},{7,6},{8,9},{9,8},{10,11... | collective-permute-start | bytes 1572872 | tf_op jit(solution)/shard_map/ppermute | solution.py:94
  94.7 11.1 %collective-permute-start.17 = (bf16[1,1024,128]{2,1,0:T(8,128)(2,1)S(1)}, bf16[1,1024,128]{2,1,0:T(8,128)(2,1)S(1)}, u32[]{:S(2)}, u32[]{:S(2)}) collective-permute-start(bf16[1,1024,128]{2,1,0:T(8,128)(2,1)S(1)} %get-tuple-element.130), channel_id=1, source_target_pairs={{0,2},{1,3},{2,0},{3,1},{4,6},{5,7},{6,4},{7,5},{8,10},{9,11},{10,... | collective-permute-start | bytes 786440 | tf_op jit(solution)/shard_map/ppermute | solution.py:94
  106.4 32.2 %all-to-all-start.2 = ((bf16[8,128,512]{2,1,0:T(8,128)(2,1)}), bf16[8,128,512]{2,1,0:T(8,128)(2,1)S(1)}, u32[]{:S(2)}, u32[]{:S(2)}) async-start(bf16[8,128,512]{2,1,0:T(8,128)(2,1)} %bitcast.31), calls=%async_computation.2 | async-start | bytes 2097152 | tf_op jit(solution)/shard_map/all_to_all | solution.py:1233
  112.3 10.8 %collective-permute-start.19 = (bf16[1,8,128,128]{3,2,1,0:T(8,128)(2,1)}, bf16[1,8,128,128]{3,2,1,0:T(8,128)(2,1)S(1)}, u32[]{:S(2)}, u32[]{:S(2)}) collective-permute-start(bf16[1,8,128,128]{3,2,1,0:T(8,128)(2,1)} %copy-done.6), channel_id=1, source_target_pairs={{0,2},{1,3},{2,0},{3,1},{4,6},{5,7},{6,4},{7,5},{8,10},{9,11},{10,... | collective-permute-start | bytes 786440 | tf_op jit(solution)/shard_map/ppermute | solution.py:94
  121.2 4.6 %collective-permute-start.23 = (f32[24,128]{1,0:T(8,128)S(1)}, f32[24,128]{1,0:T(8,128)S(1)}, u32[]{:S(2)}, u32[]{:S(2)}) collective-permute-start(f32[24,128]{1,0:T(8,128)S(1)} %get-tuple-element.151), channel_id=1, source_target_pairs={{0,3},{1,2},{2,1},{3,0},{4,7},{5,6},{6,5},{7,4},{8,11},{9,10},{10,... | collective-permute-start | bytes 36872 | tf_op jit(solution)/shard_map/ppermute | solution.py:1240
  121.6 4.3 %collective-permute-start.22 = (f32[24,128]{1,0:T(8,128)S(1)}, f32[24,128]{1,0:T(8,128)S(1)}, u32[]{:S(2)}, u32[]{:S(2)}) collective-permute-start(f32[24,128]{1,0:T(8,128)S(1)} %get-tuple-element.151), channel_id=1, source_target_pairs={{0,2},{1,3},{2,0},{3,1},{4,6},{5,7},{6,4},{7,5},{8,10},{9,11},{10,... | collective-permute-start | bytes 36872 | tf_op jit(solution)/shard_map/ppermute | solution.py:1240
  122.8 3.0 %collective-permute-start.21 = (f32[24,128]{1,0:T(8,128)S(1)}, f32[24,128]{1,0:T(8,128)S(1)}, u32[]{:S(2)}, u32[]{:S(2)}) collective-permute-start(f32[24,128]{1,0:T(8,128)S(1)} %get-tuple-element.151), channel_id=1, source_target_pairs={{0,1},{1,0},{2,3},{3,2},{4,5},{5,4},{6,7},{7,6},{8,9},{9,8},{10,11... | collective-permute-start | bytes 36872 | tf_op jit(solution)/shard_map/ppermute | solution.py:1240
  123.8 9.7 %collective-permute-start.20 = (bf16[4,160,128]{2,1,0:T(8,128)(2,1)S(1)}, bf16[4,160,128]{2,1,0:T(8,128)(2,1)S(1)}, u32[]{:S(2)}, u32[]{:S(2)}) collective-permute-start(bf16[4,160,128]{2,1,0:T(8,128)(2,1)S(1)} %get-tuple-element.150), channel_id=1, source_target_pairs={{0,4},{4,0},{8,12},{12,8},{16,20},{20,16},{24,28},{28,24},{1,5},{5... | collective-permute-start | bytes 491528 | tf_op jit(solution)/shard_map/ppermute | solution.py:94
  125.9 7.6 %collective-permute-start.24 = (f32[24,128]{1,0:T(8,128)S(1)}, f32[24,128]{1,0:T(8,128)S(1)}, u32[]{:S(2)}, u32[]{:S(2)}) collective-permute-start(f32[24,128]{1,0:T(8,128)S(1)} %add_add_fusion.refs_0_), channel_id=1, source_target_pairs={{0,4},{4,0},{8,12},{12,8},{16,20},{20,16},{24,28},{28,24},{1,5},{5... | collective-permute-start | bytes 36872 | tf_op jit(solution)/shard_map/ppermute | solution.py:94
  134.1 6.6 %collective-permute-start.25 = (bf16[192,128]{1,0:T(8,128)(2,1)S(1)}, bf16[192,128]{1,0:T(8,128)(2,1)S(1)}, u32[]{:S(2)}, u32[]{:S(2)}) collective-permute-start(bf16[192,128]{1,0:T(8,128)(2,1)S(1)} %get-tuple-element.155), channel_id=1, source_target_pairs={{0,8},{4,12},{8,0},{12,4},{16,24},{20,28},{24,16},{28,20},{1,9},{5... | collective-permute-start | bytes 147464 | tf_op jit(solution)/shard_map/ppermute | solution.py:94
  135.0 5.8 %collective-permute-start.26 = (bf16[192,128]{1,0:T(8,128)(2,1)S(1)}, bf16[192,128]{1,0:T(8,128)(2,1)S(1)}, u32[]{:S(2)}, u32[]{:S(2)}) collective-permute-start(bf16[192,128]{1,0:T(8,128)(2,1)S(1)} %get-tuple-element.156), channel_id=1, source_target_pairs={{0,16},{4,20},{8,24},{12,28},{16,0},{20,4},{24,8},{28,12},{1,17},{... | collective-permute-start | bytes 147464 | tf_op jit(solution)/shard_map/ppermute | solution.py:94
  137.2 5.9 %collective-permute-start.27 = (bf16[192,128]{1,0:T(8,128)(2,1)S(1)}, bf16[192,128]{1,0:T(8,128)(2,1)S(1)}, u32[]{:S(2)}, u32[]{:S(2)}) collective-permute-start(bf16[192,128]{1,0:T(8,128)(2,1)S(1)} %get-tuple-element.157), channel_id=1, source_target_pairs={{0,24},{4,28},{8,16},{12,20},{16,8},{20,12},{24,0},{28,4},{1,25},{... | collective-permute-start | bytes 147464 | tf_op jit(solution)/shard_map/ppermute | solution.py:94
  (6 other events, 217.1 us)

commit v2 on v1

--- a/solution.py
+++ b/solution.py
@@ -39,7 +39,7 @@
 
 
 def copies(sems, index, block, j, pairs):
-    at = pl.ds(pl.multiple_of(j * block, block), block)
+    at = pl.ds(j * block if isinstance(j, int) else pl.multiple_of(j * block, block), block)
     return [
         pltpu.make_async_copy(src.at[at], dst.at[at], sems.at[index + k, j])
         for k, (src, dst) in enumerate(pairs)
@@ -403,8 +403,14 @@
     return jnp.dot(ones, x, preferred_element_type=f32)
 
 
+def whole_block(base, block):
+    return pl.ds(base if isinstance(base, int) else pl.multiple_of(base, block), block)
+
+
 def shifted(rows, base):
     size = rows.stop - rows.start
+    if isinstance(base, int):
+        return pl.ds(base + rows.start, size)
     return pl.ds(pl.multiple_of(base + rows.start, size), size)
 
 
@@ -432,25 +438,28 @@
 
     def transform(j, carry):
         base = j * block
-        at = pl.ds(pl.multiple_of(base, block), block)
-        mean[...] = row_sums(tok_all[at, :]) * (1.0 / width)
+        side = j % 2
+        at = whole_block(base, block)
+        mean[side] = row_sums(tok_all[at, :]) * (1.0 / width)
         for r, c in chunks(block, width):
-            centred = tok_all[shifted(r, base), c].astype(f32) - mean[r, :]
-            square[r, c] = (centred * centred).astype(bf16)
-        scale[at, :] = lax.rsqrt(row_sums(square[...]) * (1.0 / width) + epsilon)
+            centred = tok_all[shifted(r, base), c].astype(f32) - mean[side, r, :]
+            square[side, r, c] = (centred * centred).astype(bf16)
+        scale[at, :] = lax.rsqrt(row_sums(square[side]) * (1.0 / width) + epsilon)
         for r, c in chunks(block, width):
             to = shifted(r, base)
-            value = (tok_all[to, c].astype(f32) - mean[r, :]) * scale[to, :]
+            value = (tok_all[to, c].astype(f32) - mean[side, r, :]) * scale[to, :]
             xhat[to, c] = value.astype(bf16)
             sig[to, c] = (value * vec[0:1, c] + vec[1:2, c]).astype(bf16)
         for copy in copies(sems, 0, block, j, saves):
             copy.start()
         value = sig[at, :]
-        xs[j] = jnp.dot(basis_ref[...], value, preferred_element_type=f32)
-        xs[j] += jnp.dot(basis_low[...], value, preferred_element_type=f32)
+        xs[j] = jnp.dot(basis_ref[...], value, preferred_element_type=f32) + jnp.dot(
+            basis_low[...], value, preferred_element_type=f32
+        )
         return carry
 
-    lax.fori_loop(0, blocks, transform, 0)
+    for j in range(blocks):
+        transform(j, 0)
     for j in range(blocks):
         for copy in copies(sems, 0, block, j, saves):
             copy.wait()
@@ -475,8 +484,8 @@
         scratch_shapes=[
             pltpu.VMEM((length, width), bf16),
             pltpu.VMEM((length, LANES), f32),
-            pltpu.VMEM((block, LANES), f32),
-            pltpu.VMEM((block, width), bf16),
+            pltpu.VMEM((2, block, LANES), f32),
+            pltpu.VMEM((2, block, width), bf16),
             pltpu.SemaphoreType.DMA((3, blocks)),
             pltpu.SemaphoreType.DMA((n,)),
         ],
@@ -516,13 +525,15 @@
     copy_w.start()
 
     def spectrum(d, carry):
-        at = pl.ds(pl.multiple_of(d * block, block), block)
+        at = whole_block(d * block, block)
         value = taps[at, :]
-        raw[d] = jnp.dot(basis_ref[...], value, preferred_element_type=f32)
-        raw[d] += jnp.dot(basis_low[...], value, preferred_element_type=f32)
+        raw[d] = jnp.dot(basis_ref[...], value, preferred_element_type=f32) + jnp.dot(
+            basis_low[...], value, preferred_element_type=f32
+        )
         return carry
 
-    lax.fori_loop(0, blocks, spectrum, 0)
+    for d in range(blocks):
+        spectrum(d, 0)
 
     def product(sign, row, lanes):
         re, im = pl.ds(row, TILE), pl.ds(pl.multiple_of(row + block, TILE), TILE)
@@ -557,27 +568,30 @@
     copy_spec.start()
 
     def tail(j, carry):
-        mix[...] = jnp.dot(basis_t[...], zs[j], preferred_element_type=f32)
-        mix[...] += jnp.dot(basis_t_low[...], zs[j], preferred_element_type=f32)
-        mix[...] += jnp.dot(basis_t[...], zs_low[j], preferred_element_type=f32)
+        value = zs[j]
+        rest = jnp.dot(basis_t_low[...], value, preferred_element_type=f32) + jnp.dot(
+            basis_t[...], zs_low[j], preferred_element_type=f32
+        )
+        side = j % 2
+        mix[side] = jnp.dot(basis_t[...], value, preferred_element_type=f32) + rest
 
         base = j * block
         for r, c in chunks(block, width):
             to = shifted(r, base)
-            v = mix[r, c] + vec[3:4, c] * sig[to, c].astype(f32)
+            v = mix[side, r, c] + vec[3:4, c] * sig[to, c].astype(f32)
             sq = v * v
             t = jnp.tanh(v * (0.7978845608 + (0.7978845608 * 0.044715) * sq))
             half_t = 0.5 + 0.5 * t
             active[to, c] = (v * half_t).astype(bf16)
             inner = 0.7978845608 * 0.5 + (0.7978845608 * 1.5 * 0.044715) * sq
             slope[to, c] = (half_t + v * (1.0 - t * t) * inner).astype(bf16)
-        whole = pl.ds(pl.multiple_of(base, block), block)
-        pre[...] = jnp.dot(active[whole, :], w[...], preferred_element_type=f32)
+        whole = whole_block(base, block)
+        pre[side] = jnp.dot(active[whole, :], w[...], preferred_element_type=f32)
         for r, c in chunks(block, width):
             to = shifted(r, base)
             far = slice(width + c.start, width + c.stop)
-            a = pre[r, c] + b_out[:, c]
-            t = 0.5 * jnp.tanh(0.5 * (pre[r, far] + b_out[:, far]))
+            a = pre[side, r, c] + b_out[:, c]
+            t = 0.5 * jnp.tanh(0.5 * (pre[side, r, far] + b_out[:, far]))
             g = 0.5 + t
             place = base + r.start + lax.broadcasted_iota(jnp.int32, a.shape, 0)
             add = jnp.where(place < seq_len, a * g, 0.0)
@@ -588,7 +602,8 @@
             c.start()
         return carry
 
-    lax.fori_loop(0, blocks, tail, 0)
+    for j in range(blocks):
+        tail(j, 0)
     copy_w.wait()
     copy_spec.wait()
     for j in range(blocks):
@@ -622,8 +637,8 @@
             pltpu.VMEM((blocks, 2 * block, width), f32),
             pltpu.VMEM((blocks, 2 * block, width), bf16),
             pltpu.VMEM((blocks, 2 * block, width), bf16),
-            pltpu.VMEM((block, width), f32),
-            pltpu.VMEM((block, 2 * width), f32),
+            pltpu.VMEM((2, block, width), f32),
+            pltpu.VMEM((2, block, 2 * width), f32),
             pltpu.VMEM((blocks, 2 * block, width), bf16),
             pltpu.VMEM((width, 2 * width), bf16),
             buffer,
@@ -634,7 +649,7 @@
             pltpu.SemaphoreType.DMA((5, blocks)),
             pltpu.SemaphoreType.DMA((2,)),
         ],
-        compiler_params=params(24),
+        compiler_params=params(26),
         cost_estimate=cost(15),
         name="forward",
     )(
@@ -691,7 +706,7 @@
         def _():
             copy_w.wait()
 
-        whole = pl.ds(pl.multiple_of(base, block), block)
+        whole = whole_block(base, block)
         bias_grad[...] += column_sums(grad_pre[whole, :])
         xs[j] = jnp.dot(basis_ref[...], sig[whole, :], preferred_element_type=f32)
         act_f[...] = lax.dot_general(
@@ -1167,7 +1182,7 @@
     vecs = [after(ln_gain, pieces), ln_bias, log_dt, skip_gain, b_out]
     blob = pack([lam_log.T, lam_im.T, w_re.T, w_im.T], vecs, w_out)
     tok_pieces = dict(enumerate(pieces[:1]))
-    waits, needs = {0: [], 1: [1], 2: [2, 3, 4, 5, 6]}, {5: 0, 6: 1, 7: 1}
+    waits, needs = {0: [], 1: [1], 2: [2, 3, 4]}, {5: 0, 6: 0, 7: 1}
     merges = {-1: ()}
     steps = n_dp.bit_length() - 1
 

time: 145 us -> 143 us (0.986)
  Pallas kernels: 71.3 us -> 69.8 us
where the time goes in v2:
time: 143 us
  Pallas kernels  69.8 us (49%)
  starting transfers between devices  52.6 us (37%)
  waiting for transfers between devices  18.7 us (13%)
    ppermute x18, starting transfers between devices, flip_bit(): return lax.ppermute(value, axis, [(k, k ^ bit) for k in range(size)])  20 us
    ppermute x7, starting transfers between devices, send(): tok_pieces[s] = lax.ppermute(piece, 'dp', pairs)  12.6 us
    ppermute x18, waiting for transfers between devices, flip_bit(): return lax.ppermute(value, axis, [(k, k ^ bit) for k in range(size)])  11.8 us
    pallas_call x1, Pallas kernels, forward(): pl.pallas_call(partial(forward_kernel, n, n_t, blocks, block), out_shape=...  11.4 us
    pallas_call x1, Pallas kernels, mix_back(): pl.pallas_call(partial(mix_back_kernel, n, n_t, blocks, block), out_shape...  11 us
    pallas_call x1, Pallas kernels, norm_back(): pl.pallas_call(partial(norm_back_kernel, blocks, block), out_shape=[hbm((...  8.57 us
    pallas_call x1, Pallas kernels, taps_back(): pl.pallas_call(partial(taps_back_kernel, n, states), out_shape=[jax.Shape...  8.34 us
    ppermute x7, waiting for transfers between devices, send(): tok_pieces[s] = lax.ppermute(piece, 'dp', pairs)  6.63 us
  transfers between devices with their start and end apart: 31, of which 13 were waited for; matrix products, arithmetic and copies ran while one was open for 0% of the time, Pallas kernels for 46%

profile of v2, /device:TPU:0, one launch (start us, length us, event | category | flops | bytes accessed | tf_op | source)
XLA Modules:
  0.0 142.8 jit_solution(6096983575013429299)
XLA Ops:
  0.7 2.0 %part.2 = (bf16[128,512]{1,0:T(8,128)(2,1)S(1)}, bf16[128,512]{1,0:T(8,128)(2,1)S(1)}, bf16[128,512]{1,0:T(8,128)(2,1)S(1)}, bf16[128,512]{1,0:T(8,128)(2,1)S(1)...) custom-call(s32[2]{0:T(128)S(1)} %pad_add_fusion.sc, ...), custom_call_target="tpu_custom_call" | custom-call | bytes 30000 | tf_op jit(solution)/shard_map/part/pallas_call | solution.py:1115
  3.7 4.1 %collective-permute-start = (bf16[1,248,128]{2,1,0:T(8,128)(2,1)S(1)}, bf16[1,248,128]{2,1,0:T(8,128)(2,1)S(1)}, u32[]{:S(2)}, u32[]{:S(2)}) collective-permute-start(bf16[1,248,128]{2,1,0:T(8,128)(2,1)S(1)} %pack.1.own), channel_id=1, source_target_pairs={{0,16},{4,20},{8,24},{12,28},{16,0},{20,4},{24,8},{28,12},{1,17},{... | collective-permute-start | bytes 190472 | tf_op jit(solution)/shard_map/ppermute | solution.py:94
  7.8 1.5 %collective-permute-start.1 = (bf16[128,512]{1,0:T(8,128)(2,1)S(1)}, bf16[128,512]{1,0:T(8,128)(2,1)S(1)}, u32[]{:S(2)}, u32[]{:S(2)}) collective-permute-start(bf16[128,512]{1,0:T(8,128)(2,1)S(1)} %get-tuple-element.91), channel_id=1, source_target_pairs={{0,4},{4,8},{8,12},{12,16},{16,20},{20,24},{24,28},{28,0},{1,5},{5... | collective-permute-start | bytes 393224 | tf_op jit(solution)/shard_map/ppermute | solution.py:1193
  9.3 2.1 %collective-permute-done.got = bf16[1,248,128]{2,1,0:T(8,128)(2,1)S(1)} collective-permute-done((bf16[1,248,128]{2,1,0:T(8,128)(2,1)S(1)}, bf16[1,248,128]{2,1,0:T(8,128)(2,1)S(1)}, u32[]{:S(2)}, u32[]{:S(2)}) %collective-permute-start) | collective-permute-done | bytes 63520 | tf_op jit(solution)/shard_map/ppermute | solution.py:94
  12.6 3.4 %collective-permute-start.5 = (bf16[128,512]{1,0:T(8,128)(2,1)S(1)}, bf16[128,512]{1,0:T(8,128)(2,1)S(1)}, u32[]{:S(2)}, u32[]{:S(2)}) collective-permute-start(bf16[128,512]{1,0:T(8,128)(2,1)S(1)} %get-tuple-element.94), channel_id=1, source_target_pairs={{0,16},{4,20},{8,24},{12,28},{16,0},{20,4},{24,8},{28,12},{1,17},{... | collective-permute-start | bytes 393224 | tf_op jit(solution)/shard_map/ppermute | solution.py:1193
  16.0 1.5 %collective-permute-start.4 = (bf16[128,512]{1,0:T(8,128)(2,1)S(1)}, bf16[128,512]{1,0:T(8,128)(2,1)S(1)}, u32[]{:S(2)}, u32[]{:S(2)}) collective-permute-start(bf16[128,512]{1,0:T(8,128)(2,1)S(1)} %get-tuple-element.93), channel_id=1, source_target_pairs={{0,12},{4,16},{8,20},{12,24},{16,28},{20,0},{24,4},{28,8},{1,13},{... | collective-permute-start | bytes 393224 | tf_op jit(solution)/shard_map/ppermute | solution.py:1193
  17.5 1.6 %collective-permute-done.2.got = bf16[2,248,128]{2,1,0:T(8,128)(2,1)S(1)} collective-permute-done((bf16[2,248,128]{2,1,0:T(8,128)(2,1)S(1)}, bf16[2,248,128]{2,1,0:T(8,128)(2,1)S(1)}, u32[]{:S(2)}, u32[]{:S(2)}) %collective-permute-start.2) | collective-permute-done | bytes 127008 | tf_op jit(solution)/shard_map/ppermute | solution.py:94
  19.6 1.5 %collective-permute-start.6 = (bf16[4,248,128]{2,1,0:T(8,128)(2,1)S(1)}, bf16[4,248,128]{2,1,0:T(8,128)(2,1)S(1)}, u32[]{:S(2)}, u32[]{:S(2)}) collective-permute-start(bf16[4,248,128]{2,1,0:T(8,128)(2,1)S(1)} %merge.4.own), channel_id=1, source_target_pairs={{0,4},{4,0},{8,12},{12,8},{16,20},{20,16},{24,28},{28,24},{1,5},{5... | collective-permute-start | bytes 761864 | tf_op jit(solution)/shard_map/ppermute | solution.py:94
  21.2 5.0 %collective-permute-start.7 = (bf16[128,512]{1,0:T(8,128)(2,1)S(1)}, bf16[128,512]{1,0:T(8,128)(2,1)S(1)}, u32[]{:S(2)}, u32[]{:S(2)}) collective-permute-start(bf16[128,512]{1,0:T(8,128)(2,1)S(1)} %get-tuple-element.104), channel_id=1, source_target_pairs={{0,20},{4,24},{8,28},{12,0},{16,4},{20,8},{24,12},{28,16},{1,21},{... | collective-permute-start | bytes 393224 | tf_op jit(solution)/shard_map/ppermute | solution.py:1193
  26.2 2.8 %collective-permute-done.5.refs_4_ = bf16[128,512]{1,0:T(8,128)(2,1)S(1)} collective-permute-done((bf16[128,512]{1,0:T(8,128)(2,1)S(1)}, bf16[128,512]{1,0:T(8,128)(2,1)S(1)}, u32[]{:S(2)}, u32[]{:S(2)}) %collective-permute-start.5) | collective-permute-done | bytes 131104 | tf_op jit(solution)/shard_map/ppermute | solution.py:1193
  29.0 3.4 %collective-permute-done.4.refs_3_ = bf16[128,512]{1,0:T(8,128)(2,1)S(1)} collective-permute-done((bf16[128,512]{1,0:T(8,128)(2,1)S(1)}, bf16[128,512]{1,0:T(8,128)(2,1)S(1)}, u32[]{:S(2)}, u32[]{:S(2)}) %collective-permute-start.4) | collective-permute-done | bytes 131104 | tf_op jit(solution)/shard_map/ppermute | solution.py:1193
  33.7 2.8 %part.3 = bf16[8,128,512]{2,1,0:T(8,128)(2,1)} custom-call(s32[2]{0:T(128)S(1)} %pad_add_fusion.sc, bf16[128,8,512]{2,1,0:T(8,128)(2,1)} %whole.3), custom_call_target="tpu_custom_call" | custom-call | bytes 30000 | tf_op jit(solution)/shard_map/part/pallas_call | solution.py:1115
  37.4 6.0 %all-to-all-start.1 = ((bf16[8,128,512]{2,1,0:T(8,128)(2,1)}), bf16[8,128,512]{2,1,0:T(8,128)(2,1)}, u32[]{:S(2)}, u32[]{:S(2)}) async-start(bf16[8,128,512]{2,1,0:T(8,128)(2,1)} %part.3), calls=%async_computation.1 | async-start | bytes 2097152 | tf_op jit(solution)/shard_map/all_to_all | solution.py:1207
  43.4 1.6 %collective-permute-start.14 = (bf16[8,128,128]{2,1,0:T(8,128)(2,1)S(1)}, bf16[8,128,128]{2,1,0:T(8,128)(2,1)S(1)}, u32[]{:S(2)}, u32[]{:S(2)}) collective-permute-start(bf16[8,128,128]{2,1,0:T(8,128)(2,1)S(1)} %slice.4.refs_4_), channel_id=1, source_target_pairs={{0,2},{1,3},{2,0},{3,1},{4,6},{5,7},{6,4},{7,5},{8,10},{9,11},{10,... | collective-permute-start | bytes 786440 | tf_op jit(solution)/shard_map/ppermute | solution.py:94
  44.9 6.1 %taps.1 = (bf16[1024,128]{1,0:T(8,128)(2,1)S(1)}, f32[4,64,128]{2,1,0:T(8,128)S(1)}, f32[8,512]{1,0:T(8,128)S(1)}, f32[1,1024]{1,0:T(1,128)S(1)}) custom-call(s32[2]{0:T(128)S(1)} %pad_add_fusion.sc, bf16[8,248,128]{2,1,0:T(8,128)(2,1)S(1)} %merge.5.blob), custom_call_target="tpu_custom_call" | custom-call | bytes 70000 | tf_op jit(solution)/shard_map/taps/pallas_call | solution.py:251
  51.7 5.7 %enter.1 = (bf16[1024,512]{1,0:T(8,128)(2,1)S(1)}, bf16[1024,512]{1,0:T(8,128)(2,1)S(1)}, f32[4,512,512]{2,1,0:T(8,128)S(1)}, bf16[1024,512]{1,0:T(8,128)(2,1)},...) custom-call(s32[2]{0:T(128)S(1)} %pad_add_fusion.sc, f32[8,512]{1,0:T(8,128)S(1)} %get-tuple-element.102.vec, ...), custom_call_target="tpu_custom_call" | custom-call | bytes 70000 | tf_op jit(solution)/shard_map/enter/pallas_call | solution.py:472
  60.1 11.4 %forward.1 = (bf16[1024,512]{1,0:T(8,128)(2,1)}, bf16[4,512,512]{2,1,0:T(8,128)(2,1)}, bf16[512,1024]{1,0:T(8,128)(2,1)}, bf16[1024,512]{1,0:T(8,128)(2,1)}, bf1...) custom-call(s32[2]{0:T(128)S(1)} %pad_add_fusion.sc, s32[32]{0:T(128)S(1)} %copy-done.5, ...), custom_call_target="tpu_custom_call" | custom-call | bytes 150000 | tf_op jit(solution)/shard_map/forward/pallas_call | solution.py:622
  71.5 6.1 %all-to-all-start = ((bf16[8,128,512]{2,1,0:T(8,128)(2,1)}), bf16[8,128,512]{2,1,0:T(8,128)(2,1)S(1)}, u32[]{:S(2)}, u32[]{:S(2)}) async-start(bf16[8,128,512]{2,1,0:T(8,128)(2,1)} %bitcast.32), calls=%async_computation | async-start | bytes 2097152 | tf_op jit(solution)/shard_map/all_to_all | solution.py:1225
  77.6 11.0 %mix_back.1 = (bf16[2,1024,128]{2,1,0:T(8,128)(2,1)S(1)}, bf16[2,1024,128]{2,1,0:T(8,128)(2,1)S(1)}, bf16[1024,1024]{1,0:T(8,128)(2,1)S(1)}, bf16[1024,512]{1,0:...) custom-call(s32[2]{0:T(128)S(1)} %pad_add_fusion.sc, s32[32]{0:T(128)S(1)} %copy-done.5, ...), custom_call_target="tpu_custom_call" | custom-call | bytes 120000 | tf_op jit(solution)/shard_map/mix_back/pallas_call | solution.py:778
  88.7 2.5 %weight_back.1 = (bf16[2,8,128,128]{3,2,1,0:T(8,128)(2,1)S(1)}, bf16[2,8,128,128]{3,2,1,0:T(8,128)(2,1)S(1)}) custom-call(s32[2]{0:T(128)S(1)} %pad_add_fusion.sc, bf16[1024,512]{1,0:T(8,128)(2,1)S(1)} %copy-done.2, bf16[1024,1024]{1,0:T(8,128)(2,1)S(1)} %get-tuple-element.126.grad_pre), custom_call_target="tpu_custom_call" | custom-call | bytes 30000 | tf_op jit(solution)/shard_map/weight_back/pallas_call | solution.py:841
  92.6 1.5 %collective-permute-start.17 = (bf16[1,1024,128]{2,1,0:T(8,128)(2,1)S(1)}, bf16[1,1024,128]{2,1,0:T(8,128)(2,1)S(1)}, u32[]{:S(2)}, u32[]{:S(2)}) collective-permute-start(bf16[1,1024,128]{2,1,0:T(8,128)(2,1)S(1)} %get-tuple-element.130), channel_id=1, source_target_pairs={{0,2},{1,3},{2,0},{3,1},{4,6},{5,7},{6,4},{7,5},{8,10},{9,11},{10,... | collective-permute-start | bytes 786440 | tf_op jit(solution)/shard_map/ppermute | solution.py:94
  94.1 8.6 %norm_back.1 = (bf16[1024,512]{1,0:T(8,128)(2,1)}, f32[8,512]{1,0:T(8,128)S(1)}, f32[8,512]{1,0:T(8,128)S(1)}) custom-call(s32[2]{0:T(128)S(1)} %pad_add_fusion.sc, f32[8,512]{1,0:T(8,128)S(1)} %get-tuple-element.102.vec, bf16[256,512]{1,0:T(8,128)(2,1)S(1)} %copy-done, f32[4,512,512]{2,1,0:T(8,128)S(1)} %get-tuple-element.132.spec_g, ...), custom_call_target="tpu_custom_call" | custom-call | bytes 100000 | tf_op jit(solution)/shard_map/norm_back/pallas_call | solution.py:953
  104.2 6.0 %all-to-all-start.2 = ((bf16[8,128,512]{2,1,0:T(8,128)(2,1)}), bf16[8,128,512]{2,1,0:T(8,128)(2,1)S(1)}, u32[]{:S(2)}, u32[]{:S(2)}) async-start(bf16[8,128,512]{2,1,0:T(8,128)(2,1)} %bitcast.31), calls=%async_computation.2 | async-start | bytes 2097152 | tf_op jit(solution)/shard_map/all_to_all | solution.py:1248
  110.7 8.3 %taps_back.1 = (bf16[4,160,128]{2,1,0:T(8,128)(2,1)S(1)}, bf16[4,160,128]{2,1,0:T(8,128)(2,1)S(1)}, f32[24,128]{1,0:T(8,128)S(1)}) custom-call(s32[2]{0:T(128)S(1)} %pad_add_fusion.sc, f32[4,64,128]{2,1,0:T(8,128)S(1)} %get-tuple-element.116.par, f32[8,512]{1,0:T(8,128)S(1)} %get-tuple-element.102.vec, bf16[1024,128]{1,0:T(8,128)(2,1)S(1)} %bitcast.29, ...), custom_call_target="tpu_custom_call" | custom-call | bytes 100000 | tf_op jit(solution)/shard_map/taps_back/pallas_call | solution.py:365
  121.6 2.1 %collective-permute-start.20 = (bf16[4,160,128]{2,1,0:T(8,128)(2,1)S(1)}, bf16[4,160,128]{2,1,0:T(8,128)(2,1)S(1)}, u32[]{:S(2)}, u32[]{:S(2)}) collective-permute-start(bf16[4,160,128]{2,1,0:T(8,128)(2,1)S(1)} %get-tuple-element.150), channel_id=1, source_target_pairs={{0,4},{4,0},{8,12},{12,8},{16,20},{20,16},{24,28},{28,24},{1,5},{5... | collective-permute-start | bytes 491528 | tf_op jit(solution)/shard_map/ppermute | solution.py:94
  125.0 2.2 %weave.2 = bf16[128,8,512]{2,1,0:T(8,128)(2,1)} custom-call(s32[2]{0:T(128)S(1)} %pad_add_fusion.sc, bf16[8,128,512]{2,1,0:T(8,128)(2,1)S(1)} %all-to-all-done.refs_0_), custom_call_target="tpu_custom_call" | custom-call | bytes 30000 | tf_op jit(solution)/shard_map/weave/pallas_call | solution.py:1069
  127.2 4.2 %collective-permute-done.24.refs_1_ = f32[24,128]{1,0:T(8,128)S(1)} collective-permute-done((f32[24,128]{1,0:T(8,128)S(1)}, f32[24,128]{1,0:T(8,128)S(1)}, u32[]{:S(2)}, u32[]{:S(2)}) %collective-permute-start.24) | collective-permute-done | bytes 12320 | tf_op jit(solution)/shard_map/ppermute | solution.py:94
  132.9 2.2 %collective-permute-start.26 = (bf16[192,128]{1,0:T(8,128)(2,1)S(1)}, bf16[192,128]{1,0:T(8,128)(2,1)S(1)}, u32[]{:S(2)}, u32[]{:S(2)}) collective-permute-start(bf16[192,128]{1,0:T(8,128)(2,1)S(1)} %get-tuple-element.156), channel_id=1, source_target_pairs={{0,16},{4,20},{8,24},{12,28},{16,0},{20,4},{24,8},{28,12},{1,17},{... | collective-permute-start | bytes 147464 | tf_op jit(solution)/shard_map/ppermute | solution.py:94
  135.1 1.3 collective-permute-start.27
  136.4 2.2 %weave.3 = bf16[128,8,512]{2,1,0:T(8,128)(2,1)} custom-call(s32[2]{0:T(128)S(1)} %pad_add_fusion.sc, bf16[8,128,512]{2,1,0:T(8,128)(2,1)S(1)} %all-to-all-done.2.refs_0_), custom_call_target="tpu_custom_call" | custom-call | bytes 30000 | tf_op jit(solution)/shard_map/weave/pallas_call | solution.py:1069
  138.6 2.3 %collective-permute-done.27.refs_3_ = bf16[192,128]{1,0:T(8,128)(2,1)S(1)} collective-permute-done((bf16[192,128]{1,0:T(8,128)(2,1)S(1)}, bf16[192,128]{1,0:T(8,128)(2,1)S(1)}, u32[]{:S(2)}, u32[]{:S(2)}) %collective-permute-start.27) | collective-permute-done | bytes 49184 | tf_op jit(solution)/shard_map/ppermute | solution.py:94
  141.0 1.7 %totals.1 = (f32[128,128]{1,0:T(8,128)}, f32[8,128]{1,0:T(8,128)}, f32[8,128]{1,0:T(8,128)}, f32[8,128]{1,0:T(8,128)}, f32[8,128]{1,0:T(8,128)}, /*index=5*/f32[...) custom-call(s32[2]{0:T(128)S(1)} %pad_add_fusion.sc, ...), custom_call_target="tpu_custom_call" | custom-call | bytes 10000 | tf_op jit(solution)/shard_map/totals/pallas_call | solution.py:1153
  (67 shorter events, 17.2 us)
Async XLA Ops:
  0.6 51.0 %copy-start.1 = (bf16[512,256]{1,0:T(8,128)(2,1)S(1)}, bf16[512,256]{1,0:T(8,128)(2,1)}, u32[]{:S(2)}) copy-start(bf16[512,256]{1,0:T(8,128)(2,1)} %constant.17.clone.basis_ref) | copy-start | bytes 786436
  3.7 7.7 %collective-permute-start = (bf16[1,248,128]{2,1,0:T(8,128)(2,1)S(1)}, bf16[1,248,128]{2,1,0:T(8,128)(2,1)S(1)}, u32[]{:S(2)}, u32[]{:S(2)}) collective-permute-start(bf16[1,248,128]{2,1,0:T(8,128)(2,1)S(1)} %pack.1.own), channel_id=1, source_target_pairs={{0,16},{4,20},{8,24},{12,28},{16,0},{20,4},{24,8},{28,12},{1,17},{... | collective-permute-start | bytes 190472 | tf_op jit(solution)/shard_map/ppermute | solution.py:94
  7.8 9.7 %collective-permute-start.1 = (bf16[128,512]{1,0:T(8,128)(2,1)S(1)}, bf16[128,512]{1,0:T(8,128)(2,1)S(1)}, u32[]{:S(2)}, u32[]{:S(2)}) collective-permute-start(bf16[128,512]{1,0:T(8,128)(2,1)S(1)} %get-tuple-element.91), channel_id=1, source_target_pairs={{0,4},{4,8},{8,12},{12,16},{16,20},{20,24},{24,28},{28,0},{1,5},{5... | collective-permute-start | bytes 393224 | tf_op jit(solution)/shard_map/ppermute | solution.py:1193
  12.0 7.1 %collective-permute-start.2 = (bf16[2,248,128]{2,1,0:T(8,128)(2,1)S(1)}, bf16[2,248,128]{2,1,0:T(8,128)(2,1)S(1)}, u32[]{:S(2)}, u32[]{:S(2)}) collective-permute-start(bf16[2,248,128]{2,1,0:T(8,128)(2,1)S(1)} %merge.3.own), channel_id=1, source_target_pairs={{0,8},{4,12},{8,0},{12,4},{16,24},{20,28},{24,16},{28,20},{1,9},{5... | collective-permute-start | bytes 380936 | tf_op jit(solution)/shard_map/ppermute | solution.py:94
  12.6 16.4 %collective-permute-start.5 = (bf16[128,512]{1,0:T(8,128)(2,1)S(1)}, bf16[128,512]{1,0:T(8,128)(2,1)S(1)}, u32[]{:S(2)}, u32[]{:S(2)}) collective-permute-start(bf16[128,512]{1,0:T(8,128)(2,1)S(1)} %get-tuple-element.94), channel_id=1, source_target_pairs={{0,16},{4,20},{8,24},{12,28},{16,0},{20,4},{24,8},{28,12},{1,17},{... | collective-permute-start | bytes 393224 | tf_op jit(solution)/shard_map/ppermute | solution.py:1193
  16.0 16.4 %collective-permute-start.4 = (bf16[128,512]{1,0:T(8,128)(2,1)S(1)}, bf16[128,512]{1,0:T(8,128)(2,1)S(1)}, u32[]{:S(2)}, u32[]{:S(2)}) collective-permute-start(bf16[128,512]{1,0:T(8,128)(2,1)S(1)} %get-tuple-element.93), channel_id=1, source_target_pairs={{0,12},{4,16},{8,20},{12,24},{16,28},{20,0},{24,4},{28,8},{1,13},{... | collective-permute-start | bytes 393224 | tf_op jit(solution)/shard_map/ppermute | solution.py:1193
  19.6 16.8 %collective-permute-start.6 = (bf16[4,248,128]{2,1,0:T(8,128)(2,1)S(1)}, bf16[4,248,128]{2,1,0:T(8,128)(2,1)S(1)}, u32[]{:S(2)}, u32[]{:S(2)}) collective-permute-start(bf16[4,248,128]{2,1,0:T(8,128)(2,1)S(1)} %merge.4.own), channel_id=1, source_target_pairs={{0,4},{4,0},{8,12},{12,8},{16,20},{20,16},{24,28},{28,24},{1,5},{5... | collective-permute-start | bytes 761864 | tf_op jit(solution)/shard_map/ppermute | solution.py:94
  21.2 15.2 %collective-permute-start.3 = (bf16[128,512]{1,0:T(8,128)(2,1)S(1)}, bf16[128,512]{1,0:T(8,128)(2,1)S(1)}, u32[]{:S(2)}, u32[]{:S(2)}) collective-permute-start(bf16[128,512]{1,0:T(8,128)(2,1)S(1)} %get-tuple-element.92), channel_id=1, source_target_pairs={{0,8},{4,12},{8,16},{12,20},{16,24},{20,28},{24,0},{28,4},{1,9},{5... | collective-permute-start | bytes 393224 | tf_op jit(solution)/shard_map/ppermute | solution.py:1193
  21.2 15.8 %collective-permute-start.7 = (bf16[128,512]{1,0:T(8,128)(2,1)S(1)}, bf16[128,512]{1,0:T(8,128)(2,1)S(1)}, u32[]{:S(2)}, u32[]{:S(2)}) collective-permute-start(bf16[128,512]{1,0:T(8,128)(2,1)S(1)} %get-tuple-element.104), channel_id=1, source_target_pairs={{0,20},{4,24},{8,28},{12,0},{16,4},{20,8},{24,12},{28,16},{1,21},{... | collective-permute-start | bytes 393224 | tf_op jit(solution)/shard_map/ppermute | solution.py:1193
  29.0 8.0 %collective-permute-start.8 = (bf16[128,512]{1,0:T(8,128)(2,1)S(1)}, bf16[128,512]{1,0:T(8,128)(2,1)S(1)}, u32[]{:S(2)}, u32[]{:S(2)}) collective-permute-start(bf16[128,512]{1,0:T(8,128)(2,1)S(1)} %get-tuple-element.105), channel_id=1, source_target_pairs={{0,24},{4,28},{8,0},{12,4},{16,8},{20,12},{24,16},{28,20},{1,25},{... | collective-permute-start | bytes 393224 | tf_op jit(solution)/shard_map/ppermute | solution.py:1193
  32.4 5.0 %collective-permute-start.9 = (bf16[128,512]{1,0:T(8,128)(2,1)S(1)}, bf16[128,512]{1,0:T(8,128)(2,1)S(1)}, u32[]{:S(2)}, u32[]{:S(2)}) collective-permute-start(bf16[128,512]{1,0:T(8,128)(2,1)S(1)} %get-tuple-element.106), channel_id=1, source_target_pairs={{0,28},{4,0},{8,4},{12,8},{16,12},{20,16},{24,20},{28,24},{1,29},{... | collective-permute-start | bytes 393224 | tf_op jit(solution)/shard_map/ppermute | solution.py:1193
  37.4 34.1 %all-to-all-start.1 = ((bf16[8,128,512]{2,1,0:T(8,128)(2,1)}), bf16[8,128,512]{2,1,0:T(8,128)(2,1)}, u32[]{:S(2)}, u32[]{:S(2)}) async-start(bf16[8,128,512]{2,1,0:T(8,128)(2,1)} %part.3), calls=%async_computation.1 | async-start | bytes 2097152 | tf_op jit(solution)/shard_map/all_to_all | solution.py:1207
  43.4 14.6 %collective-permute-start.14 = (bf16[8,128,128]{2,1,0:T(8,128)(2,1)S(1)}, bf16[8,128,128]{2,1,0:T(8,128)(2,1)S(1)}, u32[]{:S(2)}, u32[]{:S(2)}) collective-permute-start(bf16[8,128,128]{2,1,0:T(8,128)(2,1)S(1)} %slice.4.refs_4_), channel_id=1, source_target_pairs={{0,2},{1,3},{2,0},{3,1},{4,6},{5,7},{6,4},{7,5},{8,10},{9,11},{10,... | collective-permute-start | bytes 786440 | tf_op jit(solution)/shard_map/ppermute | solution.py:94
  51.1 6.9 %collective-permute-start.11 = (bf16[1024,128]{1,0:T(8,128)(2,1)S(1)}, bf16[1024,128]{1,0:T(8,128)(2,1)S(1)}, u32[]{:S(2)}, u32[]{:S(2)}) collective-permute-start(bf16[1024,128]{1,0:T(8,128)(2,1)S(1)} %get-tuple-element.111.refs_0_), channel_id=1, source_target_pairs={{0,2},{1,3},{2,0},{3,1},{4,6},{5,7},{6,4},{7,5},{8,10},{9,11},{10,... | collective-permute-start | bytes 786440 | tf_op jit(solution)/shard_map/ppermute | solution.py:94
  57.4 1.6 %collective-permute-start.10 = (bf16[1024,128]{1,0:T(8,128)(2,1)S(1)}, bf16[1024,128]{1,0:T(8,128)(2,1)S(1)}, u32[]{:S(2)}, u32[]{:S(2)}) collective-permute-start(bf16[1024,128]{1,0:T(8,128)(2,1)S(1)} %get-tuple-element.111.refs_0_), channel_id=1, source_target_pairs={{0,1},{1,0},{2,3},{3,2},{4,5},{5,4},{6,7},{7,6},{8,9},{9,8},{10,11... | collective-permute-start | bytes 786440 | tf_op jit(solution)/shard_map/ppermute | solution.py:94
  57.4 1.9 %collective-permute-start.13 = (bf16[8,128,128]{2,1,0:T(8,128)(2,1)S(1)}, bf16[8,128,128]{2,1,0:T(8,128)(2,1)S(1)}, u32[]{:S(2)}, u32[]{:S(2)}) collective-permute-start(bf16[8,128,128]{2,1,0:T(8,128)(2,1)S(1)} %slice.4.refs_4_), channel_id=1, source_target_pairs={{0,1},{1,0},{2,3},{3,2},{4,5},{5,4},{6,7},{7,6},{8,9},{9,8},{10,11... | collective-permute-start | bytes 786440 | tf_op jit(solution)/shard_map/ppermute | solution.py:94
  57.9 1.8 %collective-permute-start.12 = (bf16[1024,128]{1,0:T(8,128)(2,1)S(1)}, bf16[1024,128]{1,0:T(8,128)(2,1)S(1)}, u32[]{:S(2)}, u32[]{:S(2)}) collective-permute-start(bf16[1024,128]{1,0:T(8,128)(2,1)S(1)} %collective-permute-done.11.refs_2_), channel_id=1, source_target_pairs={{0,1},{1,0},{2,3},{3,2},{4,5},{5,4},{6,7},{7,6},{8,9},{9,8},{10,11... | collective-permute-start | bytes 786440 | tf_op jit(solution)/shard_map/ppermute | solution.py:94
  58.0 2.1 %collective-permute-start.15 = (bf16[8,128,128]{2,1,0:T(8,128)(2,1)S(1)}, bf16[8,128,128]{2,1,0:T(8,128)(2,1)S(1)}, u32[]{:S(2)}, u32[]{:S(2)}) collective-permute-start(bf16[8,128,128]{2,1,0:T(8,128)(2,1)S(1)} %collective-permute-done.14.refs_6_), channel_id=1, source_target_pairs={{0,1},{1,0},{2,3},{3,2},{4,5},{5,4},{6,7},{7,6},{8,9},{9,8},{10,11... | collective-permute-start | bytes 786440 | tf_op jit(solution)/shard_map/ppermute | solution.py:94
  71.5 32.2 %all-to-all-start = ((bf16[8,128,512]{2,1,0:T(8,128)(2,1)}), bf16[8,128,512]{2,1,0:T(8,128)(2,1)S(1)}, u32[]{:S(2)}, u32[]{:S(2)}) async-start(bf16[8,128,512]{2,1,0:T(8,128)(2,1)} %bitcast.32), calls=%async_computation | async-start | bytes 2097152 | tf_op jit(solution)/shard_map/all_to_all | solution.py:1225
  88.6 3.2 %collective-permute-start.16 = (bf16[2,1024,128]{2,1,0:T(8,128)(2,1)S(1)}, bf16[2,1024,128]{2,1,0:T(8,128)(2,1)S(1)}, u32[]{:S(2)}, u32[]{:S(2)}) collective-permute-start(bf16[2,1024,128]{2,1,0:T(8,128)(2,1)S(1)} %get-tuple-element.124), channel_id=1, source_target_pairs={{0,1},{1,0},{2,3},{3,2},{4,5},{5,4},{6,7},{7,6},{8,9},{9,8},{10,11... | collective-permute-start | bytes 1572872 | tf_op jit(solution)/shard_map/ppermute | solution.py:94
  91.2 11.5 %collective-permute-start.18 = (bf16[2,8,128,128]{3,2,1,0:T(8,128)(2,1)S(1)}, bf16[2,8,128,128]{3,2,1,0:T(8,128)(2,1)S(1)}, u32[]{:S(2)}, u32[]{:S(2)}) collective-permute-start(bf16[2,8,128,128]{3,2,1,0:T(8,128)(2,1)S(1)} %get-tuple-element.143), channel_id=1, source_target_pairs={{0,1},{1,0},{2,3},{3,2},{4,5},{5,4},{6,7},{7,6},{8,9},{9,8},{10,11... | collective-permute-start | bytes 1572872 | tf_op jit(solution)/shard_map/ppermute | solution.py:94
  92.6 11.1 %collective-permute-start.17 = (bf16[1,1024,128]{2,1,0:T(8,128)(2,1)S(1)}, bf16[1,1024,128]{2,1,0:T(8,128)(2,1)S(1)}, u32[]{:S(2)}, u32[]{:S(2)}) collective-permute-start(bf16[1,1024,128]{2,1,0:T(8,128)(2,1)S(1)} %get-tuple-element.130), channel_id=1, source_target_pairs={{0,2},{1,3},{2,0},{3,1},{4,6},{5,7},{6,4},{7,5},{8,10},{9,11},{10,... | collective-permute-start | bytes 786440 | tf_op jit(solution)/shard_map/ppermute | solution.py:94
  104.2 32.2 %all-to-all-start.2 = ((bf16[8,128,512]{2,1,0:T(8,128)(2,1)}), bf16[8,128,512]{2,1,0:T(8,128)(2,1)S(1)}, u32[]{:S(2)}, u32[]{:S(2)}) async-start(bf16[8,128,512]{2,1,0:T(8,128)(2,1)} %bitcast.31), calls=%async_computation.2 | async-start | bytes 2097152 | tf_op jit(solution)/shard_map/all_to_all | solution.py:1248
  110.2 10.8 %collective-permute-start.19 = (bf16[1,8,128,128]{3,2,1,0:T(8,128)(2,1)}, bf16[1,8,128,128]{3,2,1,0:T(8,128)(2,1)S(1)}, u32[]{:S(2)}, u32[]{:S(2)}) collective-permute-start(bf16[1,8,128,128]{3,2,1,0:T(8,128)(2,1)} %copy-done.6), channel_id=1, source_target_pairs={{0,2},{1,3},{2,0},{3,1},{4,6},{5,7},{6,4},{7,5},{8,10},{9,11},{10,... | collective-permute-start | bytes 786440 | tf_op jit(solution)/shard_map/ppermute | solution.py:94
  119.1 4.6 %collective-permute-start.23 = (f32[24,128]{1,0:T(8,128)S(1)}, f32[24,128]{1,0:T(8,128)S(1)}, u32[]{:S(2)}, u32[]{:S(2)}) collective-permute-start(f32[24,128]{1,0:T(8,128)S(1)} %get-tuple-element.151), channel_id=1, source_target_pairs={{0,3},{1,2},{2,1},{3,0},{4,7},{5,6},{6,5},{7,4},{8,11},{9,10},{10,... | collective-permute-start | bytes 36872 | tf_op jit(solution)/shard_map/ppermute | solution.py:1255
  119.4 4.3 %collective-permute-start.22 = (f32[24,128]{1,0:T(8,128)S(1)}, f32[24,128]{1,0:T(8,128)S(1)}, u32[]{:S(2)}, u32[]{:S(2)}) collective-permute-start(f32[24,128]{1,0:T(8,128)S(1)} %get-tuple-element.151), channel_id=1, source_target_pairs={{0,2},{1,3},{2,0},{3,1},{4,6},{5,7},{6,4},{7,5},{8,10},{9,11},{10,... | collective-permute-start | bytes 36872 | tf_op jit(solution)/shard_map/ppermute | solution.py:1255
  120.7 3.0 %collective-permute-start.21 = (f32[24,128]{1,0:T(8,128)S(1)}, f32[24,128]{1,0:T(8,128)S(1)}, u32[]{:S(2)}, u32[]{:S(2)}) collective-permute-start(f32[24,128]{1,0:T(8,128)S(1)} %get-tuple-element.151), channel_id=1, source_target_pairs={{0,1},{1,0},{2,3},{3,2},{4,5},{5,4},{6,7},{7,6},{8,9},{9,8},{10,11... | collective-permute-start | bytes 36872 | tf_op jit(solution)/shard_map/ppermute | solution.py:1255
  121.6 9.7 %collective-permute-start.20 = (bf16[4,160,128]{2,1,0:T(8,128)(2,1)S(1)}, bf16[4,160,128]{2,1,0:T(8,128)(2,1)S(1)}, u32[]{:S(2)}, u32[]{:S(2)}) collective-permute-start(bf16[4,160,128]{2,1,0:T(8,128)(2,1)S(1)} %get-tuple-element.150), channel_id=1, source_target_pairs={{0,4},{4,0},{8,12},{12,8},{16,20},{20,16},{24,28},{28,24},{1,5},{5... | collective-permute-start | bytes 491528 | tf_op jit(solution)/shard_map/ppermute | solution.py:94
  123.7 7.6 %collective-permute-start.24 = (f32[24,128]{1,0:T(8,128)S(1)}, f32[24,128]{1,0:T(8,128)S(1)}, u32[]{:S(2)}, u32[]{:S(2)}) collective-permute-start(f32[24,128]{1,0:T(8,128)S(1)} %add_add_fusion.refs_0_), channel_id=1, source_target_pairs={{0,4},{4,0},{8,12},{12,8},{16,20},{20,16},{24,28},{28,24},{1,5},{5... | collective-permute-start | bytes 36872 | tf_op jit(solution)/shard_map/ppermute | solution.py:94
  132.0 6.6 %collective-permute-start.25 = (bf16[192,128]{1,0:T(8,128)(2,1)S(1)}, bf16[192,128]{1,0:T(8,128)(2,1)S(1)}, u32[]{:S(2)}, u32[]{:S(2)}) collective-permute-start(bf16[192,128]{1,0:T(8,128)(2,1)S(1)} %get-tuple-element.155), channel_id=1, source_target_pairs={{0,8},{4,12},{8,0},{12,4},{16,24},{20,28},{24,16},{28,20},{1,9},{5... | collective-permute-start | bytes 147464 | tf_op jit(solution)/shard_map/ppermute | solution.py:94
  132.9 5.8 %collective-permute-start.26 = (bf16[192,128]{1,0:T(8,128)(2,1)S(1)}, bf16[192,128]{1,0:T(8,128)(2,1)S(1)}, u32[]{:S(2)}, u32[]{:S(2)}) collective-permute-start(bf16[192,128]{1,0:T(8,128)(2,1)S(1)} %get-tuple-element.156), channel_id=1, source_target_pairs={{0,16},{4,20},{8,24},{12,28},{16,0},{20,4},{24,8},{28,12},{1,17},{... | collective-permute-start | bytes 147464 | tf_op jit(solution)/shard_map/ppermute | solution.py:94
  135.1 5.9 %collective-permute-start.27 = (bf16[192,128]{1,0:T(8,128)(2,1)S(1)}, bf16[192,128]{1,0:T(8,128)(2,1)S(1)}, u32[]{:S(2)}, u32[]{:S(2)}) collective-permute-start(bf16[192,128]{1,0:T(8,128)(2,1)S(1)} %get-tuple-element.157), channel_id=1, source_target_pairs={{0,24},{4,28},{8,16},{12,20},{16,8},{20,12},{24,0},{28,4},{1,25},{... | collective-permute-start | bytes 147464 | tf_op jit(solution)/shard_map/ppermute | solution.py:94
  (6 other events, 213.3 us)

commit v3 on v2

--- a/solution.py
+++ b/solution.py
@@ -1251,6 +1251,7 @@
     )
     out = weave(scalars, after(out_back, kept))
     kept, sent = join(scalars, kept, sent, *w_two)
+    vec_sum = after(vec_sum, sent)
     others = [
         lax.ppermute(vec_sum, "tensor", [(k, k ^ e) for k in range(n_t)]) for e in range(1, n_t)
     ]

time: 143 us -> 143 us (level)
  transfers between devices with their start and end apart: 31 -> 31, of which waited for: 13 -> 14; matrix products, arithmetic and copies ran while one was open for 0% -> 0% of each run, Pallas kernels for 46% -> 46%
where the time goes in v3:
time: 143 us
  Pallas kernels  69.8 us (49%)
  starting transfers between devices  53.2 us (37%)
  waiting for transfers between devices  18 us (13%)
    ppermute x18, starting transfers between devices, flip_bit(): return lax.ppermute(value, axis, [(k, k ^ bit) for k in range(size)])  20.6 us
    ppermute x7, starting transfers between devices, send(): tok_pieces[s] = lax.ppermute(piece, 'dp', pairs)  12.6 us
    pallas_call x1, Pallas kernels, forward(): pl.pallas_call(partial(forward_kernel, n, n_t, blocks, block), out_shape=...  11.4 us
    ppermute x18, waiting for transfers between devices, flip_bit(): return lax.ppermute(value, axis, [(k, k ^ bit) for k in range(size)])  11.1 us
    pallas_call x1, Pallas kernels, mix_back(): pl.pallas_call(partial(mix_back_kernel, n, n_t, blocks, block), out_shape...  11 us
    pallas_call x1, Pallas kernels, norm_back(): pl.pallas_call(partial(norm_back_kernel, blocks, block), out_shape=[hbm((...  8.57 us
    pallas_call x1, Pallas kernels, taps_back(): pl.pallas_call(partial(taps_back_kernel, n, states), out_shape=[jax.Shape...  8.34 us
    ppermute x7, waiting for transfers between devices, send(): tok_pieces[s] = lax.ppermute(piece, 'dp', pairs)  6.63 us
  transfers between devices with their start and end apart: 31, of which 14 were waited for; matrix products, arithmetic and copies ran while one was open for 0% of the time, Pallas kernels for 46%

profile of v3, /device:TPU:0, one launch (start us, length us, event | category | flops | bytes accessed | tf_op | source)
XLA Modules:
  0.0 142.8 jit_solution(6186703415118234072)
XLA Ops:
  0.7 2.0 %part.2 = (bf16[128,512]{1,0:T(8,128)(2,1)S(1)}, bf16[128,512]{1,0:T(8,128)(2,1)S(1)}, bf16[128,512]{1,0:T(8,128)(2,1)S(1)}, bf16[128,512]{1,0:T(8,128)(2,1)S(1)...) custom-call(s32[2]{0:T(128)S(1)} %pad_add_fusion.sc, ...), custom_call_target="tpu_custom_call" | custom-call | bytes 30000 | tf_op jit(solution)/shard_map/part/pallas_call | solution.py:1115
  3.7 4.1 %collective-permute-start = (bf16[1,248,128]{2,1,0:T(8,128)(2,1)S(1)}, bf16[1,248,128]{2,1,0:T(8,128)(2,1)S(1)}, u32[]{:S(2)}, u32[]{:S(2)}) collective-permute-start(bf16[1,248,128]{2,1,0:T(8,128)(2,1)S(1)} %pack.1.own), channel_id=1, source_target_pairs={{0,16},{4,20},{8,24},{12,28},{16,0},{20,4},{24,8},{28,12},{1,17},{... | collective-permute-start | bytes 190472 | tf_op jit(solution)/shard_map/ppermute | solution.py:94
  7.8 1.5 %collective-permute-start.1 = (bf16[128,512]{1,0:T(8,128)(2,1)S(1)}, bf16[128,512]{1,0:T(8,128)(2,1)S(1)}, u32[]{:S(2)}, u32[]{:S(2)}) collective-permute-start(bf16[128,512]{1,0:T(8,128)(2,1)S(1)} %get-tuple-element.92), channel_id=1, source_target_pairs={{0,4},{4,8},{8,12},{12,16},{16,20},{20,24},{24,28},{28,0},{1,5},{5... | collective-permute-start | bytes 393224 | tf_op jit(solution)/shard_map/ppermute | solution.py:1193
  9.3 2.1 %collective-permute-done.got = bf16[1,248,128]{2,1,0:T(8,128)(2,1)S(1)} collective-permute-done((bf16[1,248,128]{2,1,0:T(8,128)(2,1)S(1)}, bf16[1,248,128]{2,1,0:T(8,128)(2,1)S(1)}, u32[]{:S(2)}, u32[]{:S(2)}) %collective-permute-start) | collective-permute-done | bytes 63520 | tf_op jit(solution)/shard_map/ppermute | solution.py:94
  12.6 3.4 %collective-permute-start.5 = (bf16[128,512]{1,0:T(8,128)(2,1)S(1)}, bf16[128,512]{1,0:T(8,128)(2,1)S(1)}, u32[]{:S(2)}, u32[]{:S(2)}) collective-permute-start(bf16[128,512]{1,0:T(8,128)(2,1)S(1)} %get-tuple-element.95), channel_id=1, source_target_pairs={{0,16},{4,20},{8,24},{12,28},{16,0},{20,4},{24,8},{28,12},{1,17},{... | collective-permute-start | bytes 393224 | tf_op jit(solution)/shard_map/ppermute | solution.py:1193
  16.0 1.5 %collective-permute-start.4 = (bf16[128,512]{1,0:T(8,128)(2,1)S(1)}, bf16[128,512]{1,0:T(8,128)(2,1)S(1)}, u32[]{:S(2)}, u32[]{:S(2)}) collective-permute-start(bf16[128,512]{1,0:T(8,128)(2,1)S(1)} %get-tuple-element.94), channel_id=1, source_target_pairs={{0,12},{4,16},{8,20},{12,24},{16,28},{20,0},{24,4},{28,8},{1,13},{... | collective-permute-start | bytes 393224 | tf_op jit(solution)/shard_map/ppermute | solution.py:1193
  17.5 1.6 %collective-permute-done.2.got = bf16[2,248,128]{2,1,0:T(8,128)(2,1)S(1)} collective-permute-done((bf16[2,248,128]{2,1,0:T(8,128)(2,1)S(1)}, bf16[2,248,128]{2,1,0:T(8,128)(2,1)S(1)}, u32[]{:S(2)}, u32[]{:S(2)}) %collective-permute-start.2) | collective-permute-done | bytes 127008 | tf_op jit(solution)/shard_map/ppermute | solution.py:94
  19.6 1.5 %collective-permute-start.6 = (bf16[4,248,128]{2,1,0:T(8,128)(2,1)S(1)}, bf16[4,248,128]{2,1,0:T(8,128)(2,1)S(1)}, u32[]{:S(2)}, u32[]{:S(2)}) collective-permute-start(bf16[4,248,128]{2,1,0:T(8,128)(2,1)S(1)} %merge.4.own), channel_id=1, source_target_pairs={{0,4},{4,0},{8,12},{12,8},{16,20},{20,16},{24,28},{28,24},{1,5},{5... | collective-permute-start | bytes 761864 | tf_op jit(solution)/shard_map/ppermute | solution.py:94
  21.2 5.0 %collective-permute-start.7 = (bf16[128,512]{1,0:T(8,128)(2,1)S(1)}, bf16[128,512]{1,0:T(8,128)(2,1)S(1)}, u32[]{:S(2)}, u32[]{:S(2)}) collective-permute-start(bf16[128,512]{1,0:T(8,128)(2,1)S(1)} %get-tuple-element.105), channel_id=1, source_target_pairs={{0,20},{4,24},{8,28},{12,0},{16,4},{20,8},{24,12},{28,16},{1,21},{... | collective-permute-start | bytes 393224 | tf_op jit(solution)/shard_map/ppermute | solution.py:1193
  26.2 2.8 %collective-permute-done.5.refs_4_ = bf16[128,512]{1,0:T(8,128)(2,1)S(1)} collective-permute-done((bf16[128,512]{1,0:T(8,128)(2,1)S(1)}, bf16[128,512]{1,0:T(8,128)(2,1)S(1)}, u32[]{:S(2)}, u32[]{:S(2)}) %collective-permute-start.5) | collective-permute-done | bytes 131104 | tf_op jit(solution)/shard_map/ppermute | solution.py:1193
  29.0 3.4 %collective-permute-done.4.refs_3_ = bf16[128,512]{1,0:T(8,128)(2,1)S(1)} collective-permute-done((bf16[128,512]{1,0:T(8,128)(2,1)S(1)}, bf16[128,512]{1,0:T(8,128)(2,1)S(1)}, u32[]{:S(2)}, u32[]{:S(2)}) %collective-permute-start.4) | collective-permute-done | bytes 131104 | tf_op jit(solution)/shard_map/ppermute | solution.py:1193
  33.7 2.8 %part.3 = bf16[8,128,512]{2,1,0:T(8,128)(2,1)} custom-call(s32[2]{0:T(128)S(1)} %pad_add_fusion.sc, bf16[128,8,512]{2,1,0:T(8,128)(2,1)} %whole.3), custom_call_target="tpu_custom_call" | custom-call | bytes 30000 | tf_op jit(solution)/shard_map/part/pallas_call | solution.py:1115
  37.4 6.0 %all-to-all-start.1 = ((bf16[8,128,512]{2,1,0:T(8,128)(2,1)}), bf16[8,128,512]{2,1,0:T(8,128)(2,1)}, u32[]{:S(2)}, u32[]{:S(2)}) async-start(bf16[8,128,512]{2,1,0:T(8,128)(2,1)} %part.3), calls=%async_computation.1 | async-start | bytes 2097152 | tf_op jit(solution)/shard_map/all_to_all | solution.py:1207
  43.4 1.6 %collective-permute-start.14 = (bf16[8,128,128]{2,1,0:T(8,128)(2,1)S(1)}, bf16[8,128,128]{2,1,0:T(8,128)(2,1)S(1)}, u32[]{:S(2)}, u32[]{:S(2)}) collective-permute-start(bf16[8,128,128]{2,1,0:T(8,128)(2,1)S(1)} %slice.4.refs_4_), channel_id=1, source_target_pairs={{0,2},{1,3},{2,0},{3,1},{4,6},{5,7},{6,4},{7,5},{8,10},{9,11},{10,... | collective-permute-start | bytes 786440 | tf_op jit(solution)/shard_map/ppermute | solution.py:94
  44.9 6.1 %taps.1 = (bf16[1024,128]{1,0:T(8,128)(2,1)S(1)}, f32[4,64,128]{2,1,0:T(8,128)S(1)}, f32[8,512]{1,0:T(8,128)S(1)}, f32[1,1024]{1,0:T(1,128)S(1)}) custom-call(s32[2]{0:T(128)S(1)} %pad_add_fusion.sc, bf16[8,248,128]{2,1,0:T(8,128)(2,1)S(1)} %merge.5.blob), custom_call_target="tpu_custom_call" | custom-call | bytes 70000 | tf_op jit(solution)/shard_map/taps/pallas_call | solution.py:251
  51.7 5.7 %enter.1 = (bf16[1024,512]{1,0:T(8,128)(2,1)S(1)}, bf16[1024,512]{1,0:T(8,128)(2,1)S(1)}, f32[4,512,512]{2,1,0:T(8,128)S(1)}, bf16[1024,512]{1,0:T(8,128)(2,1)},...) custom-call(s32[2]{0:T(128)S(1)} %pad_add_fusion.sc, f32[8,512]{1,0:T(8,128)S(1)} %get-tuple-element.103.vec, ...), custom_call_target="tpu_custom_call" | custom-call | bytes 70000 | tf_op jit(solution)/shard_map/enter/pallas_call | solution.py:472
  60.1 11.4 %forward.1 = (bf16[1024,512]{1,0:T(8,128)(2,1)}, bf16[4,512,512]{2,1,0:T(8,128)(2,1)}, bf16[512,1024]{1,0:T(8,128)(2,1)}, bf16[1024,512]{1,0:T(8,128)(2,1)}, bf1...) custom-call(s32[2]{0:T(128)S(1)} %pad_add_fusion.sc, s32[32]{0:T(128)S(1)} %copy-done.5, ...), custom_call_target="tpu_custom_call" | custom-call | bytes 150000 | tf_op jit(solution)/shard_map/forward/pallas_call | solution.py:622
  71.5 6.1 %all-to-all-start = ((bf16[8,128,512]{2,1,0:T(8,128)(2,1)}), bf16[8,128,512]{2,1,0:T(8,128)(2,1)S(1)}, u32[]{:S(2)}, u32[]{:S(2)}) async-start(bf16[8,128,512]{2,1,0:T(8,128)(2,1)} %bitcast.32), calls=%async_computation | async-start | bytes 2097152 | tf_op jit(solution)/shard_map/all_to_all | solution.py:1225
  77.6 11.0 %mix_back.1 = (bf16[2,1024,128]{2,1,0:T(8,128)(2,1)S(1)}, bf16[2,1024,128]{2,1,0:T(8,128)(2,1)S(1)}, bf16[1024,1024]{1,0:T(8,128)(2,1)S(1)}, bf16[1024,512]{1,0:...) custom-call(s32[2]{0:T(128)S(1)} %pad_add_fusion.sc, s32[32]{0:T(128)S(1)} %copy-done.5, ...), custom_call_target="tpu_custom_call" | custom-call | bytes 120000 | tf_op jit(solution)/shard_map/mix_back/pallas_call | solution.py:778
  88.7 2.5 %weight_back.1 = (bf16[2,8,128,128]{3,2,1,0:T(8,128)(2,1)S(1)}, bf16[2,8,128,128]{3,2,1,0:T(8,128)(2,1)S(1)}) custom-call(s32[2]{0:T(128)S(1)} %pad_add_fusion.sc, bf16[1024,512]{1,0:T(8,128)(2,1)S(1)} %copy-done.2, bf16[1024,1024]{1,0:T(8,128)(2,1)S(1)} %get-tuple-element.127.grad_pre), custom_call_target="tpu_custom_call" | custom-call | bytes 30000 | tf_op jit(solution)/shard_map/weight_back/pallas_call | solution.py:841
  92.6 1.5 %collective-permute-start.17 = (bf16[1,1024,128]{2,1,0:T(8,128)(2,1)S(1)}, bf16[1,1024,128]{2,1,0:T(8,128)(2,1)S(1)}, u32[]{:S(2)}, u32[]{:S(2)}) collective-permute-start(bf16[1,1024,128]{2,1,0:T(8,128)(2,1)S(1)} %get-tuple-element.131), channel_id=1, source_target_pairs={{0,2},{1,3},{2,0},{3,1},{4,6},{5,7},{6,4},{7,5},{8,10},{9,11},{10,... | collective-permute-start | bytes 786440 | tf_op jit(solution)/shard_map/ppermute | solution.py:94
  94.1 8.6 %norm_back.1 = (bf16[1024,512]{1,0:T(8,128)(2,1)}, f32[8,512]{1,0:T(8,128)S(1)}, f32[8,512]{1,0:T(8,128)S(1)}) custom-call(s32[2]{0:T(128)S(1)} %pad_add_fusion.sc, f32[8,512]{1,0:T(8,128)S(1)} %get-tuple-element.103.vec, bf16[256,512]{1,0:T(8,128)(2,1)S(1)} %copy-done, f32[4,512,512]{2,1,0:T(8,128)S(1)} %get-tuple-element.133.spec_g, ...), custom_call_target="tpu_custom_call" | custom-call | bytes 100000 | tf_op jit(solution)/shard_map/norm_back/pallas_call | solution.py:953
  104.2 6.0 %all-to-all-start.2 = ((bf16[8,128,512]{2,1,0:T(8,128)(2,1)}), bf16[8,128,512]{2,1,0:T(8,128)(2,1)S(1)}, u32[]{:S(2)}, u32[]{:S(2)}) async-start(bf16[8,128,512]{2,1,0:T(8,128)(2,1)} %bitcast.31), calls=%async_computation.2 | async-start | bytes 2097152 | tf_op jit(solution)/shard_map/all_to_all | solution.py:1248
  110.7 8.3 %taps_back.1 = (bf16[4,160,128]{2,1,0:T(8,128)(2,1)S(1)}, bf16[4,160,128]{2,1,0:T(8,128)(2,1)S(1)}, f32[24,128]{1,0:T(8,128)S(1)}) custom-call(s32[2]{0:T(128)S(1)} %pad_add_fusion.sc, f32[4,64,128]{2,1,0:T(8,128)S(1)} %get-tuple-element.117.par, f32[8,512]{1,0:T(8,128)S(1)} %get-tuple-element.103.vec, bf16[1024,128]{1,0:T(8,128)(2,1)S(1)} %bitcast.29, ...), custom_call_target="tpu_custom_call" | custom-call | bytes 100000 | tf_op jit(solution)/shard_map/taps_back/pallas_call | solution.py:365
  121.6 2.0 %collective-permute-start.20 = (bf16[4,160,128]{2,1,0:T(8,128)(2,1)S(1)}, bf16[4,160,128]{2,1,0:T(8,128)(2,1)S(1)}, u32[]{:S(2)}, u32[]{:S(2)}) collective-permute-start(bf16[4,160,128]{2,1,0:T(8,128)(2,1)S(1)} %get-tuple-element.151), channel_id=1, source_target_pairs={{0,4},{4,0},{8,12},{12,8},{16,20},{20,16},{24,28},{28,24},{1,5},{5... | collective-permute-start | bytes 491528 | tf_op jit(solution)/shard_map/ppermute | solution.py:94
  123.8 1.9 %collective-permute-start.24 = (f32[24,128]{1,0:T(8,128)S(1)}, f32[24,128]{1,0:T(8,128)S(1)}, u32[]{:S(2)}, u32[]{:S(2)}) collective-permute-start(f32[24,128]{1,0:T(8,128)S(1)} %add_add_fusion.refs_0_), channel_id=1, source_target_pairs={{0,4},{4,0},{8,12},{12,8},{16,20},{20,16},{24,28},{28,24},{1,5},{5... | collective-permute-start | bytes 36872 | tf_op jit(solution)/shard_map/ppermute | solution.py:94
  125.7 2.2 %weave.2 = bf16[128,8,512]{2,1,0:T(8,128)(2,1)} custom-call(s32[2]{0:T(128)S(1)} %pad_add_fusion.sc, bf16[8,128,512]{2,1,0:T(8,128)(2,1)S(1)} %all-to-all-done.refs_0_), custom_call_target="tpu_custom_call" | custom-call | bytes 30000 | tf_op jit(solution)/shard_map/weave/pallas_call | solution.py:1069
  127.8 3.5 %collective-permute-done.24.refs_1_ = f32[24,128]{1,0:T(8,128)S(1)} collective-permute-done((f32[24,128]{1,0:T(8,128)S(1)}, f32[24,128]{1,0:T(8,128)S(1)}, u32[]{:S(2)}, u32[]{:S(2)}) %collective-permute-start.24) | collective-permute-done | bytes 12320 | tf_op jit(solution)/shard_map/ppermute | solution.py:94
  132.8 2.2 %collective-permute-start.26 = (bf16[192,128]{1,0:T(8,128)(2,1)S(1)}, bf16[192,128]{1,0:T(8,128)(2,1)S(1)}, u32[]{:S(2)}, u32[]{:S(2)}) collective-permute-start(bf16[192,128]{1,0:T(8,128)(2,1)S(1)} %get-tuple-element.158), channel_id=1, source_target_pairs={{0,16},{4,20},{8,24},{12,28},{16,0},{20,4},{24,8},{28,12},{1,17},{... | collective-permute-start | bytes 147464 | tf_op jit(solution)/shard_map/ppermute | solution.py:94
  136.4 2.2 %weave.3 = bf16[128,8,512]{2,1,0:T(8,128)(2,1)} custom-call(s32[2]{0:T(128)S(1)} %pad_add_fusion.sc, bf16[8,128,512]{2,1,0:T(8,128)(2,1)S(1)} %all-to-all-done.2.refs_0_), custom_call_target="tpu_custom_call" | custom-call | bytes 30000 | tf_op jit(solution)/shard_map/weave/pallas_call | solution.py:1069
  138.6 2.3 %collective-permute-done.27.refs_3_ = bf16[192,128]{1,0:T(8,128)(2,1)S(1)} collective-permute-done((bf16[192,128]{1,0:T(8,128)(2,1)S(1)}, bf16[192,128]{1,0:T(8,128)(2,1)S(1)}, u32[]{:S(2)}, u32[]{:S(2)}) %collective-permute-start.27) | collective-permute-done | bytes 49184 | tf_op jit(solution)/shard_map/ppermute | solution.py:94
  140.9 1.7 %totals.1 = (f32[128,128]{1,0:T(8,128)}, f32[8,128]{1,0:T(8,128)}, f32[8,128]{1,0:T(8,128)}, f32[8,128]{1,0:T(8,128)}, f32[8,128]{1,0:T(8,128)}, /*index=5*/f32[...) custom-call(s32[2]{0:T(128)S(1)} %pad_add_fusion.sc, ...), custom_call_target="tpu_custom_call" | custom-call | bytes 10000 | tf_op jit(solution)/shard_map/totals/pallas_call | solution.py:1153
  (67 shorter events, 17.3 us)
Async XLA Ops:
  0.6 51.0 %copy-start.1 = (bf16[512,256]{1,0:T(8,128)(2,1)S(1)}, bf16[512,256]{1,0:T(8,128)(2,1)}, u32[]{:S(2)}) copy-start(bf16[512,256]{1,0:T(8,128)(2,1)} %constant.17.clone.basis_ref) | copy-start | bytes 786436
  3.7 7.7 %collective-permute-start = (bf16[1,248,128]{2,1,0:T(8,128)(2,1)S(1)}, bf16[1,248,128]{2,1,0:T(8,128)(2,1)S(1)}, u32[]{:S(2)}, u32[]{:S(2)}) collective-permute-start(bf16[1,248,128]{2,1,0:T(8,128)(2,1)S(1)} %pack.1.own), channel_id=1, source_target_pairs={{0,16},{4,20},{8,24},{12,28},{16,0},{20,4},{24,8},{28,12},{1,17},{... | collective-permute-start | bytes 190472 | tf_op jit(solution)/shard_map/ppermute | solution.py:94
  7.8 9.7 %collective-permute-start.1 = (bf16[128,512]{1,0:T(8,128)(2,1)S(1)}, bf16[128,512]{1,0:T(8,128)(2,1)S(1)}, u32[]{:S(2)}, u32[]{:S(2)}) collective-permute-start(bf16[128,512]{1,0:T(8,128)(2,1)S(1)} %get-tuple-element.92), channel_id=1, source_target_pairs={{0,4},{4,8},{8,12},{12,16},{16,20},{20,24},{24,28},{28,0},{1,5},{5... | collective-permute-start | bytes 393224 | tf_op jit(solution)/shard_map/ppermute | solution.py:1193
  12.0 7.1 %collective-permute-start.2 = (bf16[2,248,128]{2,1,0:T(8,128)(2,1)S(1)}, bf16[2,248,128]{2,1,0:T(8,128)(2,1)S(1)}, u32[]{:S(2)}, u32[]{:S(2)}) collective-permute-start(bf16[2,248,128]{2,1,0:T(8,128)(2,1)S(1)} %merge.3.own), channel_id=1, source_target_pairs={{0,8},{4,12},{8,0},{12,4},{16,24},{20,28},{24,16},{28,20},{1,9},{5... | collective-permute-start | bytes 380936 | tf_op jit(solution)/shard_map/ppermute | solution.py:94
  12.6 16.4 %collective-permute-start.5 = (bf16[128,512]{1,0:T(8,128)(2,1)S(1)}, bf16[128,512]{1,0:T(8,128)(2,1)S(1)}, u32[]{:S(2)}, u32[]{:S(2)}) collective-permute-start(bf16[128,512]{1,0:T(8,128)(2,1)S(1)} %get-tuple-element.95), channel_id=1, source_target_pairs={{0,16},{4,20},{8,24},{12,28},{16,0},{20,4},{24,8},{28,12},{1,17},{... | collective-permute-start | bytes 393224 | tf_op jit(solution)/shard_map/ppermute | solution.py:1193
  16.0 16.4 %collective-permute-start.4 = (bf16[128,512]{1,0:T(8,128)(2,1)S(1)}, bf16[128,512]{1,0:T(8,128)(2,1)S(1)}, u32[]{:S(2)}, u32[]{:S(2)}) collective-permute-start(bf16[128,512]{1,0:T(8,128)(2,1)S(1)} %get-tuple-element.94), channel_id=1, source_target_pairs={{0,12},{4,16},{8,20},{12,24},{16,28},{20,0},{24,4},{28,8},{1,13},{... | collective-permute-start | bytes 393224 | tf_op jit(solution)/shard_map/ppermute | solution.py:1193
  19.6 16.8 %collective-permute-start.6 = (bf16[4,248,128]{2,1,0:T(8,128)(2,1)S(1)}, bf16[4,248,128]{2,1,0:T(8,128)(2,1)S(1)}, u32[]{:S(2)}, u32[]{:S(2)}) collective-permute-start(bf16[4,248,128]{2,1,0:T(8,128)(2,1)S(1)} %merge.4.own), channel_id=1, source_target_pairs={{0,4},{4,0},{8,12},{12,8},{16,20},{20,16},{24,28},{28,24},{1,5},{5... | collective-permute-start | bytes 761864 | tf_op jit(solution)/shard_map/ppermute | solution.py:94
  21.2 15.2 %collective-permute-start.3 = (bf16[128,512]{1,0:T(8,128)(2,1)S(1)}, bf16[128,512]{1,0:T(8,128)(2,1)S(1)}, u32[]{:S(2)}, u32[]{:S(2)}) collective-permute-start(bf16[128,512]{1,0:T(8,128)(2,1)S(1)} %get-tuple-element.93), channel_id=1, source_target_pairs={{0,8},{4,12},{8,16},{12,20},{16,24},{20,28},{24,0},{28,4},{1,9},{5... | collective-permute-start | bytes 393224 | tf_op jit(solution)/shard_map/ppermute | solution.py:1193
  21.2 15.8 %collective-permute-start.7 = (bf16[128,512]{1,0:T(8,128)(2,1)S(1)}, bf16[128,512]{1,0:T(8,128)(2,1)S(1)}, u32[]{:S(2)}, u32[]{:S(2)}) collective-permute-start(bf16[128,512]{1,0:T(8,128)(2,1)S(1)} %get-tuple-element.105), channel_id=1, source_target_pairs={{0,20},{4,24},{8,28},{12,0},{16,4},{20,8},{24,12},{28,16},{1,21},{... | collective-permute-start | bytes 393224 | tf_op jit(solution)/shard_map/ppermute | solution.py:1193
  29.0 8.0 %collective-permute-start.8 = (bf16[128,512]{1,0:T(8,128)(2,1)S(1)}, bf16[128,512]{1,0:T(8,128)(2,1)S(1)}, u32[]{:S(2)}, u32[]{:S(2)}) collective-permute-start(bf16[128,512]{1,0:T(8,128)(2,1)S(1)} %get-tuple-element.106), channel_id=1, source_target_pairs={{0,24},{4,28},{8,0},{12,4},{16,8},{20,12},{24,16},{28,20},{1,25},{... | collective-permute-start | bytes 393224 | tf_op jit(solution)/shard_map/ppermute | solution.py:1193
  32.4 5.0 %collective-permute-start.9 = (bf16[128,512]{1,0:T(8,128)(2,1)S(1)}, bf16[128,512]{1,0:T(8,128)(2,1)S(1)}, u32[]{:S(2)}, u32[]{:S(2)}) collective-permute-start(bf16[128,512]{1,0:T(8,128)(2,1)S(1)} %get-tuple-element.107), channel_id=1, source_target_pairs={{0,28},{4,0},{8,4},{12,8},{16,12},{20,16},{24,20},{28,24},{1,29},{... | collective-permute-start | bytes 393224 | tf_op jit(solution)/shard_map/ppermute | solution.py:1193
  37.4 34.1 %all-to-all-start.1 = ((bf16[8,128,512]{2,1,0:T(8,128)(2,1)}), bf16[8,128,512]{2,1,0:T(8,128)(2,1)}, u32[]{:S(2)}, u32[]{:S(2)}) async-start(bf16[8,128,512]{2,1,0:T(8,128)(2,1)} %part.3), calls=%async_computation.1 | async-start | bytes 2097152 | tf_op jit(solution)/shard_map/all_to_all | solution.py:1207
  43.4 14.6 %collective-permute-start.14 = (bf16[8,128,128]{2,1,0:T(8,128)(2,1)S(1)}, bf16[8,128,128]{2,1,0:T(8,128)(2,1)S(1)}, u32[]{:S(2)}, u32[]{:S(2)}) collective-permute-start(bf16[8,128,128]{2,1,0:T(8,128)(2,1)S(1)} %slice.4.refs_4_), channel_id=1, source_target_pairs={{0,2},{1,3},{2,0},{3,1},{4,6},{5,7},{6,4},{7,5},{8,10},{9,11},{10,... | collective-permute-start | bytes 786440 | tf_op jit(solution)/shard_map/ppermute | solution.py:94
  51.1 6.9 %collective-permute-start.11 = (bf16[1024,128]{1,0:T(8,128)(2,1)S(1)}, bf16[1024,128]{1,0:T(8,128)(2,1)S(1)}, u32[]{:S(2)}, u32[]{:S(2)}) collective-permute-start(bf16[1024,128]{1,0:T(8,128)(2,1)S(1)} %get-tuple-element.112.refs_0_), channel_id=1, source_target_pairs={{0,2},{1,3},{2,0},{3,1},{4,6},{5,7},{6,4},{7,5},{8,10},{9,11},{10,... | collective-permute-start | bytes 786440 | tf_op jit(solution)/shard_map/ppermute | solution.py:94
  57.4 1.6 %collective-permute-start.10 = (bf16[1024,128]{1,0:T(8,128)(2,1)S(1)}, bf16[1024,128]{1,0:T(8,128)(2,1)S(1)}, u32[]{:S(2)}, u32[]{:S(2)}) collective-permute-start(bf16[1024,128]{1,0:T(8,128)(2,1)S(1)} %get-tuple-element.112.refs_0_), channel_id=1, source_target_pairs={{0,1},{1,0},{2,3},{3,2},{4,5},{5,4},{6,7},{7,6},{8,9},{9,8},{10,11... | collective-permute-start | bytes 786440 | tf_op jit(solution)/shard_map/ppermute | solution.py:94
  57.4 1.9 %collective-permute-start.13 = (bf16[8,128,128]{2,1,0:T(8,128)(2,1)S(1)}, bf16[8,128,128]{2,1,0:T(8,128)(2,1)S(1)}, u32[]{:S(2)}, u32[]{:S(2)}) collective-permute-start(bf16[8,128,128]{2,1,0:T(8,128)(2,1)S(1)} %slice.4.refs_4_), channel_id=1, source_target_pairs={{0,1},{1,0},{2,3},{3,2},{4,5},{5,4},{6,7},{7,6},{8,9},{9,8},{10,11... | collective-permute-start | bytes 786440 | tf_op jit(solution)/shard_map/ppermute | solution.py:94
  57.9 1.8 %collective-permute-start.12 = (bf16[1024,128]{1,0:T(8,128)(2,1)S(1)}, bf16[1024,128]{1,0:T(8,128)(2,1)S(1)}, u32[]{:S(2)}, u32[]{:S(2)}) collective-permute-start(bf16[1024,128]{1,0:T(8,128)(2,1)S(1)} %collective-permute-done.11.refs_2_), channel_id=1, source_target_pairs={{0,1},{1,0},{2,3},{3,2},{4,5},{5,4},{6,7},{7,6},{8,9},{9,8},{10,11... | collective-permute-start | bytes 786440 | tf_op jit(solution)/shard_map/ppermute | solution.py:94
  58.0 2.1 %collective-permute-start.15 = (bf16[8,128,128]{2,1,0:T(8,128)(2,1)S(1)}, bf16[8,128,128]{2,1,0:T(8,128)(2,1)S(1)}, u32[]{:S(2)}, u32[]{:S(2)}) collective-permute-start(bf16[8,128,128]{2,1,0:T(8,128)(2,1)S(1)} %collective-permute-done.14.refs_6_), channel_id=1, source_target_pairs={{0,1},{1,0},{2,3},{3,2},{4,5},{5,4},{6,7},{7,6},{8,9},{9,8},{10,11... | collective-permute-start | bytes 786440 | tf_op jit(solution)/shard_map/ppermute | solution.py:94
  71.5 32.2 %all-to-all-start = ((bf16[8,128,512]{2,1,0:T(8,128)(2,1)}), bf16[8,128,512]{2,1,0:T(8,128)(2,1)S(1)}, u32[]{:S(2)}, u32[]{:S(2)}) async-start(bf16[8,128,512]{2,1,0:T(8,128)(2,1)} %bitcast.32), calls=%async_computation | async-start | bytes 2097152 | tf_op jit(solution)/shard_map/all_to_all | solution.py:1225
  88.6 3.2 %collective-permute-start.16 = (bf16[2,1024,128]{2,1,0:T(8,128)(2,1)S(1)}, bf16[2,1024,128]{2,1,0:T(8,128)(2,1)S(1)}, u32[]{:S(2)}, u32[]{:S(2)}) collective-permute-start(bf16[2,1024,128]{2,1,0:T(8,128)(2,1)S(1)} %get-tuple-element.125), channel_id=1, source_target_pairs={{0,1},{1,0},{2,3},{3,2},{4,5},{5,4},{6,7},{7,6},{8,9},{9,8},{10,11... | collective-permute-start | bytes 1572872 | tf_op jit(solution)/shard_map/ppermute | solution.py:94
  91.2 11.5 %collective-permute-start.18 = (bf16[2,8,128,128]{3,2,1,0:T(8,128)(2,1)S(1)}, bf16[2,8,128,128]{3,2,1,0:T(8,128)(2,1)S(1)}, u32[]{:S(2)}, u32[]{:S(2)}) collective-permute-start(bf16[2,8,128,128]{3,2,1,0:T(8,128)(2,1)S(1)} %get-tuple-element.144), channel_id=1, source_target_pairs={{0,1},{1,0},{2,3},{3,2},{4,5},{5,4},{6,7},{7,6},{8,9},{9,8},{10,11... | collective-permute-start | bytes 1572872 | tf_op jit(solution)/shard_map/ppermute | solution.py:94
  92.6 11.1 %collective-permute-start.17 = (bf16[1,1024,128]{2,1,0:T(8,128)(2,1)S(1)}, bf16[1,1024,128]{2,1,0:T(8,128)(2,1)S(1)}, u32[]{:S(2)}, u32[]{:S(2)}) collective-permute-start(bf16[1,1024,128]{2,1,0:T(8,128)(2,1)S(1)} %get-tuple-element.131), channel_id=1, source_target_pairs={{0,2},{1,3},{2,0},{3,1},{4,6},{5,7},{6,4},{7,5},{8,10},{9,11},{10,... | collective-permute-start | bytes 786440 | tf_op jit(solution)/shard_map/ppermute | solution.py:94
  104.2 32.1 %all-to-all-start.2 = ((bf16[8,128,512]{2,1,0:T(8,128)(2,1)}), bf16[8,128,512]{2,1,0:T(8,128)(2,1)S(1)}, u32[]{:S(2)}, u32[]{:S(2)}) async-start(bf16[8,128,512]{2,1,0:T(8,128)(2,1)} %bitcast.31), calls=%async_computation.2 | async-start | bytes 2097152 | tf_op jit(solution)/shard_map/all_to_all | solution.py:1248
  110.2 8.9 %collective-permute-start.19 = (bf16[1,8,128,128]{3,2,1,0:T(8,128)(2,1)}, bf16[1,8,128,128]{3,2,1,0:T(8,128)(2,1)S(1)}, u32[]{:S(2)}, u32[]{:S(2)}) collective-permute-start(bf16[1,8,128,128]{3,2,1,0:T(8,128)(2,1)} %copy-done.6), channel_id=1, source_target_pairs={{0,2},{1,3},{2,0},{3,1},{4,6},{5,7},{6,4},{7,5},{8,10},{9,11},{10,... | collective-permute-start | bytes 786440 | tf_op jit(solution)/shard_map/ppermute | solution.py:94
  119.7 3.9 %collective-permute-start.23 = (f32[24,128]{1,0:T(8,128)S(1)}, f32[24,128]{1,0:T(8,128)S(1)}, u32[]{:S(2)}, u32[]{:S(2)}) collective-permute-start(f32[24,128]{1,0:T(8,128)S(1)} %get-tuple-element.153), channel_id=1, source_target_pairs={{0,3},{1,2},{2,1},{3,0},{4,7},{5,6},{6,5},{7,4},{8,11},{9,10},{10,... | collective-permute-start | bytes 36872 | tf_op jit(solution)/shard_map/ppermute | solution.py:1256
  120.0 3.7 %collective-permute-start.22 = (f32[24,128]{1,0:T(8,128)S(1)}, f32[24,128]{1,0:T(8,128)S(1)}, u32[]{:S(2)}, u32[]{:S(2)}) collective-permute-start(f32[24,128]{1,0:T(8,128)S(1)} %get-tuple-element.153), channel_id=1, source_target_pairs={{0,2},{1,3},{2,0},{3,1},{4,6},{5,7},{6,4},{7,5},{8,10},{9,11},{10,... | collective-permute-start | bytes 36872 | tf_op jit(solution)/shard_map/ppermute | solution.py:1256
  121.3 2.4 %collective-permute-start.21 = (f32[24,128]{1,0:T(8,128)S(1)}, f32[24,128]{1,0:T(8,128)S(1)}, u32[]{:S(2)}, u32[]{:S(2)}) collective-permute-start(f32[24,128]{1,0:T(8,128)S(1)} %get-tuple-element.153), channel_id=1, source_target_pairs={{0,1},{1,0},{2,3},{3,2},{4,5},{5,4},{6,7},{7,6},{8,9},{9,8},{10,11... | collective-permute-start | bytes 36872 | tf_op jit(solution)/shard_map/ppermute | solution.py:1256
  121.6 9.7 %collective-permute-start.20 = (bf16[4,160,128]{2,1,0:T(8,128)(2,1)S(1)}, bf16[4,160,128]{2,1,0:T(8,128)(2,1)S(1)}, u32[]{:S(2)}, u32[]{:S(2)}) collective-permute-start(bf16[4,160,128]{2,1,0:T(8,128)(2,1)S(1)} %get-tuple-element.151), channel_id=1, source_target_pairs={{0,4},{4,0},{8,12},{12,8},{16,20},{20,16},{24,28},{28,24},{1,5},{5... | collective-permute-start | bytes 491528 | tf_op jit(solution)/shard_map/ppermute | solution.py:94
  123.8 7.5 %collective-permute-start.24 = (f32[24,128]{1,0:T(8,128)S(1)}, f32[24,128]{1,0:T(8,128)S(1)}, u32[]{:S(2)}, u32[]{:S(2)}) collective-permute-start(f32[24,128]{1,0:T(8,128)S(1)} %add_add_fusion.refs_0_), channel_id=1, source_target_pairs={{0,4},{4,0},{8,12},{12,8},{16,20},{20,16},{24,28},{28,24},{1,5},{5... | collective-permute-start | bytes 36872 | tf_op jit(solution)/shard_map/ppermute | solution.py:94
  131.9 6.6 %collective-permute-start.25 = (bf16[192,128]{1,0:T(8,128)(2,1)S(1)}, bf16[192,128]{1,0:T(8,128)(2,1)S(1)}, u32[]{:S(2)}, u32[]{:S(2)}) collective-permute-start(bf16[192,128]{1,0:T(8,128)(2,1)S(1)} %get-tuple-element.157), channel_id=1, source_target_pairs={{0,8},{4,12},{8,0},{12,4},{16,24},{20,28},{24,16},{28,20},{1,9},{5... | collective-permute-start | bytes 147464 | tf_op jit(solution)/shard_map/ppermute | solution.py:94
  132.8 5.8 %collective-permute-start.26 = (bf16[192,128]{1,0:T(8,128)(2,1)S(1)}, bf16[192,128]{1,0:T(8,128)(2,1)S(1)}, u32[]{:S(2)}, u32[]{:S(2)}) collective-permute-start(bf16[192,128]{1,0:T(8,128)(2,1)S(1)} %get-tuple-element.158), channel_id=1, source_target_pairs={{0,16},{4,20},{8,24},{12,28},{16,0},{20,4},{24,8},{28,12},{1,17},{... | collective-permute-start | bytes 147464 | tf_op jit(solution)/shard_map/ppermute | solution.py:94
  135.0 5.9 %collective-permute-start.27 = (bf16[192,128]{1,0:T(8,128)(2,1)S(1)}, bf16[192,128]{1,0:T(8,128)(2,1)S(1)}, u32[]{:S(2)}, u32[]{:S(2)}) collective-permute-start(bf16[192,128]{1,0:T(8,128)(2,1)S(1)} %get-tuple-element.159), channel_id=1, source_target_pairs={{0,24},{4,28},{8,16},{12,20},{16,8},{20,12},{24,0},{28,4},{1,25},{... | collective-permute-start | bytes 147464 | tf_op jit(solution)/shard_map/ppermute | solution.py:94
  (6 other events, 213.3 us)
